TPU v7x, 32 devices: a whole 2x2x4 slice. The times are simulated.
32 devices in a mesh: fsdp: 32 (over z, y, x, core).
Axes of the slice: x: 2, y: 2, z: 4, core: 2. Of those that a mesh axis runs over, the one named last changes fastest.
Arguments:
- tokens: bfloat16 [2, 32, 576, 1024], P(None, 'fsdp'), may hold values from -5 to 5
- lengths: int32 [2, 32], P(None, 'fsdp'), may hold values from 196 to 576, as said below
- cotangent: float32 [2, 32, 8, 1024], P(None, 'fsdp'), may hold values from -768 to 768
- ln1_gain: bfloat16 [1024], P('fsdp'), may hold values from 0.5 to 1.5
- ln1_bias: bfloat16 [1024], P('fsdp'), may hold values from -1.1953125 to 1.1953125
- w_qkv: bfloat16 [1024, 3072], P('fsdp'), may hold values from -0.25 to 0.25
- b_qv: bfloat16 [2048], P('fsdp'), may hold values from -1.1953125 to 1.1953125
- w_out: bfloat16 [1024, 1024], P('fsdp'), may hold values from -0.375 to 0.375
- b_out: bfloat16 [1024], P('fsdp'), may hold values from -1.1953125 to 1.1953125
- ln2_gain: bfloat16 [1024], P('fsdp'), may hold values from 0.5 to 1.5
- ln2_bias: bfloat16 [1024], P('fsdp'), may hold values from -1.1953125 to 1.1953125
- w_up: bfloat16 [1024, 4096], P('fsdp'), may hold values from -0.1875 to 0.1875
- b_up: bfloat16 [4096], P('fsdp'), may hold values from -1.1953125 to 1.1953125
- w_down: bfloat16 [4096, 1024], P('fsdp'), may hold values from -0.09375 to 0.09375
- b_down: bfloat16 [1024], P('fsdp'), may hold values from -1.1953125 to 1.1953125
- ln3_gain: bfloat16 [1024], P('fsdp'), may hold values from 0.5 to 1.5
- ln3_bias: bfloat16 [1024], P('fsdp'), may hold values from -1.1953125 to 1.1953125
- w_learn: bfloat16 [1024, 1024], P('fsdp'), may hold values from -0.1875 to 0.1875
- b_learn: bfloat16 [1024], P('fsdp'), may hold values from -1.1953125 to 1.1953125
- w_map: bfloat16 [1024, 8], P('fsdp'), may hold values from -0.75 to 0.75
Outputs:
- pooled: float32 [2, 32, 8, 1024], P(None, 'fsdp')
- d_tokens: float32 [2, 32, 576, 1024], P(None, 'fsdp')
- grad_ln1_gain: float32 [1024], P('fsdp')
- grad_ln1_bias: float32 [1024], P('fsdp')
- grad_w_qkv: float32 [1024, 3072], P('fsdp')
- grad_b_qv: float32 [2048], P('fsdp')
- grad_w_out: float32 [1024, 1024], P('fsdp')
- grad_b_out: float32 [1024], P('fsdp')
- grad_ln2_gain: float32 [1024], P('fsdp')
- grad_ln2_bias: float32 [1024], P('fsdp')
- grad_w_up: float32 [1024, 4096], P('fsdp')
- grad_b_up: float32 [4096], P('fsdp')
- grad_w_down: float32 [4096, 1024], P('fsdp')
- grad_b_down: float32 [1024], P('fsdp')
- grad_ln3_gain: float32 [1024], P('fsdp')
- grad_ln3_bias: float32 [1024], P('fsdp')
- grad_w_learn: float32 [1024, 1024], P('fsdp')
- grad_b_learn: float32 [1024], P('fsdp')
- grad_w_map: float32 [1024, 8], P('fsdp')
Inputs may be any that keep to these rules, and one draw needn't show every extreme that they name: `lengths`: each image has 196 or 576 patches; both counts occur in every draw.
All inputs are finite; a program needn't handle non-finite values.
Results may differ from a plain program's by a relative error of at most 0.013.
Values may be sent and summed in bfloat16 or wider, within the bound.
No kernel may reach another device: no remote copies, remote signals or barrier semaphores. Data moves between devices by JAX's collectives and lax.ppermute only.
A program may use at most 448 MiB of HBM per device.

v0:
```python
import jax
import jax.numpy as jnp
from jax import lax
from jax.sharding import PartitionSpec as P

D = 1024
HEADS = 16
HD = 64


EPSILON = 1e-06
SCALE = 0.125


def layer_norm(values, gain, shift):
    row_mean = jnp.mean(values, axis=-1, keepdims=True)
    centered = values - row_mean
    variance = jnp.mean(centered * centered, axis=-1, keepdims=True)
    return centered * lax.rsqrt(variance + EPSILON) * gain + shift


def norm_back(values, gain, shift, incoming):
    _, pull_back = jax.vjp(layer_norm, values, gain, shift)
    return pull_back(incoming)


def gelu_exact(values):
    return jax.nn.gelu(values, approximate=False)


def gelu_slope(values, incoming):
    _, pull_back = jax.vjp(gelu_exact, values)
    return pull_back(incoming)[0]


def product(left, right):
    return jnp.dot(left, right, preferred_element_type=jnp.float32)


def product_rows(left, right):
    return lax.dot_general(
        left, right, (((0,), (0,)), ((), ())), preferred_element_type=jnp.float32
    )


def product_back(left, right):
    return lax.dot_general(
        left, right, (((1,), (1,)), ((), ())), preferred_element_type=jnp.float32
    )


def attention_scores(queries, key_rows, slot_valid):
    scores = (
        jnp.einsum("qhd,khd->hqk", queries, key_rows, preferred_element_type=jnp.float32) * SCALE
    )
    return jnp.where(slot_valid[None, None, :], scores, -1e30)


def unflatten_all(flat_local, grads, devices):
    pieces = []
    offset = 0
    for item in grads:
        local_shape = (item.shape[0] // devices,) + item.shape[1:]
        count = item.size // devices
        pieces.append(flat_local[offset : offset + count].reshape(local_shape))
        offset = offset + count
    return tuple(pieces)


def image_forward(params, image_rows, length):
    (
        ln1_gain,
        ln1_bias,
        w_qkv,
        b_qv,
        w_out,
        b_out,
        ln2_gain,
        ln2_bias,
        w_up,
        b_up,
        w_down,
        b_down,
        ln3_gain,
        ln3_bias,
        w_learn,
        b_learn,
        w_map,
    ) = params
    slot_count = image_rows.shape[0]
    slot_valid = lax.iota(jnp.int32, slot_count) < length
    source = image_rows.astype(jnp.float32)
    hidden = layer_norm(source, ln1_gain.astype(jnp.float32), ln1_bias.astype(jnp.float32)).astype(
        jnp.bfloat16
    )
    qkv_rows = product(hidden, w_qkv)
    qv_bias = b_qv.astype(jnp.float32)
    queries = (qkv_rows[:, :D] + qv_bias[:D]).astype(jnp.bfloat16).reshape(slot_count, HEADS, HD)
    key_rows = qkv_rows[:, D : 2 * D].astype(jnp.bfloat16).reshape(slot_count, HEADS, HD)
    values = (
        (qkv_rows[:, 2 * D :] + qv_bias[D:]).astype(jnp.bfloat16).reshape(slot_count, HEADS, HD)
    )
    scores = attention_scores(queries, key_rows, slot_valid)
    row_top = jnp.max(scores, axis=-1, keepdims=True)
    row_total = jnp.sum(jnp.exp(scores - row_top), axis=-1, keepdims=True)
    log_total = row_top + jnp.log(row_total)
    probs_low = jnp.exp(scores - log_total).astype(jnp.bfloat16)
    attended = jnp.einsum("hqk,khd->qhd", probs_low, values, preferred_element_type=jnp.float32)
    attended = attended.reshape(slot_count, D).astype(jnp.bfloat16)
    middle = source + product(attended, w_out) + b_out.astype(jnp.float32)
    normed = layer_norm(middle, ln2_gain.astype(jnp.float32), ln2_bias.astype(jnp.float32)).astype(
        jnp.bfloat16
    )
    up_proj = product(normed, w_up) + b_up.astype(jnp.float32)
    up_act = gelu_exact(up_proj).astype(jnp.bfloat16)
    output = middle + product(up_act, w_down) + b_down.astype(jnp.float32)
    learn_in = layer_norm(
        output, ln3_gain.astype(jnp.float32), ln3_bias.astype(jnp.float32)
    ).astype(jnp.bfloat16)
    learn_mid = product(learn_in, w_learn) + b_learn.astype(jnp.float32)
    learn_act = gelu_exact(learn_mid).astype(jnp.bfloat16)
    logits = product(learn_act, w_map)
    pool_share = slot_valid.astype(jnp.float32) / length.astype(jnp.float32)
    pool_maps = jax.nn.sigmoid(logits) * pool_share[:, None]
    pooled = jnp.einsum("sm,sd->md", pool_maps, output, precision=lax.Precision.HIGHEST)
    saved = (
        queries,
        key_rows,
        values,
        log_total,
        attended,
        middle,
        normed,
        up_proj,
        up_act,
        output,
        learn_in,
        learn_mid,
        learn_act,
        logits,
    )
    return (pooled, saved)


def image_backward(params, image_rows, length, pool_grad, saved):
    (
        ln1_gain,
        ln1_bias,
        w_qkv,
        b_qv,
        w_out,
        b_out,
        ln2_gain,
        ln2_bias,
        w_up,
        b_up,
        w_down,
        b_down,
        ln3_gain,
        ln3_bias,
        w_learn,
        b_learn,
        w_map,
    ) = params
    (
        queries,
        key_rows,
        values,
        log_total,
        attended,
        middle,
        normed,
        up_proj,
        up_act,
        output,
        learn_in,
        learn_mid,
        learn_act,
        logits,
    ) = saved
    slot_count = image_rows.shape[0]
    slot_valid = lax.iota(jnp.int32, slot_count) < length
    source = image_rows.astype(jnp.float32)
    pool_share = slot_valid.astype(jnp.float32) / length.astype(jnp.float32)
    squashed = jax.nn.sigmoid(logits)
    pool_maps = squashed * pool_share[:, None]
    d_maps = jnp.einsum("sd,md->sm", output, pool_grad, precision=lax.Precision.HIGHEST)
    d_logits = (d_maps * pool_share[:, None] * squashed * (1.0 - squashed)).astype(jnp.bfloat16)
    d_output = jnp.einsum("sm,md->sd", pool_maps, pool_grad, precision=lax.Precision.HIGHEST)
    g_map = product_rows(learn_act, d_logits)
    d_learn = gelu_slope(learn_mid, product_back(d_logits, w_map)).astype(jnp.bfloat16)
    g_blearn = jnp.sum(d_learn.astype(jnp.float32), axis=0)
    g_wlearn = product_rows(learn_in, d_learn)
    d_norm3, g_ln3, h_ln3 = norm_back(
        output,
        ln3_gain.astype(jnp.float32),
        ln3_bias.astype(jnp.float32),
        product_back(d_learn, w_learn),
    )
    d_output = d_output + d_norm3
    d_mlp = d_output.astype(jnp.bfloat16)
    g_bdown = jnp.sum(d_mlp.astype(jnp.float32), axis=0)
    g_wdown = product_rows(up_act, d_mlp)
    d_up = gelu_slope(up_proj, product_back(d_mlp, w_down)).astype(jnp.bfloat16)
    g_bup = jnp.sum(d_up.astype(jnp.float32), axis=0)
    g_wup = product_rows(normed, d_up)
    d_norm2, g_ln2, h_ln2 = norm_back(
        middle, ln2_gain.astype(jnp.float32), ln2_bias.astype(jnp.float32), product_back(d_up, w_up)
    )
    d_middle = d_output + d_norm2
    d_branch = d_middle.astype(jnp.bfloat16)
    g_bout = jnp.sum(d_branch.astype(jnp.float32), axis=0)
    g_wout = product_rows(attended, d_branch)
    d_attn = product_back(d_branch, w_out).astype(jnp.bfloat16).reshape(slot_count, HEADS, HD)
    scores = attention_scores(queries, key_rows, slot_valid)
    probs = jnp.exp(scores - log_total)
    probs_low = probs.astype(jnp.bfloat16)
    d_values = jnp.einsum(
        "hqk,qhd->khd", probs_low, d_attn, preferred_element_type=jnp.float32
    ).astype(jnp.bfloat16)
    d_probs = jnp.einsum("qhd,khd->hqk", d_attn, values, preferred_element_type=jnp.float32)
    d_scores = (probs * (d_probs - jnp.sum(probs * d_probs, axis=-1, keepdims=True))).astype(
        jnp.bfloat16
    )
    d_queries = (
        jnp.einsum("hqk,khd->qhd", d_scores, key_rows, preferred_element_type=jnp.float32) * SCALE
    ).astype(jnp.bfloat16)
    d_keys = (
        jnp.einsum("hqk,qhd->khd", d_scores, queries, preferred_element_type=jnp.float32) * SCALE
    ).astype(jnp.bfloat16)
    d_qkv = jnp.concatenate(
        [
            d_queries.reshape(slot_count, D),
            d_keys.reshape(slot_count, D),
            d_values.reshape(slot_count, D),
        ],
        axis=1,
    )
    g_bqv = jnp.concatenate(
        [
            jnp.sum(d_queries.reshape(slot_count, D).astype(jnp.float32), axis=0),
            jnp.sum(d_values.reshape(slot_count, D).astype(jnp.float32), axis=0),
        ]
    )
    gain_one = ln1_gain.astype(jnp.float32)
    bias_one = ln1_bias.astype(jnp.float32)
    hidden = layer_norm(source, gain_one, bias_one).astype(jnp.bfloat16)
    g_wqkv = product_rows(hidden, d_qkv)
    d_norm1, g_ln1, h_ln1 = norm_back(source, gain_one, bias_one, product_back(d_qkv, w_qkv))
    d_image = d_middle + d_norm1
    grad_parts = (
        g_ln1,
        h_ln1,
        g_wqkv,
        g_bqv,
        g_wout,
        g_bout,
        g_ln2,
        h_ln2,
        g_wup,
        g_bup,
        g_wdown,
        g_bdown,
        g_ln3,
        h_ln3,
        g_wlearn,
        g_blearn,
        g_map,
    )
    return (d_image, grad_parts)


def body(
    tokens,
    lengths,
    cotangent,
    ln1_gain,
    ln1_bias,
    w_qkv,
    b_qv,
    w_out,
    b_out,
    ln2_gain,
    ln2_bias,
    w_up,
    b_up,
    w_down,
    b_down,
    ln3_gain,
    ln3_bias,
    w_learn,
    b_learn,
    w_map,
):
    shards = (
        ln1_gain,
        ln1_bias,
        w_qkv,
        b_qv,
        w_out,
        b_out,
        ln2_gain,
        ln2_bias,
        w_up,
        b_up,
        w_down,
        b_down,
        ln3_gain,
        ln3_bias,
        w_learn,
        b_learn,
        w_map,
    )
    devices = lax.axis_size("fsdp")
    micro_count = tokens.shape[0]
    pooled_parts = []
    grad_image_parts = []
    grad_total = None
    for micro_step in range(micro_count):
        forward_params = (
            lax.all_gather(shards[0], "fsdp", axis=0, tiled=True),
            lax.all_gather(shards[1], "fsdp", axis=0, tiled=True),
            lax.all_gather(shards[2], "fsdp", axis=0, tiled=True),
            lax.all_gather(shards[3], "fsdp", axis=0, tiled=True),
            lax.all_gather(shards[4], "fsdp", axis=0, tiled=True),
            lax.all_gather(shards[5], "fsdp", axis=0, tiled=True),
            lax.all_gather(shards[6], "fsdp", axis=0, tiled=True),
            lax.all_gather(shards[7], "fsdp", axis=0, tiled=True),
            lax.all_gather(shards[8], "fsdp", axis=0, tiled=True),
            lax.all_gather(shards[9], "fsdp", axis=0, tiled=True),
            lax.all_gather(shards[10], "fsdp", axis=0, tiled=True),
            lax.all_gather(shards[11], "fsdp", axis=0, tiled=True),
            lax.all_gather(shards[12], "fsdp", axis=0, tiled=True),
            lax.all_gather(shards[13], "fsdp", axis=0, tiled=True),
            lax.all_gather(shards[14], "fsdp", axis=0, tiled=True),
            lax.all_gather(shards[15], "fsdp", axis=0, tiled=True),
            lax.all_gather(shards[16], "fsdp", axis=0, tiled=True),
        )

        def forward_one(item_pack):
            return image_forward(forward_params, item_pack[0], item_pack[1])

        pooled, saved = lax.map(forward_one, (tokens[micro_step], lengths[micro_step]))
        backward_params = (
            lax.all_gather(shards[0], "fsdp", axis=0, tiled=True),
            lax.all_gather(shards[1], "fsdp", axis=0, tiled=True),
            lax.all_gather(shards[2], "fsdp", axis=0, tiled=True),
            lax.all_gather(shards[3], "fsdp", axis=0, tiled=True),
            lax.all_gather(shards[4], "fsdp", axis=0, tiled=True),
            lax.all_gather(shards[5], "fsdp", axis=0, tiled=True),
            lax.all_gather(shards[6], "fsdp", axis=0, tiled=True),
            lax.all_gather(shards[7], "fsdp", axis=0, tiled=True),
            lax.all_gather(shards[8], "fsdp", axis=0, tiled=True),
            lax.all_gather(shards[9], "fsdp", axis=0, tiled=True),
            lax.all_gather(shards[10], "fsdp", axis=0, tiled=True),
            lax.all_gather(shards[11], "fsdp", axis=0, tiled=True),
            lax.all_gather(shards[12], "fsdp", axis=0, tiled=True),
            lax.all_gather(shards[13], "fsdp", axis=0, tiled=True),
            lax.all_gather(shards[14], "fsdp", axis=0, tiled=True),
            lax.all_gather(shards[15], "fsdp", axis=0, tiled=True),
            lax.all_gather(shards[16], "fsdp", axis=0, tiled=True),
        )
        grad_zero = tuple((jnp.zeros(item.shape, jnp.float32) for item in backward_params))

        def backward_one(grad_carry, item_pack):
            d_image, grad_parts = image_backward(
                backward_params, item_pack[0], item_pack[1], item_pack[2], item_pack[3]
            )
            return (tuple((left + right for left, right in zip(grad_carry, grad_parts))), d_image)

        micro_grads, d_images = lax.scan(
            backward_one,
            grad_zero,
            (tokens[micro_step], lengths[micro_step], cotangent[micro_step], saved),
        )
        if grad_total is None:
            grad_total = micro_grads
        else:
            grad_total = tuple((left + right for left, right in zip(grad_total, micro_grads)))
        pooled_parts.append(pooled)
        grad_image_parts.append(d_images)
    flat_terms = jnp.concatenate([item.reshape(devices, -1) for item in grad_total], axis=1)
    summed = lax.psum_scatter(flat_terms.reshape(-1), "fsdp", scatter_dimension=0, tiled=True)
    grad_total = unflatten_all(summed, grad_total, devices)
    return (jnp.stack(pooled_parts), jnp.stack(grad_image_parts)) + tuple(grad_total)


def solution(mesh):
    placed = (
        P(None, "fsdp", None, None),
        P(None, "fsdp"),
        P(None, "fsdp", None, None),
        P("fsdp"),
        P("fsdp"),
        P("fsdp", None),
        P("fsdp"),
        P("fsdp", None),
        P("fsdp"),
        P("fsdp"),
        P("fsdp"),
        P("fsdp", None),
        P("fsdp"),
        P("fsdp", None),
        P("fsdp"),
        P("fsdp"),
        P("fsdp"),
        P("fsdp", None),
        P("fsdp"),
        P("fsdp", None),
    )
    return jax.shard_map(
        body,
        mesh=mesh,
        in_specs=placed,
        out_specs=(
            P(None, "fsdp", None, None),
            P(None, "fsdp", None, None),
            P("fsdp"),
            P("fsdp"),
            P("fsdp", None),
            P("fsdp"),
            P("fsdp", None),
            P("fsdp"),
            P("fsdp"),
            P("fsdp"),
            P("fsdp", None),
            P("fsdp"),
            P("fsdp", None),
            P("fsdp"),
            P("fsdp"),
            P("fsdp"),
            P("fsdp", None),
            P("fsdp"),
            P("fsdp", None),
        ),
        check_vma=False,
    )
```

profile of v0, /device:TPU:0, one launch (start us, length us, event | category | flops | bytes accessed | tf_op | source)
XLA Modules:
  0.0 1820.5 jit_solution(6046457286659416338)
XLA Ops:
  26.6 42.9 %all-reduce.11 = (bf16[2048]{0:T(1024)(128)(2,1)S(1)}, bf16[1024]{0:T(1024)(128)(2,1)S(1)}, bf16[1024]{0:T(1024)(128)(2,1)S(1)}, bf16[1024]{0:T(1024)(128)(2,1)S...) all-reduce(bf16[2048]{0:T(1024)(128)(2,1)S(1)} %dynamic-update-slic, ...), channel_id=1, replica_groups=mesh['fsdp'=32] {'fsdp'}, use_global_device_ids=true, to_apply=%add.2 | all-reduce | flops 11264 | bytes 45056
  76.5 40.1 %all-gather = bf16[32,1,128]{2,1,0:T(2,128)(2,1)S(1)} all-gather(bf16[1,1,128]{2,1,0:T(2,128)(2,1)S(1)} %bitcast.258), channel_id=1, replica_groups=mesh['fsdp'=32] {'fsdp'}, dimensions={0}, use_global_device_ids=true | all-gather | bytes 8448 | tf_op jit(solution)/shard_map/all_gather | solution.py:330
  117.3 37.5 %all-gather.1 = bf16[32,32,8]{1,2,0:T(8,128)(2,1)S(1)} all-gather(bf16[1,32,8]{1,2,0:T(8,128)(2,1)S(1)} %bitcast.257), channel_id=1, replica_groups=mesh['fsdp'=32] {'fsdp'}, dimensions={0}, use_global_device_ids=true | all-gather | bytes 16896 | tf_op jit(solution)/shard_map/all_gather | solution.py:337
  155.5 6.2 fusion.118
  166.1 6.3 fusion.115
  187.5 14.6 fusion
  202.1 11.7 exponential_reduce_fusion.1
  237.2 10.5 fusion.1
  247.7 11.5 exponential_reduce_fusion
  276.6 8.6 fusion.126
  288.8 53.0 %multiply_convert_fusion.3 = (bf16[576,4096]{1,0:T(8,128)(2,1)}, f32[576,4096]{1,0:T(8,128)}, bf16[576,4096]{1,0:T(8,128)(2,1)}, f32[576,4096]{1,0:T(8,128)}, f32[576,4096]{1,0:T(8,128)}) fusion(f32[4096]{0:T(1024)S(1)} %bitcast.254, f32[576,4096]{1,0:T(8,128)S(1)} %fusion.126, bf16[1024,4096]{1,0:T(8,128)(2,1)S(1)} %copy-done.133, ...), kind=kOutput, calls=%fused_computation.35 | convolution fusion | flops 5146214400 | bytes 57963008 | tf_op jit(solution)/shard_map/while/body/eval_jaxpr/dot_general | solution.py:37
  341.9 10.1 fusion.145
  365.6 12.2 multiply_convert_fusion.9
  400.4 10.3 fusion.108
  410.7 17.6 convert_reduce_fusion.1
  428.3 13.0 fusion.122
  443.6 10.0 fusion.148
  453.7 17.1 convert_reduce_fusion
  470.8 14.1 multiply_reduce_fusion.4
  484.9 5.6 fusion.130
  496.1 10.0 convert_reduce_fusion.4
  506.1 16.8 multiply_reduce_fusion
  522.9 20.2 %multiply_convert_fusion = bf16[16,576,576]{1,2,0:T(8,128)(2,1)} fusion(f32[16,576,576]{1,2,0:T(8,128)} %get-tuple-element.659, f32[16,576,576]{1,2,0:T(8,128)} %get-tuple-element.595, f32[16,576]{1,0:T(8,128)S(1)} %get-tuple-element.658, f32[16,576]{1,0:T(8,128)S(1)} %copy-done.56, pred[576]{0:T(1024)(128)(4,1)S(1)} %copy-done.101), kind=kLoop, calls=%fused_computation | loop fusion | flops 31850496 | bytes 53158464 | tf_op jit(solution)/shard_map/while/body/eval_jaxpr/convert_element_type | solution.py:222
  543.1 9.2 multiply_convert_fusion.4
  552.3 8.4 convert_reduce_fusion.5
  568.4 9.7 convert_reduce_fusion.6
  578.0 16.2 multiply_reduce_fusion.1
  594.3 20.4 %multiply_convert_fusion.1 = bf16[16,576,576]{1,2,0:T(8,128)(2,1)} fusion(f32[16,576,576]{1,2,0:T(8,128)} %get-tuple-element.657, f32[16,576,576]{1,2,0:T(8,128)} %get-tuple-element.597, f32[16,576]{1,0:T(8,128)S(1)} %get-tuple-element.656, f32[16,576]{1,0:T(8,128)S(1)} %copy-done.54, pred[576]{0:T(1024)(128)(4,1)S(1)} %copy-done.99), kind=kLoop, calls=%fused_computation.2 | loop fusion | flops 31850496 | bytes 53158464 | tf_op jit(solution)/shard_map/while/body/eval_jaxpr/convert_element_type | solution.py:222
  614.7 9.1 multiply_convert_fusion.6
  623.8 7.7 convert_reduce_fusion.7
  633.3 6.5 convolution_add_fusion.3
  645.2 5.9 convolution_add_fusion.4
  656.2 15.2 convolution_add_fusion
  671.4 12.7 reshape.578
  684.1 15.0 convolution_add_fusion.1
  699.1 12.4 reshape.579
  711.5 12.3 fusion.61
  723.9 7.5 fusion.60
  731.5 6.5 fusion.39
  742.7 5.7 add_bitcast_fusion.1
  748.6 15.8 convolution_add_fusion.2
  764.4 9.9 reshape.576
  777.2 37.1 %dynamic-update-slice.12 = f32[32,426720]{1,0:T(8,128)} dynamic-update-slice(f32[32,426720]{1,0:T(8,128)} %dynamic-update-slice.11, f32[32,98304]{1,0:T(8,128)} %reshape.576, s32[]{} %constant.650, s32[]{} %constant.652) | dynamic-update-slice | bytes 25165828
  824.6 48.2 %dynamic-update-slice.18 = f32[32,426720]{1,0:T(8,128)} dynamic-update-slice(f32[32,426720]{1,0:T(8,128)} %dynamic-update-slice.17, f32[32,131072]{1,0:T(8,128)} %reshape.578, s32[]{} %constant.650, s32[]{} %constant.658) | dynamic-update-slice | bytes 33554436
  874.3 48.2 %dynamic-update-slice.20 = f32[32,426720]{1,0:T(8,128)} dynamic-update-slice(f32[32,426720]{1,0:T(8,128)} %dynamic-update-slice.19, f32[32,131072]{1,0:T(8,128)} %reshape.579, s32[]{} %constant.650, s32[]{} %constant.660) | dynamic-update-slice | bytes 33554436
  926.8 14.3 dynamic-update-slice.24
  944.6 77.1 %reshape.582 = f32[13655040]{0:T(1024)} reshape(f32[32,426720]{1,0:T(8,128)} %dynamic-update-slice.26) | data formatting | bytes 109240320 | tf_op jit(solution)/shard_map/reshape | solution.py:383
  1032.1 767.9 %all-reduce.14.cloned.1.call-done = f32[13655040]{0:T(1024)} async-done(((f32[13655040]{0:T(1024)}), f32[13655040]{0:T(1024)}) %all-reduce.14.cloned.1.call-update) | async-done | bytes 54620176
  (481 shorter events, 204.5 us)
Async XLA Ops:
  7.2 67.9 %copy-start.4 = (bf16[2,1,576,1024]{3,2,1,0:T(8,128)(2,1)S(1)}, bf16[2,1,576,1024]{3,2,1,0:T(8,128)(2,1)}, u32[]{:S(2)}) copy-start(bf16[2,1,576,1024]{3,2,1,0:T(8,128)(2,1)} %param.20) | copy-start | bytes 7077892
  7.2 148.3 %all-gather.8.cloned.1.call-start = ((), (), s32[]{:S(2)}) async-start(), calls=%async_computation | async-start | bytes 6488064 | tf_op jit(solution)/shard_map/all_gather | solution.py:323
  7.9 223.4 %all-gather.10.cloned.1.call-start = ((), (), s32[]{:S(2)}) async-start(), calls=%async_computation.1 | async-start | bytes 2162688 | tf_op jit(solution)/shard_map/all_gather | solution.py:325
  8.7 267.9 %all-gather.12.cloned.1.call-start = ((), (), s32[]{:S(2)}) async-start(), calls=%async_computation.2 | async-start | bytes 8650752 | tf_op jit(solution)/shard_map/all_gather | solution.py:329
  9.4 332.4 %all-gather.14.cloned.1.call-start = ((), (), s32[]{:S(2)}) async-start(), calls=%async_computation.3 | async-start | bytes 8650752 | tf_op jit(solution)/shard_map/all_gather | solution.py:331
  10.0 351.6 %all-gather.16.cloned.1.call-start = ((), (), s32[]{:S(2)}) async-start(), calls=%async_computation.4 | async-start | bytes 2162688 | tf_op jit(solution)/shard_map/all_gather | solution.py:335
  10.6 1789.5 %all-reduce.14.cloned.1.call-start = ((), (), s32[]{:S(2)}) async-start(), calls=%async_computation.5 | async-start | bytes 109240320
  69.4 96.7 %copy-start.76 = (f32[1024]{0:T(1024)}, f32[1024]{0:T(1024)S(1)}, u32[]{:S(2)}) copy-start(f32[1024]{0:T(1024)S(1)} %convert_element_type.370) | copy-start | bytes 12292
  70.0 85.5 %copy-start.124 = (f32[1024]{0:T(1024)}, f32[1024]{0:T(1024)S(1)}, u32[]{:S(2)}) copy-start(f32[1024]{0:T(1024)S(1)} %convert_element_type.371) | copy-start | bytes 12292
  70.0 358.3 %copy-start.57 = (f32[1024]{0:T(1024)}, f32[1024]{0:T(1024)S(1)}, u32[]{:S(2)}) copy-start(f32[1024]{0:T(1024)S(1)} %convert_element_type.382) | copy-start | bytes 12292
  73.0 44.3 %copy-start.131 = (bf16[32,8]{0,1:T(8,128)(2,1)S(1)}, bf16[32,8]{0,1:T(8,128)(2,1)}, u32[]{:S(2)}) copy-start(bf16[32,8]{0,1:T(8,128)(2,1)} %param.39) | copy-start | bytes 1540
  75.1 80.4 %copy-start.66 = (f32[576]{0:T(1024)}, f32[576]{0:T(1024)S(1)}, u32[]{:S(2)}) copy-start(f32[576]{0:T(1024)S(1)} %get-tuple-element.677) | copy-start | bytes 6916
  75.1 91.0 %copy-start.68 = (f32[576]{0:T(1024)}, f32[576]{0:T(1024)S(1)}, u32[]{:S(2)}) copy-start(f32[576]{0:T(1024)S(1)} %get-tuple-element.678) | copy-start | bytes 6916
  76.5 79.0 %copy-start.78 = (f32[576]{0:T(1024)}, f32[576]{0:T(1024)S(1)}, u32[]{:S(2)}) copy-start(f32[576]{0:T(1024)S(1)} %fusion.96) | copy-start | bytes 6916
  202.1 15.0 copy-start
  247.7 14.8 copy-start.1
  288.8 53.1 %copy-start.129 = (f32[1024]{0:T(1024)S(1)}, f32[1024]{0:T(1024)}, u32[]{:S(2)}) copy-start(f32[1024]{0:T(1024)} %convert_element_type.386) | copy-start | bytes 12292
  352.0 44.1 %copy-start.6 = (f32[576,1024]{1,0:T(8,128)}, f32[576,1024]{1,0:T(8,128)S(1)}, u32[]{:S(2)}) copy-start(f32[576,1024]{1,0:T(8,128)S(1)} %get-tuple-element.650) | copy-start | bytes 7077892
  359.7 36.3 %copy-start.93 = (f32[576]{0:T(1024)}, f32[576]{0:T(1024)S(1)}, u32[]{:S(2)}) copy-start(f32[576]{0:T(1024)S(1)} %broadcast_multiply_fusion) | copy-start | bytes 6916
  361.6 34.5 %copy-start.111 = (f32[576]{0:T(1024)}, f32[576]{0:T(1024)S(1)}, u32[]{:S(2)}) copy-start(f32[576]{0:T(1024)S(1)} %fusion.98) | copy-start | bytes 6916
  365.6 12.6 copy-start.63
  365.6 12.6 copy-start.70
  378.2 20.1 %copy-start.59 = (f32[576,8]{0,1:T(8,128)}, f32[576,8]{0,1:T(8,128)S(1)}, u32[]{:S(2)}) copy-start(f32[576,8]{0,1:T(8,128)S(1)} %fusion.68) | copy-start | bytes 55300
  381.6 59.7 %copy-start.61 = (f32[576,8]{0,1:T(8,128)}, f32[576,8]{0,1:T(8,128)S(1)}, u32[]{:S(2)}) copy-start(f32[576,8]{0,1:T(8,128)S(1)} %fusion.65) | copy-start | bytes 55300
  400.4 160.3 %copy-start.14 = (f32[576,1024]{1,0:T(8,128)}, f32[576,1024]{1,0:T(8,128)S(1)}, u32[]{:S(2)}) copy-start(f32[576,1024]{1,0:T(8,128)S(1)} %add_add_fusion.9) | copy-start | bytes 7077892
  410.7 17.6 copy-start.21
  428.3 13.0 copy-start.38
  443.6 46.9 %copy-start.11 = (f32[576,1024]{1,0:T(8,128)}, f32[576,1024]{1,0:T(8,128)S(1)}, u32[]{:S(2)}) copy-start(f32[576,1024]{1,0:T(8,128)S(1)} %add_add_fusion.7) | copy-start | bytes 7077892
  453.6 17.1 copy-start.92
  453.7 17.1 copy-start.110
  470.8 14.1 copy-start.86
  470.8 14.1 copy-start.88
  470.8 14.1 copy-start.22
  470.8 14.1 copy-start.36
  522.9 20.2 %copy-start.31 = (bf16[576,1024]{0,1:T(8,128)(2,1)S(1)}, bf16[576,1024]{0,1:T(8,128)(2,1)}, u32[]{:S(2)}) copy-start(bf16[576,1024]{0,1:T(8,128)(2,1)} %copy.88) | copy-start | bytes 3538948
  594.3 20.4 %copy-start.29 = (bf16[576,1024]{0,1:T(8,128)(2,1)S(1)}, bf16[576,1024]{0,1:T(8,128)(2,1)}, u32[]{:S(2)}) copy-start(bf16[576,1024]{0,1:T(8,128)(2,1)} %copy.83) | copy-start | bytes 3538948
  671.4 12.7 copy-start.12
  699.1 12.4 copy-start.5
  699.1 12.4 copy-start.69
  699.1 12.4 copy-start.77
  699.1 12.4 copy-start.80
  699.1 12.4 copy-start.125
  711.5 12.4 copy-start.46
  711.5 12.4 copy-start.49
  711.5 19.9 %slice-start.4 = ((s8[6291456]{0:T(1024)(128)(4,1)}), s8[4194304]{0:T(1024)(128)(4,1)S(1)}, s32[]{:S(2)}) async-start(s8[6291456]{0:T(1024)(128)(4,1)} %bitcast.261), calls=%async_computation.10 | async-start | bytes 8388608
  777.2 37.1 %copy-start.95 = (f32[16,64]{1,0:T(8,128)S(1)}, f32[16,64]{1,0:T(8,128)}, u32[]{:S(2)}) copy-start(f32[16,64]{1,0:T(8,128)} %get-tuple-element.667) | copy-start | bytes 12292
  777.2 37.1 %copy-start.96 = (f32[16,64]{1,0:T(8,128)S(1)}, f32[16,64]{1,0:T(8,128)}, u32[]{:S(2)}) copy-start(f32[16,64]{1,0:T(8,128)} %get-tuple-element.665) | copy-start | bytes 12292
  777.2 37.1 %copy-start.97 = (f32[16,64]{1,0:T(8,128)S(1)}, f32[16,64]{1,0:T(8,128)}, u32[]{:S(2)}) copy-start(f32[16,64]{1,0:T(8,128)} %get-tuple-element.661) | copy-start | bytes 12292
  (106 other events, 564.7 us)
Sparse Core Ops, SparseCore 0:
  10.9 73.0 all-gather.7
  86.8 54.9 all-gather.9
  144.7 76.2 all-gather.11
  223.7 76.0 all-gather.13
  302.5 55.0 all-gather.15
  1021.9 778.1 all-reduce.13
where the time goes:
time: 1830 us; the launch traced here: 1820 us
  waiting for transfers between devices  771 us (42%)
  matrix products  433 us (24%)
  local copies, waits for them, and re-layouts  364 us (20%)
  blocking collectives  120 us (7%)
  other arithmetic  115 us (6%)
    unnamed x7, waiting for transfers between devices  771 us
    unnamed x334, local copies, waits for them, and re-layouts  207 us
    dot_general x12, matrix products, product(): return jnp.dot(left, right, preferred_element_type=jnp.float32)  112 us
    dot_general x12, matrix products, product_rows(): lax.dot_general(left, right, (((0,), (0,)), ((), ())), preferred_element_...  103 us
    dot_general x12, matrix products, product_back(): lax.dot_general(left, right, (((1,), (1,)), ((), ())), preferred_element_...  83.7 us
    reshape x1, local copies, waits for them, and re-layouts, body(): flat_terms.reshape(-1)  77.1 us
    reshape x6, local copies, waits for them, and re-layouts, body(): item.reshape(devices, -1)  45.4 us
    unnamed x1, blocking collectives  42.9 us
  transfers between devices with their start and end apart: 6, of which 1 were waited for; matrix products, arithmetic and copies ran while one was open for 12% of the time, Pallas kernels for 0%

commit v1 on v0

v1 whole, which is shorter than its diff:
```python
import functools

import jax
import jax.numpy as jnp
from jax import lax
from jax.experimental import pallas as pl
from jax.experimental.pallas import tpu as pltpu
from jax.sharding import PartitionSpec as P

D = 1024
HEADS = 16
HD = 64
PAIR = 2 * HD
EPSILON = 1e-06
SCALE = 0.125
LOG2E = 1.4426950408889634
SHORT_ROWS = 256
PAIRS = 2
BF = jnp.bfloat16
F32 = jnp.float32

NN = (((1,), (0,)), ((), ()))
NT = (((1,), (1,)), ((), ()))
TN = (((0,), (0,)), ((), ()))


def mm(left, right, dims):
    return lax.dot_general(left, right, dims, preferred_element_type=F32)


def layer_norm_parts(values):
    row_mean = jnp.mean(values, axis=-1, keepdims=True)
    centered = values - row_mean
    variance = jnp.mean(centered * centered, axis=-1, keepdims=True)
    rstd = lax.rsqrt(variance + EPSILON)
    return centered * rstd, rstd


def layer_norm(values, gain, shift):
    return layer_norm_parts(values)[0] * gain + shift


def norm_back(values, gain, incoming):
    normed, rstd = layer_norm_parts(values)
    scaled = incoming * gain
    grad = rstd * (
        scaled
        - jnp.mean(scaled, axis=-1, keepdims=True)
        - normed * jnp.mean(scaled * normed, axis=-1, keepdims=True)
    )
    return grad, jnp.sum(incoming * normed, axis=0), jnp.sum(incoming, axis=0)


def gelu_exact(values):
    return jax.nn.gelu(values, approximate=False)


def gelu_pair(values):
    half = 0.5 * lax.erfc(-values * (0.5**0.5))
    slope = half + values * (jnp.exp(-0.5 * values * values) * 0.3989422804014327)
    return values * half, slope


def head_lanes(shape, head):
    return (lax.broadcasted_iota(jnp.int32, shape, 1) // HD) == head


def key_mask(scores, length):
    return jnp.where(lax.broadcasted_iota(jnp.int32, scores.shape, 0) < length, scores, -1e30)


def attention_forward_kernel(slots, len_ref, q_ref, k_ref, v_ref, o_ref, lse_ref):
    length = len_ref[pl.program_id(0)]

    def attend(rows, masked):
        for pair in range(PAIRS):
            lanes = pl.ds(pair * PAIR, PAIR)
            q = q_ref[:rows, lanes]
            k = k_ref[:rows, lanes]
            v_t = v_ref[:rows, lanes].T
            outs = []
            for head in range(2):
                q_one = jnp.where(head_lanes(q.shape, head), q, jnp.zeros_like(q))
                scores = mm(k, q_one, NT)
                if masked:
                    scores = key_mask(scores, length)
                top = jnp.max(scores, axis=0, keepdims=True)
                probs = jnp.exp2((scores - top) * (SCALE * LOG2E))
                total = jnp.sum(probs, axis=0, keepdims=True)
                out = mm(v_t[head * HD : (head + 1) * HD], probs.astype(BF), NN)
                outs.append(out * (1.0 / total))
                lse_ref[0, pair * 2 + head : pair * 2 + head + 1, :rows] = top * (
                    SCALE * LOG2E
                ) + jnp.log2(total)
            o_ref[:rows, lanes] = jnp.concatenate(outs, 0).astype(BF).T

    @pl.when(length > SHORT_ROWS)
    def _():
        attend(slots, False)

    @pl.when(length <= SHORT_ROWS)
    def _():
        o_ref[...] = jnp.zeros_like(o_ref)
        lse_ref[...] = jnp.zeros_like(lse_ref)
        attend(SHORT_ROWS, True)


def attention_backward_kernel(
    slots, len_ref, q_ref, k_ref, v_ref, o_ref, do_ref, lse_ref, dq_ref, dk_ref, dv_ref
):
    length = len_ref[pl.program_id(0)]

    def attend(rows, masked):
        for pair in range(PAIRS):
            lanes = pl.ds(pair * PAIR, PAIR)
            q = q_ref[:rows, lanes]
            k = k_ref[:rows, lanes]
            v = v_ref[:rows, lanes]
            do = do_ref[:rows, lanes]
            weighted = o_ref[:rows, lanes].astype(F32) * do.astype(F32)
            k_t = k.T
            zero = jnp.zeros_like(q)
            dqs = []
            dks = []
            dvs = []
            for head in range(2):
                own = head_lanes(q.shape, head)
                ones = jnp.where(head_lanes((8, PAIR), head), 1.0, 0.0)
                row_dot = lax.dot_general(
                    ones, weighted, NT, precision=lax.Precision.HIGHEST, preferred_element_type=F32
                )[0:1]
                scores = mm(k, jnp.where(own, q, zero), NT)
                if masked:
                    scores = key_mask(scores, length)
                lse = lse_ref[0, pair * 2 + head : pair * 2 + head + 1, :rows]
                probs = jnp.exp2(scores * (SCALE * LOG2E) - lse)
                d_probs = mm(v, jnp.where(own, do, zero), NT)
                d_scores = (probs * (d_probs - row_dot)).astype(BF)
                dvs.append(mm(probs.astype(BF), do, NN))
                dks.append(mm(d_scores, q, NN))
                dqs.append(mm(k_t[head * HD : (head + 1) * HD], d_scores, NN))
            low = head_lanes(dks[0].shape, 0)
            dv_ref[:rows, lanes] = jnp.where(low, dvs[0], dvs[1]).astype(BF)
            dk_ref[:rows, lanes] = (jnp.where(low, dks[0], dks[1]) * SCALE).astype(BF)
            dq_ref[:rows, lanes] = (jnp.concatenate(dqs, 0) * SCALE).astype(BF).T

    @pl.when(length > SHORT_ROWS)
    def _():
        attend(slots, False)

    @pl.when(length <= SHORT_ROWS)
    def _():
        for ref in (dq_ref, dk_ref, dv_ref):
            ref[...] = jnp.zeros_like(ref)
        attend(SHORT_ROWS, True)


def head_blocks(slots, part):
    steps = HEADS // (2 * PAIRS)
    return pl.BlockSpec((slots, PAIRS * PAIR), lambda b, h, lens: (b, part * steps + h))


def lse_blocks(slots):
    steps = HEADS // (2 * PAIRS)
    return pl.BlockSpec((1, 2 * PAIRS, slots), lambda b, h, lens: (b * steps + h, 0, 0))


def attention_forward(qkv, lengths):
    images = lengths.shape[0]
    slots = qkv.shape[0] // images
    steps = HEADS // (2 * PAIRS)
    return pl.pallas_call(
        functools.partial(attention_forward_kernel, slots),
        out_shape=(
            jax.ShapeDtypeStruct((images * slots, D), BF),
            jax.ShapeDtypeStruct((images * steps, 2 * PAIRS, slots), F32),
        ),
        grid_spec=pltpu.PrefetchScalarGridSpec(
            num_scalar_prefetch=1,
            grid=(images, steps),
            in_specs=[head_blocks(slots, 0), head_blocks(slots, 1), head_blocks(slots, 2)],
            out_specs=(head_blocks(slots, 0), lse_blocks(slots)),
        ),
        name="attention_forward",
    )(lengths, qkv, qkv, qkv)


def attention_backward(qkv, attended, d_attended, lse, lengths):
    images = lengths.shape[0]
    slots = qkv.shape[0] // images
    steps = HEADS // (2 * PAIRS)
    first = head_blocks(slots, 0)
    return pl.pallas_call(
        functools.partial(attention_backward_kernel, slots),
        out_shape=tuple(jax.ShapeDtypeStruct((images * slots, D), BF) for _ in range(3)),
        grid_spec=pltpu.PrefetchScalarGridSpec(
            num_scalar_prefetch=1,
            grid=(images, steps),
            in_specs=[
                first,
                head_blocks(slots, 1),
                head_blocks(slots, 2),
                first,
                first,
                lse_blocks(slots),
            ],
            out_specs=(first, first, first),
        ),
        name="attention_backward",
    )(lengths, qkv, qkv, qkv, attended, d_attended, lse)


def gather(shard):
    return lax.all_gather(shard, "fsdp", axis=0, tiled=True)


def scatter_sum(grad):
    return lax.psum_scatter(grad.astype(BF), "fsdp", scatter_dimension=0, tiled=True).astype(F32)


def columns(vector, rows):
    return vector.reshape(-1, rows).T


def body(
    tokens,
    lengths,
    cotangent,
    ln1_gain,
    ln1_bias,
    w_qkv,
    b_qv,
    w_out,
    b_out,
    ln2_gain,
    ln2_bias,
    w_up,
    b_up,
    w_down,
    b_down,
    ln3_gain,
    ln3_bias,
    w_learn,
    b_learn,
    w_map,
):
    micro, local, slots, _ = tokens.shape
    images = micro * local
    shard_rows = w_qkv.shape[0]
    devices = D // shard_rows
    vectors = (
        ln1_gain, ln1_bias, b_out, ln2_gain, ln2_bias, b_down, ln3_gain, ln3_bias, b_learn, b_qv, b_up,
    )
    small = jnp.concatenate([columns(item, shard_rows) for item in vectors] + [w_map], axis=1)
    small_count = small.shape[1]
    pad = (-small_count) % 128
    first = gather(jnp.concatenate([w_qkv, jnp.pad(small, ((0, 0), (0, pad)))], axis=1))
    w_qkv = first[:, : 3 * D]
    spread = first[:, 3 * D : 3 * D + small_count]
    lines = spread.reshape(devices, shard_rows, small_count).transpose(2, 0, 1)
    named = []
    offset = 0
    for item in vectors:
        count = item.shape[0] // shard_rows
        part = lines[offset : offset + count].transpose(1, 0, 2).reshape(1, -1)
        named.append(part.astype(F32))
        offset = offset + count
    (ln1_gain, ln1_bias, b_out, ln2_gain, ln2_bias, b_down, ln3_gain, ln3_bias, b_learn, b_qv, b_up) = named
    w_map = spread[:, offset:]
    w_out = gather(w_out)
    w_up = gather(w_up)
    w_down = gather(w_down)
    w_learn = gather(w_learn)

    lengths = lengths.reshape(images)
    row_total = images * slots
    source = tokens.reshape(row_total, D).astype(F32)
    hidden = layer_norm(source, ln1_gain, ln1_bias).astype(BF)
    qkv_bias = jnp.concatenate([b_qv[:, :D], jnp.zeros((1, D), F32), b_qv[:, D:]], axis=1)
    qkv = (mm(hidden, w_qkv, NN) + qkv_bias).astype(BF)
    attended, lse = attention_forward(qkv, lengths)
    middle = source + mm(attended, w_out, NN) + b_out
    normed = layer_norm(middle, ln2_gain, ln2_bias).astype(BF)
    up_act, up_slope = gelu_pair(mm(normed, w_up, NN) + b_up)
    up_act = up_act.astype(BF)
    up_slope = up_slope.astype(BF)
    output = middle + mm(up_act, w_down, NN) + b_down
    learn_in = layer_norm(output, ln3_gain, ln3_bias).astype(BF)
    learn_act, learn_slope = gelu_pair(mm(learn_in, w_learn, NN) + b_learn)
    learn_act = learn_act.astype(BF)
    learn_slope = learn_slope.astype(BF)
    logits = mm(learn_act, w_map, NN)
    slot_valid = lax.broadcasted_iota(jnp.int32, (images, slots, 1), 1) < lengths[:, None, None]
    pool_share = (slot_valid.astype(F32) / lengths[:, None, None].astype(F32)).reshape(row_total, 1)
    squashed = jax.nn.sigmoid(logits)
    pool_maps = (squashed * pool_share).reshape(images, slots, -1)
    by_image = output.reshape(images, slots, D)
    pooled = jnp.einsum("bsm,bsd->bmd", pool_maps, by_image, precision=lax.Precision.HIGHEST)
    pool_grad = cotangent.reshape(images, -1, D)
    d_maps = jnp.einsum("bsd,bmd->bsm", by_image, pool_grad, precision=lax.Precision.HIGHEST)
    d_maps = d_maps.reshape(row_total, -1)
    d_output = jnp.einsum("bsm,bmd->bsd", pool_maps, pool_grad, precision=lax.Precision.HIGHEST)
    d_output = d_output.reshape(row_total, D)
    d_logits = (d_maps * pool_share * squashed * (1.0 - squashed)).astype(BF)
    g_map = mm(learn_act, d_logits, TN)
    d_learn = (learn_slope.astype(F32) * mm(d_logits, w_map, NT)).astype(BF)
    g_blearn = jnp.sum(d_learn.astype(F32), axis=0)
    g_wlearn = scatter_sum(mm(learn_in, d_learn, TN))
    d_norm3, g_ln3, h_ln3 = norm_back(output, ln3_gain, mm(d_learn, w_learn, NT))
    d_output = d_output + d_norm3
    d_mlp = d_output.astype(BF)
    g_bdown = jnp.sum(d_mlp.astype(F32), axis=0)
    g_wdown = scatter_sum(mm(up_act, d_mlp, TN))
    d_up = (up_slope.astype(F32) * mm(d_mlp, w_down, NT)).astype(BF)
    g_bup = jnp.sum(d_up.astype(F32), axis=0)
    g_wup = scatter_sum(mm(normed, d_up, TN))
    d_norm2, g_ln2, h_ln2 = norm_back(middle, ln2_gain, mm(d_up, w_up, NT))
    d_middle = d_output + d_norm2
    d_branch = d_middle.astype(BF)
    g_bout = jnp.sum(d_branch.astype(F32), axis=0)
    g_wout = scatter_sum(mm(attended, d_branch, TN))
    d_attended = mm(d_branch, w_out, NT).astype(BF)
    d_queries, d_keys, d_values = attention_backward(qkv, attended, d_attended, lse, lengths)
    d_qkv = jnp.concatenate([d_queries, d_keys, d_values], axis=1)
    g_bqv = jnp.concatenate(
        [jnp.sum(d_queries.astype(F32), axis=0), jnp.sum(d_values.astype(F32), axis=0)]
    )
    g_wqkv = mm(hidden, d_qkv, TN)
    d_norm1, g_ln1, h_ln1 = norm_back(source, ln1_gain, mm(d_qkv, w_qkv, NT))
    d_image = (d_middle + d_norm1).reshape(tokens.shape)

    grads = (g_ln1, h_ln1, g_bout, g_ln2, h_ln2, g_bdown, g_ln3, h_ln3, g_blearn, g_bqv, g_bup)
    spread = jnp.concatenate(
        [item.reshape(devices, -1, shard_rows).transpose(0, 2, 1).reshape(D, -1) for item in grads]
        + [g_map, jnp.zeros((D, pad), F32)],
        axis=1,
    )
    last = scatter_sum(jnp.concatenate([g_wqkv, spread], axis=1))
    small = last[:, 3 * D :]
    outs = []
    offset = 0
    for item in vectors:
        count = item.shape[0] // shard_rows
        outs.append(small[:, offset : offset + count].T.reshape(-1))
        offset = offset + count
    (g_ln1, h_ln1, g_bout, g_ln2, h_ln2, g_bdown, g_ln3, h_ln3, g_blearn, g_bqv, g_bup) = outs
    g_map = small[:, offset:small_count]
    pooled = pooled.reshape(cotangent.shape)
    return (
        pooled, d_image, g_ln1, h_ln1, last[:, : 3 * D], g_bqv, g_wout, g_bout, g_ln2, h_ln2,
        g_wup, g_bup, g_wdown, g_bdown, g_ln3, h_ln3, g_wlearn, g_blearn, g_map,
    )


def solution(mesh):
    rows = P("fsdp", None)
    line = P("fsdp")
    batch = P(None, "fsdp", None, None)
    params = (line, line, rows, line, rows, line, line, line, rows, line, rows, line, line, line, rows, line, rows)
    return jax.shard_map(
        body,
        mesh=mesh,
        in_specs=(batch, P(None, "fsdp"), batch) + params,
        out_specs=(batch, batch) + params,
        check_vma=False,
    )
```

time: 1830 us -> 1120 us (0.61)
  local copies, waits for them, and re-layouts: 364 us -> 48.2 us
  matrix products: 433 us -> 252 us
  blocking collectives: 120 us -> 0 us
  other arithmetic: 115 us -> 38.8 us
  waiting for transfers between devices: 771 us -> 702 us
  Pallas kernels: 0 us -> 49.8 us
    unnamed x7 -> x10, waiting for transfers between devices: 771 us -> 2.53 us
    reduce_scatter x0 -> x5, waiting for transfers between devices: none -> 487 us  [scatter_sum(): lax.psum_scatter(grad.astype(BF), 'fsdp', scatter_dimension=0, tiled=True)]
    all_gather x5, waiting for transfers between devices: 0.05 us -> 212 us  [gather(): return lax.all_gather(shard, 'fsdp', axis=0, tiled=True)]
    unnamed x334 -> x65, local copies, waits for them, and re-layouts: 207 us -> 11.6 us
    dot_general x54 -> x21, matrix products: 433 us -> 252 us  [the longest x18 239 us: mm(): return lax.dot_general(left, right, dims, preferred_element_type=F32)]
    reshape x13 -> x8, local copies, waits for them, and re-layouts: 126 us -> 3.5 us  [the longest x2 1.63 us: columns(): return vector.reshape(-1, rows).T]
    all_gather x2 -> x0, blocking collectives: 77.6 us -> none  [the longest x1 40.1 us: body(): lax.all_gather(shards[9], 'fsdp', axis=0, tiled=True)]
    pallas_call x0 -> x2, Pallas kernels: none -> 49.8 us  [the longest x1 30.5 us: attention_backward(): pl.pallas_call(functools.partial(attention_backward_kernel, slots), out_s...]
  transfers between devices with their start and end apart: 6 -> 10, of which waited for: 1 -> 9; matrix products, arithmetic and copies ran while one was open for 12% -> 27% of each run, Pallas kernels for 0% -> 5%
where the time goes in v1:
time: 1120 us; the launch traced here: 1110 us
  waiting for transfers between devices  702 us (63%)
  matrix products  252 us (22%)
  Pallas kernels  49.8 us (4%)
  local copies, waits for them, and re-layouts  48.2 us (4%)
  other arithmetic  38.8 us (3%)
  between operations  15.1 us (1%)
    reduce_scatter x5, waiting for transfers between devices, scatter_sum(): lax.psum_scatter(grad.astype(BF), 'fsdp', scatter_dimension=0, tiled=True)  487 us
    dot_general x18, matrix products, mm(): return lax.dot_general(left, right, dims, preferred_element_type=F32)  239 us
    all_gather x5, waiting for transfers between devices, gather(): return lax.all_gather(shard, 'fsdp', axis=0, tiled=True)  212 us
    pallas_call x1, Pallas kernels, attention_backward(): pl.pallas_call(functools.partial(attention_backward_kernel, slots), out_s...  30.5 us
  transfers between devices with their start and end apart: 10, of which 9 were waited for; matrix products, arithmetic and copies ran while one was open for 27% of the time, Pallas kernels for 5%

profile of v1, /device:TPU:0, one launch (start us, length us, event | category | flops | bytes accessed | tf_op | source)
XLA Modules:
  0.0 1106.4 jit_solution(9592315873655187583)
XLA Ops:
  8.9 2.3 concatenate.25
  11.3 1.6 fusion.52
  15.6 2.1 convert_reduce_fusion
  19.4 67.0 %all-gather.6.cloned.1.call-done = bf16[1024,3200]{1,0:T(8,128)(2,1)} async-done(((bf16[32,3200]{1,0:T(8,128)(2,1)}), bf16[1024,3200]{1,0:T(8,128)(2,1)}) %all-gather.6.cloned.1.call-update) | async-done | bytes 6553616 | tf_op jit(solution)/shard_map/all_gather | solution.py:214
  93.6 12.2 %add_convert_fusion.q_ref.k_ref.v_ref = bf16[1152,3072]{1,0:T(8,128)(2,1)} fusion(bf16[1152,1024]{1,0:T(8,128)(2,1)S(1)} %fusion.32, f32[3072]{0:T(1024)S(1)} %bitcast.119, bf16[1024,3200]{1,0:T(8,128)(2,1)} %all-gather.6.cloned.1.call-done), kind=kOutput, calls=%fused_computation.27 | convolution fusion | flops 7254835200 | bytes 15740928 | tf_op jit(solution)/shard_map/dot_general | solution.py:28
  105.8 19.3 %attention_forward.1 = (bf16[1152,1024]{1,0:T(8,128)(2,1)}, f32[8,4,576]{2,1,0:T(4,128)}) custom-call(s32[2]{0:T(128)} %bitcast.120, bf16[1152,3072]{1,0:T(8,128)(2,1)} %add_convert_fusion.q_ref.k_ref.v_ref, bf16[1152,3072]{1,0:T(8,128)(2,1)} %add_convert_fusion.q_ref.k_ref.v_ref, bf16[1152,3072]{1,0:T(8,128)(2,1)} %add_convert_fusion.q_ref.k_ref.v_ref), custom_call_target="tpu_custom_call" | custom-call | tf_op jit(solution)/shard_map/attention_forward/pallas_call | solution.py:172
  125.1 19.1 %all-gather.8.cloned.1.call-done = bf16[1024,1024]{1,0:T(8,128)(2,1)} async-done(((bf16[32,1024]{1,0:T(8,128)(2,1)}), bf16[1024,1024]{1,0:T(8,128)(2,1)}) %all-gather.8.cloned.1.call-update) | async-done | bytes 2097168 | tf_op jit(solution)/shard_map/all_gather | solution.py:214
  144.2 5.3 fusion.69
  149.5 2.2 copy-done.5
  152.3 71.1 %all-gather.10.cloned.1.call-done = bf16[1024,4096]{1,0:T(8,128)(2,1)} async-done(((bf16[32,4096]{1,0:T(8,128)(2,1)}), bf16[1024,4096]{1,0:T(8,128)(2,1)}) %all-gather.10.cloned.1.call-update) | async-done | bytes 8388624 | tf_op jit(solution)/shard_map/all_gather | solution.py:214
  223.4 56.4 %multiply_convert_fusion = (bf16[1152,4096]{1,0:T(8,128)(2,1)}, f32[1152,4096]{1,0:T(8,128)}, f32[1152,4096]{1,0:T(8,128)}) fusion(f32[4096]{0:T(1024)S(1)} %reshape.359, bf16[1024,4096]{1,0:T(8,128)(2,1)} %all-gather.10.cloned.1.call-done, f32[1152,1024]{1,0:T(8,128)} %copy-done.5, f32[1024]{0:T(1024)S(1)} %reshape.358, f32[1024]{0:T(1024)S(1)} %reshape.357, ...), kind=kOutput, calls=%fused_computation.10 | convolution fusion | flops 9981001728 | bytes 60326912 | tf_op jit(solution)/shard_map/dot_general | solution.py:28
  279.8 22.4 %all-gather.12.cloned.1.call-done = bf16[4096,1024]{1,0:T(8,128)(2,1)} async-done(((bf16[128,1024]{1,0:T(8,128)(2,1)}), bf16[4096,1024]{1,0:T(8,128)(2,1)}) %all-gather.12.cloned.1.call-update) | async-done | bytes 8388624 | tf_op jit(solution)/shard_map/all_gather | solution.py:214
  302.2 15.7 %fusion.70 = (f32[1152]{0:T(1024)S(1)}, f32[1152,1024]{1,0:T(8,128)S(1)}) fusion(f32[1024]{0:T(1024)S(1)} %copy-done.27, f32[1152,1024]{1,0:T(8,128)} %copy-done.5, bf16[1152,4096]{1,0:T(8,128)(2,1)} %get-tuple-element.113, bf16[4096,1024]{1,0:T(8,128)(2,1)} %all-gather.12.cloned.1.call-done), kind=kOutput, calls=%fused_computation.170 | convolution fusion | flops 9667214336 | bytes 27271680 | tf_op jit(solution)/shard_map/dot_general | solution.py:28
  318.0 2.1 copy-done.1
  320.1 4.1 fusion.53
  324.3 2.9 multiply_reduce_fusion.4
  327.3 32.7 %all-gather.14.cloned.1.call-done = bf16[1024,1024]{1,0:T(8,128)(2,1)} async-done(((bf16[32,1024]{1,0:T(8,128)(2,1)}), bf16[1024,1024]{1,0:T(8,128)(2,1)}) %all-gather.14.cloned.1.call-update) | async-done | bytes 2097168 | tf_op jit(solution)/shard_map/all_gather | solution.py:214
  360.0 16.8 %multiply_convert_fusion.1 = (bf16[1152,1024]{1,0:T(8,128)(2,1)S(1)}, f32[1152,1024]{1,0:T(8,128)}, f32[1152,1024]{1,0:T(8,128)}) fusion(f32[1024]{0:T(1024)S(1)} %copy-done.26, bf16[1024,1024]{1,0:T(8,128)(2,1)} %all-gather.14.cloned.1.call-done, f32[1152,1024]{1,0:T(8,128)} %copy-done.1, f32[1024]{0:T(1024)S(1)} %copy-done.24, f32[1024]{0:T(1024)S(1)} %copy-done.20, ...), kind=kOutput, calls=%fused_computation.69 | convolution fusion | flops 2499674112 | bytes 18633728 | tf_op jit(solution)/shard_map/dot_general | solution.py:28
  376.7 1.8 multiply_convert_fusion.2
  379.2 5.8 fusion.71
  385.3 4.4 convolution_convert_fusion.4
  389.8 6.6 multiply_reduce_fusion
  396.8 3.9 fusion.55
  400.7 4.8 convert_reduce_fusion.2
  405.5 25.5 %fusion.72 = (bf16[4096]{0:T(1024)(128)(2,1)S(1)}, bf16[1152,4096]{1,0:T(8,128)(2,1)}) fusion(bf16[4096,1024]{1,0:T(8,128)(2,1)} %all-gather.12.cloned.1.call-done, f32[1152,1024]{1,0:T(8,128)} %get-tuple-element.108, f32[1152,4096]{1,0:T(8,128)} %get-tuple-element.114, f32[1152,4096]{1,0:T(8,128)} %get-tuple-element.134), kind=kOutput, calls=%fused_computation.172 | convolution fusion | flops 9712037888 | bytes 60301312 | tf_op jit(solution)/shard_map/dot_general | solution.py:28
  432.1 17.0 %multiply_reduce_fusion.1 = (bf16[1024]{0:T(1024)(128)(2,1)S(1)}, f32[1152]{0:T(1024)S(1)}, f32[1152]{0:T(1024)S(1)}, bf16[1024]{0:T(1024)(128)(2,1)S(1)}, f32[1152,1024]{1,0:T(8,128)S(1)}) fusion(f32[1152,1024]{1,0:T(8,128)} %copy-done.5, f32[1152]{0:T(1024)S(1)} %add_rsqrt_fusion.1, f32[1152]{0:T(1024)S(1)} %broadcast_multiply_fusion.8, ...), kind=kOutput, calls=%fused_computation.65 | convolution fusion | flops 9674289152 | bytes 27289600 | tf_op jit(solution)/shard_map/dot_general | solution.py:28
  449.2 3.6 convert_reduce_fusion.1
  456.9 3.9 convolution_convert_fusion.3.do_ref
  460.9 30.5 %attention_backward.1 = (bf16[1152,1024]{1,0:T(8,128)(2,1)}, bf16[1152,1024]{1,0:T(8,128)(2,1)}, bf16[1152,1024]{1,0:T(8,128)(2,1)}) custom-call(s32[2]{0:T(128)} %bitcast.121, bf16[1152,3072]{1,0:T(8,128)(2,1)} %add_convert_fusion.q_ref.k_ref.v_ref, bf16[1152,3072]{1,0:T(8,128)(2,1)} %add_convert_fusion.q_ref.k_ref.v_ref, ...), custom_call_target="tpu_custom_call" | custom-call | tf_op jit(solution)/shard_map/attention_backward/pallas_call | solution.py:193
  491.4 4.0 fusion.66
  495.5 6.5 convolution_convert_fusion.5
  502.1 3.6 constant_dynamic-update-slice_fusion.1
  505.7 3.8 fusion.67
  510.6 14.4 %fusion.37 = (bf16[1024]{0:T(1024)(128)(2,1)S(1)}, f32[1152]{0:T(1024)S(1)}, f32[1152]{0:T(1024)S(1)}, bf16[1024]{0:T(1024)(128)(2,1)S(1)}, f32[1152,1024]{1,0:T(8,128)}) fusion(bf16[2,1,576,1024]{3,2,1,0:T(8,128)(2,1)S(1)} %copy-done.3, f32[1152]{0:T(1024)S(1)} %copy-done.16, f32[1152]{0:T(1024)S(1)} %copy-done.14, f32[1024]{0:T(1024)S(1)} %copy-done.18, ...), kind=kOutput, calls=%fused_computation.62 | convolution fusion | flops 7259549696 | bytes 20473856 | tf_op jit(solution)/shard_map/dot_general | solution.py:28
  526.9 10.2 convolution_convert_fusion.2
  537.8 12.5 %concatenate.32 = bf16[1024,3200]{1,0:T(8,128)(2,1)} concatenate(bf16[1024,3072]{1,0:T(8,128)(2,1)} %convolution_convert_fusion.2, bf16[1024,1]{1,0:T(8,128)(2,1)} %reshape_transpose_reshape.45, bf16[1024,1]{1,0:T(8,128)(2,1)} %reshape_transpose_reshape.46, bf16[1024,1]{1,0:T(8,128)(2,1)} %reshape_transpose_reshape.47, bf16[1024,1]{1,0:T(8,128)(2,1)} %reshape_transpose_reshape.48, ...), dimensions={1} | concatenate | bytes 13107200 | tf_op jit(solution)/shard_map/concatenate | solution.py:338
  551.0 17.9 %convolution_convert_fusion.1 = bf16[1024,4096]{1,0:T(8,128)(2,1)} fusion(bf16[1152,4096]{1,0:T(8,128)(2,1)} %get-tuple-element.144, f32[1152,1024]{1,0:T(8,128)} %copy-done.5, f32[1024]{0:T(1024)S(1)} %copy-done.23, f32[1024]{0:T(1024)S(1)} %reshape.357, f32[1152]{0:T(1024)S(1)} %add_rsqrt_fusion.1, f32[1152]{0:T(1024)S(1)} %broadcast_multiply_fusion.8), kind=kOutput, calls=%fused_computation.29 | convolution fusion | flops 9673768960 | bytes 22561792 | tf_op jit(solution)/shard_map/dot_general | solution.py:28
  568.9 18.0 %convolution_convert_fusion = bf16[4096,1024]{1,0:T(8,128)(2,1)} fusion(bf16[1152,4096]{1,0:T(8,128)(2,1)} %get-tuple-element.113, f32[1152,1024]{1,0:T(8,128)} %get-tuple-element.108), kind=kOutput, calls=%fused_computation.28 | convolution fusion | flops 9669050368 | bytes 22544384 | tf_op jit(solution)/shard_map/dot_general | solution.py:28
  587.7 5.3 convolution_bitcast_fusion
  593.0 6.0 fusion.36
  599.1 1.5 convert_element_type.313
  600.6 59.1 %reduce-scatter.8.cloned.1.call-done = bf16[32,1024]{1,0:T(8,128)(2,1)} async-done(((bf16[1024,1024]{1,0:T(8,128)(2,1)}), bf16[32,1024]{1,0:T(8,128)(2,1)}) %reduce-scatter.8.cloned.1.call-update) | async-done | bytes 65552 | tf_op jit(solution)/shard_map/reduce_scatter | solution.py:218
  661.2 142.0 %reduce-scatter.6.cloned.1.call-done = bf16[32,3200]{1,0:T(8,128)(2,1)} async-done(((bf16[1024,3200]{1,0:T(8,128)(2,1)}), bf16[32,3200]{1,0:T(8,128)(2,1)}) %reduce-scatter.6.cloned.1.call-update) | async-done | bytes 204816 | tf_op jit(solution)/shard_map/reduce_scatter | solution.py:218
  807.0 1.7 slice.148
  809.6 140.8 %reduce-scatter.10.cloned.1.call-done = bf16[32,4096]{1,0:T(8,128)(2,1)} async-done(((bf16[1024,4096]{1,0:T(8,128)(2,1)}), bf16[32,4096]{1,0:T(8,128)(2,1)}) %reduce-scatter.10.cloned.1.call-update) | async-done | bytes 262160 | tf_op jit(solution)/shard_map/reduce_scatter | solution.py:218
  950.4 1.8 convert_element_type.309
  952.2 145.2 %reduce-scatter.12.cloned.1.call-done = bf16[128,1024]{1,0:T(8,128)(2,1)} async-done(((bf16[4096,1024]{1,0:T(8,128)(2,1)}), bf16[128,1024]{1,0:T(8,128)(2,1)}) %reduce-scatter.12.cloned.1.call-update) | async-done | bytes 262160 | tf_op jit(solution)/shard_map/reduce_scatter | solution.py:218
  1097.4 1.8 convert_element_type.311
  (158 shorter events, 32.1 us)
Async XLA Ops:
  7.2 312.9 %copy-start = (f32[2,1,8,1024]{3,2,1,0:T(8,128)S(1)}, f32[2,1,8,1024]{3,2,1,0:T(8,128)}, u32[]{:S(2)}) copy-start(f32[2,1,8,1024]{3,2,1,0:T(8,128)} %param.22) | copy-start | bytes 196612
  7.2 10.5 copy-start.2
  7.2 11.3 %copy-start.21 = (s32[2,1]{0,1:T(1,128)S(1)}, s32[2,1]{0,1:T(1,128)}, u32[]{:S(2)}) copy-start(s32[2,1]{0,1:T(1,128)} %param.21) | copy-start | bytes 28
  7.2 79.2 %all-gather.6.cloned.1.call-start = ((), (), s32[]{:S(2)}) async-start(), calls=%async_computation.5 | async-start | bytes 6758400 | tf_op jit(solution)/shard_map/all_gather | solution.py:214
  12.9 131.3 %all-gather.8.cloned.1.call-start = ((), (), s32[]{:S(2)}) async-start(), calls=%async_computation.6 | async-start | bytes 2162688 | tf_op jit(solution)/shard_map/all_gather | solution.py:214
  13.7 209.7 %all-gather.10.cloned.1.call-start = ((), (), s32[]{:S(2)}) async-start(), calls=%async_computation.7 | async-start | bytes 8650752 | tf_op jit(solution)/shard_map/all_gather | solution.py:214
  14.4 287.8 %all-gather.12.cloned.1.call-start = ((), (), s32[]{:S(2)}) async-start(), calls=%async_computation.8 | async-start | bytes 8650752 | tf_op jit(solution)/shard_map/all_gather | solution.py:214
  15.0 345.0 %all-gather.14.cloned.1.call-start = ((), (), s32[]{:S(2)}) async-start(), calls=%async_computation.9 | async-start | bytes 2162688 | tf_op jit(solution)/shard_map/all_gather | solution.py:214
  15.6 583.5 %reduce-scatter.14.cloned.1.call-start = ((), (), s32[]{:S(2)}) async-start(), calls=%async_computation.14 | async-start | bytes 2162688 | tf_op jit(solution)/shard_map/reduce_scatter | solution.py:218
  18.5 87.3 %copy-start.13 = (f32[1152]{0:T(1024)}, f32[1152]{0:T(1024)S(1)}, u32[]{:S(2)}) copy-start(f32[1152]{0:T(1024)S(1)} %div.65) | copy-start | bytes 13828
  19.4 86.4 %copy-start.15 = (f32[1152]{0:T(1024)}, f32[1152]{0:T(1024)S(1)}, u32[]{:S(2)}) copy-start(f32[1152]{0:T(1024)S(1)} %rsqrt.31) | copy-start | bytes 13828
  89.0 16.8 %copy-start.17 = (f32[1024]{0:T(1024)}, f32[1024]{0:T(1024)S(1)}, u32[]{:S(2)}) copy-start(f32[1024]{0:T(1024)S(1)} %reshape.353) | copy-start | bytes 12292
  89.7 133.7 %copy-start.22 = (f32[1024]{0:T(1024)}, f32[1024]{0:T(1024)S(1)}, u32[]{:S(2)}) copy-start(f32[1024]{0:T(1024)S(1)} %reshape.358) | copy-start | bytes 12292
  92.1 1.5 copy-start.8
  149.5 2.2 copy-start.5
  223.4 78.8 %copy-start.27 = (f32[1024]{0:T(1024)S(1)}, f32[1024]{0:T(1024)}, u32[]{:S(2)}) copy-start(f32[1024]{0:T(1024)} %reshape.360) | copy-start | bytes 12292
  317.9 2.1 copy-start.1
  320.1 39.9 %copy-start.20 = (f32[1024]{0:T(1024)S(1)}, f32[1024]{0:T(1024)}, u32[]{:S(2)}) copy-start(f32[1024]{0:T(1024)} %reshape.361) | copy-start | bytes 12292
  320.1 39.9 %copy-start.24 = (f32[1024]{0:T(1024)S(1)}, f32[1024]{0:T(1024)}, u32[]{:S(2)}) copy-start(f32[1024]{0:T(1024)} %reshape.362) | copy-start | bytes 12292
  320.1 39.9 %copy-start.26 = (f32[1024]{0:T(1024)S(1)}, f32[1024]{0:T(1024)}, u32[]{:S(2)}) copy-start(f32[1024]{0:T(1024)} %reshape.363) | copy-start | bytes 12292
  327.3 49.5 %copy-start.19 = (f32[1152]{0:T(1024)S(1)}, f32[1152]{0:T(1024)}, u32[]{:S(2)}) copy-start(f32[1152]{0:T(1024)} %div.74) | copy-start | bytes 13828
  378.5 6.8 slice-start
  379.0 17.7 %copy-start.11 = (f32[2,576,8]{1,0,2:T(2,128)}, f32[2,576,8]{1,0,2:T(2,128)S(1)}, u32[]{:S(2)}) copy-start(f32[2,576,8]{1,0,2:T(2,128)S(1)} %reshape.340) | copy-start | bytes 110596
  379.2 6.1 slice-start.1
  379.2 6.1 copy-start.25
  389.7 269.9 %reduce-scatter.8.cloned.1.call-start = ((), (), s32[]{:S(2)}) async-start(), calls=%async_computation.11 | async-start | bytes 2162688 | tf_op jit(solution)/shard_map/reduce_scatter | solution.py:218
  432.1 17.1 %copy-start.6 = (f32[1152,1024]{1,0:T(8,128)S(1)}, f32[1152,1024]{1,0:T(8,128)}, u32[]{:S(2)}) copy-start(f32[1152,1024]{1,0:T(8,128)} %get-tuple-element.108) | copy-start | bytes 14155780
  449.2 7.8 copy-start.28
  452.8 8.1 copy-start.4
  491.4 4.1 copy-start.7
  502.0 301.1 %reduce-scatter.6.cloned.1.call-start = ((), (), s32[]{:S(2)}) async-start(), calls=%async_computation.10 | async-start | bytes 6758400 | tf_op jit(solution)/shard_map/reduce_scatter | solution.py:218
  502.0 8.5 copy-start.3
  502.1 8.5 copy-start.14
  502.1 8.5 copy-start.16
  502.1 8.5 copy-start.18
  510.6 16.3 %copy-start.9 = (bf16[1152,1024]{1,0:T(8,128)(2,1)S(1)}, bf16[1152,1024]{1,0:T(8,128)(2,1)}, u32[]{:S(2)}) copy-start(bf16[1152,1024]{1,0:T(8,128)(2,1)} %copy-done.8) | copy-start | bytes 7077892
  510.6 16.3 %copy-start.10 = (bf16[1152,3072]{1,0:T(8,128)(2,1)S(1)}, bf16[1152,3072]{1,0:T(8,128)(2,1)}, u32[]{:S(2)}) copy-start(bf16[1152,3072]{1,0:T(8,128)(2,1)} %get-tuple-element.118) | copy-start | bytes 21233668
  550.3 0.7 copy-start.23
  550.3 400.1 %reduce-scatter.10.cloned.1.call-start = ((), (), s32[]{:S(2)}) async-start(), calls=%async_computation.12 | async-start | bytes 8650752 | tf_op jit(solution)/shard_map/reduce_scatter | solution.py:218
  568.9 528.5 %reduce-scatter.12.cloned.1.call-start = ((), (), s32[]{:S(2)}) async-start(), calls=%async_computation.13 | async-start | bytes 8650752 | tf_op jit(solution)/shard_map/reduce_scatter | solution.py:218
  587.0 0.8 copy-start.12
Sparse Core Ops, SparseCore 0:
  13.0 73.3 all-gather.5
  89.3 54.8 all-gather.7
  147.1 76.2 all-gather.9
  226.1 76.0 all-gather.11
  304.9 55.0 all-gather.13
  389.8 135.1 reduce-scatter.13
  527.4 132.2 reduce-scatter.7
  662.0 141.1 reduce-scatter.5
  805.4 144.9 reduce-scatter.9
  952.5 144.7 reduce-scatter.11

commit v2 on v1

--- a/solution.py
+++ b/solution.py
@@ -51,14 +51,131 @@
     return grad, jnp.sum(incoming * normed, axis=0), jnp.sum(incoming, axis=0)
 
 
-def gelu_exact(values):
-    return jax.nn.gelu(values, approximate=False)
-
-
-def gelu_pair(values):
-    half = 0.5 * lax.erfc(-values * (0.5**0.5))
-    slope = half + values * (jnp.exp(-0.5 * values * values) * 0.3989422804014327)
-    return values * half, slope
+ERFCX = (
+    0.18636609783492827,
+    0.1828374067871815,
+    0.2019228837403338,
+    0.045013532984771946,
+    0.4125364399329413,
+    -0.3554335531070661,
+    0.46268519224041466,
+    -0.13592808196895617,
+)
+ERFCX_SCALE = 0.33
+
+
+def gelu_with_slope(values):
+    near = 1.0 / (1.0 + jnp.abs(values) * (ERFCX_SCALE * 0.5**0.5))
+    series = 0.5 * ERFCX[-1] * near + 0.5 * ERFCX[-2]
+    for item in ERFCX[-3::-1]:
+        series = series * near + 0.5 * item
+    bell = jnp.exp2((values * values) * (-0.5 * LOG2E))
+    tail = (bell * near) * series
+    half = jnp.where(values < 0, tail, 1.0 - tail)
+    return values * half, half + values * (bell * 0.3989422804014327)
+
+
+def gelu_matmul_kernel(chunk, tiles, x_ref, b_ref, *refs):
+    w_refs = refs[: len(tiles)]
+    act_ref, slope_ref = refs[len(tiles) :]
+    step = pl.program_id(0)
+    first = 0
+    for w_ref, count in zip(w_refs, tiles):
+
+        @pl.when((step >= first) & (step < first + count))
+        def _(w_ref=w_ref):
+            for start in range(0, x_ref.shape[0], chunk):
+                rows = pl.ds(start, chunk)
+                act, slope = gelu_with_slope(mm(x_ref[rows], w_ref[...], NN) + b_ref[...])
+                act_ref[rows] = act.astype(BF)
+                slope_ref[rows] = slope.astype(BF)
+
+        first = first + count
+
+
+def slope_matmul_kernel(chunk, x_ref, w_ref, slope_ref, out_ref, sum_ref):
+    total = jnp.zeros(sum_ref.shape, F32)
+    for start in range(0, x_ref.shape[0], chunk):
+        rows = pl.ds(start, chunk)
+        out = (mm(x_ref[rows], w_ref[...], NT) * slope_ref[rows].astype(F32)).astype(BF)
+        out_ref[rows] = out
+        total = total + jnp.sum(out.astype(F32), axis=0, keepdims=True)
+    sum_ref[...] = total
+
+
+def light():
+    return pl.CostEstimate(flops=1024, bytes_accessed=1024, transcendentals=0)
+
+
+def gelu_matmul(x, pieces, bias):
+    rows, inner = x.shape
+    tile = 512
+    width = bias.shape[1]
+    tiles = [item[2] // tile for item in pieces]
+    specs = []
+    before = 0
+    for (_, first, _), count in zip(pieces, tiles):
+
+        def place(j, first=first, before=before, count=count):
+            return 0, first // tile + jnp.clip(j - before, 0, count - 1)
+
+        specs.append(pl.BlockSpec((inner, tile), place))
+        before = before + count
+    out = pl.BlockSpec((rows, tile), lambda j: (0, j))
+    return pl.pallas_call(
+        functools.partial(gelu_matmul_kernel, rows // 4, tiles),
+        out_shape=(jax.ShapeDtypeStruct((rows, width), BF),) * 2,
+        grid=(width // tile,),
+        in_specs=[pl.BlockSpec((rows, inner), lambda j: (0, 0)), pl.BlockSpec((1, tile), lambda j: (0, j))] + specs,
+        out_specs=(out, out),
+        cost_estimate=light(),
+        name="gelu_matmul",
+    )(x, bias, *[item[0] for item in pieces])
+
+
+def back_product_kernel(count, *refs):
+    total = mm(refs[0][...], refs[count][...], NT)
+    for i in range(1, count):
+        total = total + mm(refs[i][...], refs[count + i][...], NT)
+    refs[-1][...] = total
+
+
+def back_product(pieces, w):
+    count = len(pieces)
+    rows, width = pieces[0].shape
+    height = w.shape[0]
+    tile = 512
+    whole = pl.BlockSpec((rows, width), lambda j: (0, 0))
+    parts = [pl.BlockSpec((tile, width), lambda j, i=i: (j, i)) for i in range(count)]
+    return pl.pallas_call(
+        functools.partial(back_product_kernel, count),
+        out_shape=jax.ShapeDtypeStruct((rows, height), F32),
+        grid=(height // tile,),
+        in_specs=[whole] * count + parts,
+        out_specs=pl.BlockSpec((rows, tile), lambda j: (0, j)),
+        cost_estimate=light(),
+        name="back_product",
+    )(*pieces, *[w] * count)
+
+
+def slope_matmul(x, w, slope):
+    rows, inner = x.shape
+    width = w.shape[0]
+    tile = 1024
+    block = pl.BlockSpec((rows, tile), lambda j: (0, j))
+    return pl.pallas_call(
+        functools.partial(slope_matmul_kernel, rows // 4),
+        out_shape=(jax.ShapeDtypeStruct((rows, width), BF), jax.ShapeDtypeStruct((1, width), F32)),
+        grid=(width // tile,),
+        in_specs=[
+            pl.BlockSpec((rows, inner), lambda j: (0, 0)),
+            pl.BlockSpec((tile, inner), lambda j: (j, 0)),
+            block,
+        ],
+        out_specs=(block, pl.BlockSpec((1, tile), lambda j: (0, j))),
+        cost_estimate=light(),
+        name="slope_matmul",
+    )(x, w, slope)
 
 
 def head_lanes(shape, head):
@@ -69,8 +186,8 @@
     return jnp.where(lax.broadcasted_iota(jnp.int32, scores.shape, 0) < length, scores, -1e30)
 
 
-def attention_forward_kernel(slots, len_ref, q_ref, k_ref, v_ref, o_ref, lse_ref):
-    length = len_ref[pl.program_id(0)]
+def attention_forward_kernel(slots, image, len_ref, q_ref, k_ref, v_ref, o_ref, lse_ref):
+    length = len_ref[image]
 
     def attend(rows, masked):
         for pair in range(PAIRS):
@@ -106,9 +223,9 @@
 
 
 def attention_backward_kernel(
-    slots, len_ref, q_ref, k_ref, v_ref, o_ref, do_ref, lse_ref, dq_ref, dk_ref, dv_ref
+    slots, image, len_ref, q_ref, k_ref, v_ref, o_ref, do_ref, lse_ref, dq_ref, dk_ref, dv_ref
 ):
-    length = len_ref[pl.program_id(0)]
+    length = len_ref[image]
 
     def attend(rows, masked):
         for pair in range(PAIRS):
@@ -155,59 +272,72 @@
         attend(SHORT_ROWS, True)
 
 
-def head_blocks(slots, part):
+def head_blocks(slots, image, part=0):
+    first = part * (HEADS // (2 * PAIRS))
+    return pl.BlockSpec((slots, PAIRS * PAIR), lambda h, lens: (image, first + h))
+
+
+def lse_blocks(slots, image):
     steps = HEADS // (2 * PAIRS)
-    return pl.BlockSpec((slots, PAIRS * PAIR), lambda b, h, lens: (b, part * steps + h))
-
-
-def lse_blocks(slots):
-    steps = HEADS // (2 * PAIRS)
-    return pl.BlockSpec((1, 2 * PAIRS, slots), lambda b, h, lens: (b * steps + h, 0, 0))
-
-
-def attention_forward(qkv, lengths):
+    return pl.BlockSpec((1, 2 * PAIRS, slots), lambda h, lens: (image * steps + h, 0, 0))
+
+
+def held_in_place(kernel, count):
+    def whole(len_ref, *refs):
+        return kernel(len_ref, *refs[count:])
+
+    return whole
+
+
+def attention_forward(image, qkv, lengths, filled):
     images = lengths.shape[0]
     slots = qkv.shape[0] // images
     steps = HEADS // (2 * PAIRS)
+    block = head_blocks(slots, image)
+    outs = (block, lse_blocks(slots, image))
+    kernel = functools.partial(attention_forward_kernel, slots, image)
+    anywhere = [pl.BlockSpec(memory_space=pl.ANY)] * len(filled)
     return pl.pallas_call(
-        functools.partial(attention_forward_kernel, slots),
+        held_in_place(kernel, len(filled)),
         out_shape=(
             jax.ShapeDtypeStruct((images * slots, D), BF),
             jax.ShapeDtypeStruct((images * steps, 2 * PAIRS, slots), F32),
         ),
         grid_spec=pltpu.PrefetchScalarGridSpec(
             num_scalar_prefetch=1,
-            grid=(images, steps),
-            in_specs=[head_blocks(slots, 0), head_blocks(slots, 1), head_blocks(slots, 2)],
-            out_specs=(head_blocks(slots, 0), lse_blocks(slots)),
+            grid=(steps,),
+            in_specs=anywhere + [head_blocks(slots, image, part) for part in range(3)],
+            out_specs=outs,
         ),
+        input_output_aliases={1 + i: i for i in range(len(filled))},
+        cost_estimate=light(),
         name="attention_forward",
-    )(lengths, qkv, qkv, qkv)
-
-
-def attention_backward(qkv, attended, d_attended, lse, lengths):
+    )(lengths, *filled, qkv, qkv, qkv)
+
+
+def attention_backward(image, qkv, attended, d_attended, lse, lengths, filled):
     images = lengths.shape[0]
     slots = qkv.shape[0] // images
     steps = HEADS // (2 * PAIRS)
-    first = head_blocks(slots, 0)
+    block = head_blocks(slots, image)
+    kernel = functools.partial(attention_backward_kernel, slots, image)
+    anywhere = [pl.BlockSpec(memory_space=pl.ANY)] * len(filled)
     return pl.pallas_call(
-        functools.partial(attention_backward_kernel, slots),
+        held_in_place(kernel, len(filled)),
         out_shape=tuple(jax.ShapeDtypeStruct((images * slots, D), BF) for _ in range(3)),
         grid_spec=pltpu.PrefetchScalarGridSpec(
             num_scalar_prefetch=1,
-            grid=(images, steps),
-            in_specs=[
-                first,
-                head_blocks(slots, 1),
-                head_blocks(slots, 2),
-                first,
-                first,
-                lse_blocks(slots),
-            ],
-            out_specs=(first, first, first),
+            grid=(steps,),
+            in_specs=anywhere
+            + [head_blocks(slots, image, part) for part in range(3)]
+            + [block] * 2
+            + [lse_blocks(slots, image)],
+            out_specs=(block, block, block),
         ),
+        input_output_aliases={1 + i: i for i in range(len(filled))},
+        cost_estimate=light(),
         name="attention_backward",
-    )(lengths, qkv, qkv, qkv, attended, d_attended, lse)
+    )(lengths, *filled, qkv, qkv, qkv, attended, d_attended, lse)
 
 
 def gather(shard):
@@ -218,8 +348,128 @@
     return lax.psum_scatter(grad.astype(BF), "fsdp", scatter_dimension=0, tiled=True).astype(F32)
 
 
-def columns(vector, rows):
-    return vector.reshape(-1, rows).T
+def bit_value(bit):
+    return (lax.axis_index("fsdp") >> bit) & 1
+
+
+def swap(value, bit):
+    count = lax.axis_size("fsdp")
+    return lax.ppermute(value, "fsdp", [(i, i ^ (1 << bit)) for i in range(count)])
+
+
+def pick(value, axis, index):
+    return lax.dynamic_index_in_dim(value, index, axis, keepdims=False)
+
+
+def rotations():
+    bits = (lax.axis_size("fsdp") - 1).bit_length()
+    if bits == 5:
+        return ((1, 2, 3, 4), (2, 3, 4, 1), (3, 4, 1, 2))
+    rest = tuple(range(1, bits))
+    third = max(1, len(rest) // 3)
+    return (rest, rest[third:] + rest[:third], rest[2 * third :] + rest[: 2 * third])
+
+
+def tie(*values):
+    return lax.optimization_barrier(values)
+
+
+class Gathering:
+    def __init__(self, shard, order):
+        self.width = shard.shape[-1]
+        self.order = tuple(reversed(order)) + (0,)
+        self.held = shard
+        self.have = []
+        self.other = None
+
+    def send(self):
+        if len(self.have) < len(self.order):
+            self.other = swap(self.held, self.order[len(self.have)])
+
+    def step(self, value):
+        self.join()
+        if len(self.have) < len(self.order):
+            self.held, value = tie(self.held, value)
+        self.send()
+        return value
+
+    def join(self):
+        if self.other is None:
+            return
+        bit = self.order[len(self.have)]
+        place = sum(1 for item in self.have if item > bit)
+        shape = self.held.shape[:place] + (2,) + self.held.shape[place:]
+        own = lax.broadcasted_iota(jnp.int32, shape, place) == bit_value(bit)
+        self.held = jnp.where(own, jnp.expand_dims(self.held, place), jnp.expand_dims(self.other, place))
+        self.have.append(bit)
+        self.other = None
+
+    def finish(self, *widths):
+        mine = bit_value(0)
+        outs = []
+        first = 0
+        for width in widths:
+            columns = slice(first, first + width)
+            held, other = self.held[..., columns], self.other[..., columns]
+            place = len(self.have)
+            shape = held.shape[:place] + (2,) + held.shape[place:]
+            own = lax.broadcasted_iota(jnp.int32, shape, place) == mine
+            joined = jnp.where(own, jnp.expand_dims(held, place), jnp.expand_dims(other, place))
+            outs.append(joined.reshape(-1, width))
+            first = first + width
+        return outs
+
+
+class Scattering:
+    def __init__(self, grad, order):
+        self.order = (0,) + tuple(order)
+        self.left = sorted(self.order, reverse=True)
+        self.width = grad.shape[1]
+        self.parts = [grad.astype(BF).reshape((2,) * len(self.order) + (-1, self.width))]
+        self.done = 0
+
+    def split(self):
+        bit = self.order[self.done]
+        axis = self.left.index(bit)
+        mine = bit_value(bit)
+        self.keep = sum(pick(item, axis, mine).astype(F32) for item in self.parts).astype(BF)
+        self.left.remove(bit)
+        return sum(pick(item, axis, 1 - mine).astype(F32) for item in self.parts).astype(BF)
+
+    def send(self, away):
+        self.parts = [self.keep, swap(away, self.order[self.done])]
+        self.done = self.done + 1
+
+    def total(self):
+        return sum(item.astype(F32) for item in self.parts).reshape(-1, self.width)
+
+
+def scatter_step(streams, *values):
+    live = [item for item in streams if item.done < len(item.order)]
+    away = [item.split() for item in live]
+    tied = list(tie(*away, *values))
+    for item, value in zip(live, tied):
+        item.send(value)
+    return tied[len(live) :]
+
+
+def chip_groups():
+    return [[i for i in range(lax.axis_size("fsdp")) if i % 2 == c] for c in range(2)]
+
+
+def chip_sum(grad):
+    return lax.psum_scatter(grad, "fsdp", scatter_dimension=0, axis_index_groups=chip_groups(), tiled=True)
+
+
+def advance(streams, *values):
+    for item in streams:
+        item.join()
+    live = [item for item in streams if len(item.have) < len(item.order)]
+    held = tie(*[item.held for item in live], *values)
+    for item, value in zip(live, held):
+        item.held = value
+        item.send()
+    return held[len(live) :]
 
 
 def body(
@@ -251,44 +501,56 @@
     vectors = (
         ln1_gain, ln1_bias, b_out, ln2_gain, ln2_bias, b_down, ln3_gain, ln3_bias, b_learn, b_qv, b_up,
     )
-    small = jnp.concatenate([columns(item, shard_rows) for item in vectors] + [w_map], axis=1)
-    small_count = small.shape[1]
+    lines = jnp.concatenate([item.reshape(-1, shard_rows).T for item in vectors], axis=1)
+    line_count = lines.shape[1]
+    small_count = line_count + w_map.shape[1]
     pad = (-small_count) % 128
-    first = gather(jnp.concatenate([w_qkv, jnp.pad(small, ((0, 0), (0, pad)))], axis=1))
-    w_qkv = first[:, : 3 * D]
-    spread = first[:, 3 * D : 3 * D + small_count]
-    lines = spread.reshape(devices, shard_rows, small_count).transpose(2, 0, 1)
+    order_x, order_y, order_z = rotations()
+    small = jnp.concatenate([lines, w_map, jnp.zeros((shard_rows, pad), BF)], axis=1)
+    wide = gather(jnp.concatenate([w_up, w_out, w_learn], axis=1))
+    w_down = gather(w_down)
+    streams = [
+        Gathering(w_qkv[:, D : 2 * D], order_y),
+        Gathering(w_qkv[:, 2 * D :], order_z),
+        Gathering(jnp.concatenate([w_qkv[:, :D], small], axis=1), order_x),
+    ]
+    for _ in range(len(streams[0].order)):
+        advance(streams)
+    (w_k,) = streams[0].finish(D)
+    (w_v,) = streams[1].finish(D)
+    w_q, spread = streams[2].finish(D, small.shape[1])
+    w_qkv = jnp.concatenate([w_q, w_k, w_v], axis=1)
+    spread = spread[:, :small_count]
+    w_out = wide[:, 4 * D : 5 * D]
+    w_learn = wide[:, 5 * D :]
+    lines = spread[:, :line_count].T.astype(F32)
     named = []
     offset = 0
     for item in vectors:
         count = item.shape[0] // shard_rows
-        part = lines[offset : offset + count].transpose(1, 0, 2).reshape(1, -1)
-        named.append(part.astype(F32))
+        part = lines[offset : offset + count]
+        if count > 1:
+            part = part.reshape(count, devices, shard_rows).transpose(1, 0, 2)
+        named.append(part.reshape(1, -1))
         offset = offset + count
     (ln1_gain, ln1_bias, b_out, ln2_gain, ln2_bias, b_down, ln3_gain, ln3_bias, b_learn, b_qv, b_up) = named
     w_map = spread[:, offset:]
-    w_out = gather(w_out)
-    w_up = gather(w_up)
-    w_down = gather(w_down)
-    w_learn = gather(w_learn)
-
     lengths = lengths.reshape(images)
     row_total = images * slots
     source = tokens.reshape(row_total, D).astype(F32)
     hidden = layer_norm(source, ln1_gain, ln1_bias).astype(BF)
     qkv_bias = jnp.concatenate([b_qv[:, :D], jnp.zeros((1, D), F32), b_qv[:, D:]], axis=1)
     qkv = (mm(hidden, w_qkv, NN) + qkv_bias).astype(BF)
-    attended, lse = attention_forward(qkv, lengths)
+    filled = ()
+    for image in range(images):
+        filled = attention_forward(image, qkv, lengths, filled)
+    attended, lse = filled
     middle = source + mm(attended, w_out, NN) + b_out
     normed = layer_norm(middle, ln2_gain, ln2_bias).astype(BF)
-    up_act, up_slope = gelu_pair(mm(normed, w_up, NN) + b_up)
-    up_act = up_act.astype(BF)
-    up_slope = up_slope.astype(BF)
+    up_act, up_slope = gelu_matmul(normed, [(wide, 0, 4 * D)], b_up)
     output = middle + mm(up_act, w_down, NN) + b_down
     learn_in = layer_norm(output, ln3_gain, ln3_bias).astype(BF)
-    learn_act, learn_slope = gelu_pair(mm(learn_in, w_learn, NN) + b_learn)
-    learn_act = learn_act.astype(BF)
-    learn_slope = learn_slope.astype(BF)
+    learn_act, learn_slope = gelu_matmul(learn_in, [(wide, 5 * D, D)], b_learn)
     logits = mm(learn_act, w_map, NN)
     slot_valid = lax.broadcasted_iota(jnp.int32, (images, slots, 1), 1) < lengths[:, None, None]
     pool_share = (slot_valid.astype(F32) / lengths[:, None, None].astype(F32)).reshape(row_total, 1)
@@ -305,38 +567,75 @@
     g_map = mm(learn_act, d_logits, TN)
     d_learn = (learn_slope.astype(F32) * mm(d_logits, w_map, NT)).astype(BF)
     g_blearn = jnp.sum(d_learn.astype(F32), axis=0)
-    g_wlearn = scatter_sum(mm(learn_in, d_learn, TN))
     d_norm3, g_ln3, h_ln3 = norm_back(output, ln3_gain, mm(d_learn, w_learn, NT))
     d_output = d_output + d_norm3
     d_mlp = d_output.astype(BF)
     g_bdown = jnp.sum(d_mlp.astype(F32), axis=0)
-    g_wdown = scatter_sum(mm(up_act, d_mlp, TN))
-    d_up = (up_slope.astype(F32) * mm(d_mlp, w_down, NT)).astype(BF)
-    g_bup = jnp.sum(d_up.astype(F32), axis=0)
-    g_wup = scatter_sum(mm(normed, d_up, TN))
-    d_norm2, g_ln2, h_ln2 = norm_back(middle, ln2_gain, mm(d_up, w_up, NT))
+    mine = bit_value(0)
+
+    def core_parts(grad):
+        blocks = grad.astype(BF).reshape(devices // 2, 2, -1, grad.shape[1])
+        return pick(blocks, 1, mine), pick(blocks, 1, 1 - mine)
+
+    def add(left, right):
+        return (left.astype(F32) + right.astype(F32)).astype(BF)
+
+    keep, away = core_parts(mm(up_act, d_mlp, TN))
+    keep, away, d_learn = tie(keep, away, d_learn)
+    other = swap(away, 0)
+    g_wlearn = mm(learn_in, d_learn, TN).astype(BF)
+    other, keep, g_wlearn, d_mlp = tie(other, keep, g_wlearn, d_mlp)
+    g_down = add(keep, other)
+    g_down, d_mlp = tie(g_down, d_mlp)
+    g_wdown = chip_sum(g_down.reshape(-1, D)).astype(F32)
+    d_up, g_bup = slope_matmul(d_mlp, w_down, up_slope)
+    up_keep, up_away = core_parts(mm(normed, d_up, TN))
+    up_keep, up_away, d_up = tie(up_keep, up_away, d_up)
+    up_other = swap(up_away, 0)
+    d_normed = back_product([d_up], wide)
+    d_norm2, g_ln2, h_ln2 = norm_back(middle, ln2_gain, d_normed)
     d_middle = d_output + d_norm2
     d_branch = d_middle.astype(BF)
+    up_other, d_branch = tie(up_other, d_branch)
+    g_up = add(up_keep, up_other)
+    g_up, d_branch = tie(g_up, d_branch)
+    g_wup = chip_sum(g_up.reshape(-1, g_up.shape[-1])).astype(F32)
     g_bout = jnp.sum(d_branch.astype(F32), axis=0)
-    g_wout = scatter_sum(mm(attended, d_branch, TN))
+    out_stream = Scattering(jnp.concatenate([mm(attended, d_branch, TN).astype(BF), g_wlearn], axis=1), order_y)
     d_attended = mm(d_branch, w_out, NT).astype(BF)
-    d_queries, d_keys, d_values = attention_backward(qkv, attended, d_attended, lse, lengths)
-    d_qkv = jnp.concatenate([d_queries, d_keys, d_values], axis=1)
-    g_bqv = jnp.concatenate(
-        [jnp.sum(d_queries.astype(F32), axis=0), jnp.sum(d_values.astype(F32), axis=0)]
+    (d_attended,) = scatter_step([out_stream], d_attended)
+    filled = ()
+    for image in range(images):
+        filled = attention_backward(image, qkv, attended, d_attended, lse, lengths, filled)
+        filled = scatter_step([out_stream], *filled)
+    late = []
+    parts = list(filled)
+    for n, order in enumerate((order_x, order_y, order_z)):
+        stream = Scattering(mm(hidden, parts[n], TN), order)
+        parts = scatter_step([stream], *parts)
+        late.append(stream)
+    d_hidden = back_product(parts, w_qkv)
+    g_bqv = jnp.concatenate([jnp.sum(item.astype(F32), axis=0) for item in (parts[0], parts[2])])
+    (d_hidden,) = scatter_step(late, d_hidden)
+    d_norm1, g_ln1, h_ln1 = norm_back(source, ln1_gain, d_hidden)
+    grads = (g_ln1, h_ln1, g_bout, g_ln2, h_ln2, g_bdown, g_ln3, h_ln3, g_blearn, g_bqv, g_bup)
+    lines = jnp.concatenate(
+        [item.reshape(devices, -1, shard_rows).transpose(1, 0, 2).reshape(-1, D) for item in grads], axis=0
     )
-    g_wqkv = mm(hidden, d_qkv, TN)
-    d_norm1, g_ln1, h_ln1 = norm_back(source, ln1_gain, mm(d_qkv, w_qkv, NT))
+    spread = jnp.concatenate([lines.T, g_map, jnp.zeros((D, pad), F32)], axis=1)
+    (spread,) = scatter_step(late, spread)
+    small = Scattering(spread, order_z)
     d_image = (d_middle + d_norm1).reshape(tokens.shape)
-
-    grads = (g_ln1, h_ln1, g_bout, g_ln2, h_ln2, g_bdown, g_ln3, h_ln3, g_blearn, g_bqv, g_bup)
-    spread = jnp.concatenate(
-        [item.reshape(devices, -1, shard_rows).transpose(0, 2, 1).reshape(D, -1) for item in grads]
-        + [g_map, jnp.zeros((D, pad), F32)],
-        axis=1,
-    )
-    last = scatter_sum(jnp.concatenate([g_wqkv, spread], axis=1))
-    small = last[:, 3 * D :]
+    (d_image,) = scatter_step([small], d_image)
+    for _ in range(len(small.order)):
+        (d_image,) = scatter_step(late + [small], d_image)
+    for _ in range(len(small.order)):
+        (d_image,) = scatter_step([out_stream], d_image)
+    g_wqkv = jnp.concatenate([item.total() for item in late], axis=1)
+    small = small.total()
+    joint = out_stream.total()
+    g_wout = joint[:, :D]
+    g_wlearn = joint[:, D:]
     outs = []
     offset = 0
     for item in vectors:
@@ -347,7 +646,7 @@
     g_map = small[:, offset:small_count]
     pooled = pooled.reshape(cotangent.shape)
     return (
-        pooled, d_image, g_ln1, h_ln1, last[:, : 3 * D], g_bqv, g_wout, g_bout, g_ln2, h_ln2,
+        pooled, d_image, g_ln1, h_ln1, g_wqkv, g_bqv, g_wout, g_bout, g_ln2, h_ln2,
         g_wup, g_bup, g_wdown, g_bdown, g_ln3, h_ln3, g_wlearn, g_blearn, g_map,
     )
 

time: 1120 us -> 610 us (0.54)
  waiting for transfers between devices: 702 us -> 137 us
  matrix products: 252 us -> 109 us
  Pallas kernels: 49.8 us -> 147 us
  starting transfers between devices: 0.4 us -> 54.8 us
  other arithmetic: 38.8 us -> 82.9 us
    reduce_scatter x5 -> x2, waiting for transfers between devices: 487 us -> 0.02 us  [chip_sum(): lax.psum_scatter(grad, 'fsdp', scatter_dimension=0, axis_index_groups=chi...]
    all_gather x5 -> x2, waiting for transfers between devices: 212 us -> 14.9 us  [gather(): return lax.all_gather(shard, 'fsdp', axis=0, tiled=True)]
    dot_general x18 -> x15, matrix products: 239 us -> 95.6 us  [mm(): return lax.dot_general(left, right, dims, preferred_element_type=F32)]
    ppermute x0 -> x42, waiting for transfers between devices: none -> 121 us  [swap(): lax.ppermute(value, 'fsdp', [(i, i ^ 1 << bit) for i in range(count)])]
    pallas_call x2 -> x9, Pallas kernels: 49.8 us -> 147 us  [the longest x2 43.1 us: gelu_matmul(): pl.pallas_call(functools.partial(gelu_matmul_kernel, rows // 4, tiles), o...]
    ppermute x0 -> x42, starting transfers between devices: none -> 54.6 us  [swap(): lax.ppermute(value, 'fsdp', [(i, i ^ 1 << bit) for i in range(count)])]
    convert_element_type x8 -> x30, other arithmetic: 7.56 us -> 46.4 us  [the longest x14 18.8 us: split(): sum((pick(item, axis, mine).astype(F32) for item in self.parts)).astype(BF)]
    concatenate x4 -> x5, local copies, waits for them, and re-layouts: 14.9 us -> 0.46 us  [the longest x2 0.16 us: body(): jnp.concatenate([jnp.sum(item.astype(F32), axis=0) for item in (parts[0],...]
  transfers between devices with their start and end apart: 10 -> 46, of which waited for: 9 -> 19; matrix products, arithmetic and copies ran while one was open for 27% -> 26% of each run, Pallas kernels for 5% -> 20%
where the time goes in v2:
time: 610 us; the launch traced here: 605 us
  Pallas kernels  147 us (24%)
  waiting for transfers between devices  137 us (22%)
  matrix products  109 us (18%)
  other arithmetic  82.9 us (14%)
  local copies, waits for them, and re-layouts  59.3 us (10%)
  starting transfers between devices  54.8 us (9%)
  between operations  15.5 us (3%)
    ppermute x42, waiting for transfers between devices, swap(): lax.ppermute(value, 'fsdp', [(i, i ^ 1 << bit) for i in range(count)])  121 us
    dot_general x15, matrix products, mm(): return lax.dot_general(left, right, dims, preferred_element_type=F32)  95.6 us
    ppermute x42, starting transfers between devices, swap(): lax.ppermute(value, 'fsdp', [(i, i ^ 1 << bit) for i in range(count)])  54.6 us
    pallas_call x2, Pallas kernels, gelu_matmul(): pl.pallas_call(functools.partial(gelu_matmul_kernel, rows // 4, tiles), o...  43.1 us
    pallas_call x2, Pallas kernels, attention_backward(): pl.pallas_call(held_in_place(kernel, len(filled)), out_shape=tuple((jax.S...  33.6 us
    pallas_call x2, Pallas kernels, back_product(): pl.pallas_call(functools.partial(back_product_kernel, count), out_shape=j...  31.2 us
    pallas_call x2, Pallas kernels, attention_forward(): pl.pallas_call(held_in_place(kernel, len(filled)), out_shape=(jax.ShapeDt...  21.8 us
    convert_element_type x14, other arithmetic, split(): sum((pick(item, axis, mine).astype(F32) for item in self.parts)).astype(BF)  18.8 us
  transfers between devices with their start and end apart: 46, of which 19 were waited for; matrix products, arithmetic and copies ran while one was open for 26% of the time, Pallas kernels for 20%

profile of v2, /device:TPU:0, one launch (start us, length us, event | category | flops | bytes accessed | tf_op | source)
XLA Modules:
  0.0 605.3 jit_solution(14848407013630567050)
XLA Ops:
  28.7 6.8 %collective-permute-done.2 = bf16[32,1152]{1,0:T(8,128)(2,1)S(1)} collective-permute-done((bf16[32,1152]{1,0:T(8,128)(2,1)S(1)}, bf16[32,1152]{1,0:T(8,128)(2,1)S(1)}, u32[]{:S(2)}, u32[]{:S(2)}) %collective-permute-start.2) | collective-permute-done | bytes 73760 | tf_op jit(solution)/shard_map/ppermute | solution.py:357
  38.6 5.4 collective-permute-done.3
  48.4 18.7 %collective-permute-done.6 = bf16[2,2,32,1024]{3,2,1,0:T(8,128)(2,1)S(1)} collective-permute-done((bf16[2,2,32,1024]{3,2,1,0:T(8,128)(2,1)S(1)}, bf16[2,2,32,1024]{3,2,1,0:T(8,128)(2,1)S(1)}, u32[]{:S(2)}, u32[]{:S(2)}) %collective-permute-start.6) | collective-permute-done | bytes 262176 | tf_op jit(solution)/shard_map/ppermute | solution.py:357
  73.6 5.9 collective-permute-done.9
  79.6 6.6 %collective-permute-done.10 = bf16[2,2,2,32,1024]{4,3,2,1,0:T(8,128)(2,1)S(1)} collective-permute-done((bf16[2,2,2,32,1024]{4,3,2,1,0:T(8,128)(2,1)S(1)}, bf16[2,2,2,32,1024]{4,3,2,1,0:T(8,128)(2,1)S(1)}, u32[]{:S(2)}, u32[]{:S(2)}) %collective-permute-start.10) | collective-permute-done | bytes 524320 | tf_op jit(solution)/shard_map/ppermute | solution.py:357
  115.8 9.9 %add_convert_fusion.refs_0_.refs_1_.refs_2_.refs_3_.refs_4_.refs_5_ = bf16[1152,3072]{1,0:T(8,128)(2,1)} fusion(bf16[1152,1024]{1,0:T(8,128)(2,1)S(1)} %fusion.8, f32[3072]{0:T(1024)S(1)} %bitcast.429, bf16[1024,1024]{1,0:T(8,128)(2,1)S(1)} %get-tuple-element.350, bf16[1024,1024]{1,0:T(8,128)(2,1)S(1)} %get-tuple-element.349, ...), kind=kOutput, calls=%fused_computation | convolution fusion | flops 7273709568 | bytes 15740928 | tf_op jit(solution)/shard_map/dot_general | solution.py:28
  125.7 13.4 %attention_forward.2 = (bf16[1152,1024]{1,0:T(8,128)(2,1)}, f32[8,4,576]{2,1,0:T(4,128)}) custom-call(s32[2]{0:T(128)} %bitcast.424, bf16[1152,3072]{1,0:T(8,128)(2,1)} %add_convert_fusion.refs_0_.refs_1_.refs_2_.refs_3_.refs_4_.refs_5_, bf16[1152,3072]{1,0:T(8,128)(2,1)} %add_convert_fusion.refs_0_.refs_1_.refs_2_.refs_3_.refs_4_.refs_5_, ...), custom_call_target="tpu_custom_call" | custom-call | flops 1024 | bytes 1024 | tf_op jit(solution)/shard_map/attention_forward/pallas_call | solution.py:300
  139.1 8.4 %attention_forward.3 = (bf16[1152,1024]{1,0:T(8,128)(2,1)}, f32[8,4,576]{2,1,0:T(4,128)}) custom-call(s32[2]{0:T(128)} %bitcast.425, bf16[1152,1024]{1,0:T(8,128)(2,1)} %get-tuple-element.131.refs_0_, f32[8,4,576]{2,1,0:T(4,128)} %get-tuple-element.132.refs_1_, ...), custom_call_target="tpu_custom_call", output_to_operand_aliasing={{0}: (1, {}), {1}: (2, {})} | custom-call | flops 1024 | bytes 1024 | tf_op jit(solution)/shard_map/attention_forward/pallas_call | solution.py:300
  148.4 5.3 fusion.92
  158.2 32.3 %gelu_matmul.2 = (bf16[1152,4096]{1,0:T(8,128)(2,1)}, bf16[1152,4096]{1,0:T(8,128)(2,1)}) custom-call(bf16[1152,1024]{1,0:T(8,128)(2,1)} %add_convert_fusion.4.x_ref, f32[1,4096]{1,0:T(1,128)} %reshape.565.b_ref, bf16[1024,6144]{1,0:T(8,128)(2,1)} %all-gather.3.cloned.1.call-done.refs_0_.refs_1_), custom_call_target="tpu_custom_call" | custom-call | flops 1024 | bytes 1024 | tf_op jit(solution)/shard_map/gelu_matmul/pallas_call | solution.py:125
  190.5 14.9 %all-gather.5.cloned.1.call-done.w_ref = bf16[4096,1024]{1,0:T(8,128)(2,1)} async-done(((bf16[128,1024]{1,0:T(8,128)(2,1)}), bf16[4096,1024]{1,0:T(8,128)(2,1)}) %all-gather.5.cloned.1.call-update) | async-done | bytes 8388624 | tf_op jit(solution)/shard_map/all_gather | solution.py:344
  205.4 15.8 %fusion.93 = (f32[1152]{0:T(1024)S(1)}, f32[1152,1024]{1,0:T(8,128)S(1)}) fusion(f32[1024]{0:T(1024)S(1)} %bitcast.432, f32[1152,1024]{1,0:T(8,128)} %copy-done.3, bf16[1152,4096]{1,0:T(8,128)(2,1)} %get-tuple-element.134, bf16[4096,1024]{1,0:T(8,128)(2,1)} %all-gather.5.cloned.1.call-done.w_ref), kind=kOutput, calls=%fused_computation.270 | convolution fusion | flops 9667214336 | bytes 27271680 | tf_op jit(solution)/shard_map/dot_general | solution.py:28
  221.9 4.1 fusion.65
  226.1 4.6 add_convert_fusion.3.x_ref
  230.7 10.8 %gelu_matmul.3 = (bf16[1152,1024]{1,0:T(8,128)(2,1)}, bf16[1152,1024]{1,0:T(8,128)(2,1)}) custom-call(bf16[1152,1024]{1,0:T(8,128)(2,1)} %add_convert_fusion.3.x_ref, f32[1,1024]{1,0:T(1,128)} %get-tuple-element.335.b_ref, bf16[1024,6144]{1,0:T(8,128)(2,1)} %all-gather.3.cloned.1.call-done.refs_0_.refs_1_), custom_call_target="tpu_custom_call" | custom-call | flops 1024 | bytes 1024 | tf_op jit(solution)/shard_map/gelu_matmul/pallas_call | solution.py:125
  244.2 3.9 fusion.67
  250.3 6.7 %multiply_reduce_fusion = (f32[1024]{0:T(1024)}, f32[1152]{0:T(1024)S(1)}, f32[1152]{0:T(1024)S(1)}, f32[1024]{0:T(1024)}, f32[1152,1024]{1,0:T(8,128)S(1)}) fusion(f32[1152,1024]{1,0:T(8,128)S(1)} %bitcast.379, f32[1152]{0:T(1024)S(1)} %add_rsqrt_fusion, f32[1152]{0:T(1024)S(1)} %broadcast_multiply_fusion.7, f32[1024]{0:T(1024)S(1)} %bitcast.412, ...), kind=kOutput, calls=%fused_computation.30 | convolution fusion | flops 2426531840 | bytes 13924352 | tf_op jit(solution)/shard_map/dot_general | solution.py:28
  257.1 3.8 convert_reduce_fusion.4
  260.9 13.5 %convolution_convert_fusion = bf16[4096,1024]{1,0:T(8,128)(2,1)} fusion(bf16[1152,4096]{1,0:T(8,128)(2,1)S(1)} %bitcast.446, bf16[1152,1024]{1,0:T(8,128)(2,1)S(1)} %get-tuple-element.143.x_ref), kind=kOutput, calls=%fused_computation.3 | convolution fusion | flops 9667870720 | bytes 20185088 | tf_op jit(solution)/shard_map/dot_general | solution.py:28
  274.5 4.9 dynamic-slice_bitcast_fusion.2
  279.7 4.2 convolution_convert_fusion.7
  286.6 4.2 add_convert_fusion.2
  290.8 17.2 %slope_matmul.1 = (bf16[1152,4096]{1,0:T(8,128)(2,1)}, f32[1,4096]{1,0:T(1,128)}) custom-call(bf16[1152,1024]{1,0:T(8,128)(2,1)} %copy-done.13, bf16[4096,1024]{1,0:T(8,128)(2,1)} %all-gather.5.cloned.1.call-done.w_ref, bf16[1152,4096]{1,0:T(8,128)(2,1)} %get-tuple-element.144.slope_ref), custom_call_target="tpu_custom_call" | custom-call | flops 1024 | bytes 1024 | tf_op jit(solution)/shard_map/slope_matmul/pallas_call | solution.py:166
  308.0 13.7 %convolution_convert_fusion.1 = bf16[1024,4096]{1,0:T(8,128)(2,1)S(1)} fusion(bf16[1152,1024]{1,0:T(8,128)(2,1)S(1)} %copy-done.17, bf16[1152,4096]{1,0:T(8,128)(2,1)} %get-tuple-element.148.refs_0_), kind=kOutput, calls=%fused_computation.4 | convolution fusion | flops 9667870720 | bytes 20185088 | tf_op jit(solution)/shard_map/dot_general | solution.py:28
  321.7 3.9 dynamic-slice_bitcast_fusion
  326.0 17.2 %back_product.2 = f32[1152,1024]{1,0:T(8,128)} custom-call(bf16[1152,4096]{1,0:T(8,128)(2,1)} %get-tuple-element.148.refs_0_, bf16[1024,6144]{1,0:T(8,128)(2,1)} %all-gather.3.cloned.1.call-done.refs_0_.refs_1_), custom_call_target="tpu_custom_call" | custom-call | flops 1024 | bytes 1024 | tf_op jit(solution)/shard_map/back_product/pallas_call | solution.py:150
  343.2 5.6 multiply_reduce_fusion.1
  348.9 6.3 %fusion.87 = (bf16[1152,1024]{1,0:T(8,128)(2,1)S(1)}, f32[1152,1024]{1,0:T(8,128)}) fusion(f32[1152,1024]{1,0:T(8,128)} %get-tuple-element.293, f32[1152]{0:T(1024)S(1)} %broadcast_multiply_fusion.3, f32[1152,1024]{1,0:T(8,128)} %copy-done.3, f32[1152]{0:T(1024)S(1)} %broadcast_multiply_fusion.8, f32[1152]{0:T(1024)S(1)} %broadcast_multiply_fusion.4, ...), kind=kLoop, calls=%fused_computation.264 | loop fusion | flops 10616832 | bytes 21256192 | tf_op jit(solution)/shard_map/convert_element_type | solution.py:598
  355.2 6.6 %add_convert_fusion.1 = bf16[16,32,4096]{2,1,0:T(8,128)(2,1)} fusion(bf16[16,32,4096]{2,1,0:T(8,128)(2,1)} %collective-permute-done.16, bf16[16,32,4096]{2,1,0:T(8,128)(2,1)S(1)} %copy-done.11), kind=kLoop, calls=%fused_computation.1 | loop fusion | flops 8388608 | bytes 12582912 | tf_op jit(solution)/shard_map/convert_element_type | solution.py:581
  367.2 5.8 convolution_convert_fusion.2.refs_4_.refs_7_
  373.2 23.1 %attention_backward.2 = (bf16[1152,1024]{1,0:T(8,128)(2,1)}, bf16[1152,1024]{1,0:T(8,128)(2,1)}, bf16[1152,1024]{1,0:T(8,128)(2,1)}) custom-call(s32[2]{0:T(128)} %bitcast.426, bf16[1152,3072]{1,0:T(8,128)(2,1)} %add_convert_fusion.refs_0_.refs_1_.refs_2_.refs_3_.refs_4_.refs_5_, ...), custom_call_target="tpu_custom_call" | custom-call | flops 1024 | bytes 1024 | tf_op jit(solution)/shard_map/attention_backward/pallas_call | solution.py:325
  396.3 4.2 fusion.22
  402.1 5.6 pad_maximum_fusion.refs_3_.refs_4_.refs_5_
  411.0 10.6 %attention_backward.3 = (bf16[1152,1024]{1,0:T(8,128)(2,1)}, bf16[1152,1024]{1,0:T(8,128)(2,1)}, bf16[1152,1024]{1,0:T(8,128)(2,1)}) custom-call(s32[2]{0:T(128)} %bitcast.427, bf16[1152,1024]{1,0:T(8,128)(2,1)} %get-tuple-element.160.refs_0_, ...), custom_call_target="tpu_custom_call", output_to_operand_aliasing={{0}: (1, {}), {1}: (2, {}), {2}: (3, {})} | custom-call | flops 1024 | bytes 1024 | tf_op jit(solution)/shard_map/attention_backward/pallas_call | solution.py:325
  421.6 5.9 collective-permute-done.18
  430.1 4.9 convolution_convert_fusion.5
  453.2 14.0 %back_product.3 = f32[1152,1024]{1,0:T(8,128)} custom-call(bf16[1152,1024]{1,0:T(8,128)(2,1)} %get-tuple-element.179.refs_0_, bf16[1152,1024]{1,0:T(8,128)(2,1)} %get-tuple-element.180.refs_1_, bf16[1152,1024]{1,0:T(8,128)(2,1)} %get-tuple-element.181.refs_2_, bf16[1024,3072]{1,0:T(8,128)(2,1)} %pad_maximum_fusion.refs_3_.refs_4_.refs_5_, ...), custom_call_target="tpu_custom_call" | custom-call | flops 1024 | bytes 1024 | tf_op jit(solution)/shard_map/back_product/pallas_call | solution.py:150
  475.3 9.8 %collective-permute-start.23 = (bf16[2,2,2,32,1024]{4,3,0,2,1:T(8,128)(2,1)S(1)}, bf16[2,2,2,32,1024]{4,3,0,2,1:T(8,128)(2,1)}, u32[]{:S(2)}, u32[]{:S(2)}) collective-permute-start(bf16[2,2,2,32,1024]{4,3,0,2,1:T(8,128)(2,1)S(1)} %get-tuple-element.182), channel_id=1, source_target_pairs={{0,2},{1,3},{2,0},{3,1},{4,6},{5,7},{6,4},{7,5},{8,10},{9,11},{10,... | collective-permute-start | bytes 1572872 | tf_op jit(solution)/shard_map/ppermute | solution.py:357
  489.0 3.3 fusion.13
  492.9 22.3 %collective-permute-done.23 = bf16[2,2,2,32,1024]{4,3,0,2,1:T(8,128)(2,1)} collective-permute-done((bf16[2,2,2,32,1024]{4,3,0,2,1:T(8,128)(2,1)S(1)}, bf16[2,2,2,32,1024]{4,3,0,2,1:T(8,128)(2,1)}, u32[]{:S(2)}, u32[]{:S(2)}) %collective-permute-start.23) | collective-permute-done | bytes 524320 | tf_op jit(solution)/shard_map/ppermute | solution.py:357
  521.0 4.3 collective-permute-start.27
  527.3 7.0 %collective-permute-done.29 = bf16[2,2,32,1024]{3,2,1,0:T(8,128)(2,1)S(1)} collective-permute-done((bf16[2,2,32,1024]{3,2,1,0:T(8,128)(2,1)S(1)}, bf16[2,2,32,1024]{3,2,1,0:T(8,128)(2,1)S(1)}, u32[]{:S(2)}, u32[]{:S(2)}) %collective-permute-start.29) | collective-permute-done | bytes 262176 | tf_op jit(solution)/shard_map/ppermute | solution.py:357
  534.5 15.1 %collective-permute-done.28 = bf16[2,2,32,1024]{3,2,1,0:T(8,128)(2,1)S(1)} collective-permute-done((bf16[2,2,32,1024]{3,2,1,0:T(8,128)(2,1)S(1)}, bf16[2,2,32,1024]{3,2,1,0:T(8,128)(2,1)S(1)}, u32[]{:S(2)}, u32[]{:S(2)}) %collective-permute-start.28) | collective-permute-done | bytes 262176 | tf_op jit(solution)/shard_map/ppermute | solution.py:357
  554.9 3.9 collective-permute-done.31
  561.3 3.4 collective-permute-done.34
  565.0 5.3 convolution_bitcast_fusion
  582.4 8.2 %collective-permute-done.36 = bf16[2,32,2048]{2,1,0:T(8,128)(2,1)S(1)} collective-permute-done((bf16[2,32,2048]{2,1,0:T(8,128)(2,1)S(1)}, bf16[2,32,2048]{2,1,0:T(8,128)(2,1)S(1)}, u32[]{:S(2)}, u32[]{:S(2)}) %collective-permute-start.36) | collective-permute-done | bytes 262176 | tf_op jit(solution)/shard_map/ppermute | solution.py:357
  591.8 3.9 collective-permute-done.41
  (369 shorter events, 154.4 us)
Async XLA Ops:
  7.2 214.7 %copy-start = (f32[2,1,8,1024]{3,2,1,0:T(8,128)S(1)}, f32[2,1,8,1024]{3,2,1,0:T(8,128)}, u32[]{:S(2)}) copy-start(f32[2,1,8,1024]{3,2,1,0:T(8,128)} %param.22) | copy-start | bytes 196612
  7.2 66.4 %copy-start.52 = (s32[2,1]{0,1:T(1,128)S(1)}, s32[2,1]{0,1:T(1,128)}, u32[]{:S(2)}) copy-start(s32[2,1]{0,1:T(1,128)} %param.21) | copy-start | bytes 28
  7.2 141.2 %all-gather.3.cloned.1.call-start = ((), (), s32[]{:S(2)}) async-start(), calls=%async_computation.2 | async-start | bytes 12976128 | tf_op jit(solution)/shard_map/all_gather | solution.py:344
  9.1 196.3 %all-gather.5.cloned.1.call-start = ((), (), s32[]{:S(2)}) async-start(), calls=%async_computation.3 | async-start | bytes 8650752 | tf_op jit(solution)/shard_map/all_gather | solution.py:344
  9.8 561.4 %reduce-scatter.5.cloned.1.call-start = ((), (), s32[]{:S(2)}) async-start(), calls=%async_computation.5 | async-start | bytes 4456448 | tf_op jit(solution)/shard_map/reduce_scatter | solution.py:461
  20.2 7.1 %collective-permute-start = (bf16[32,1024]{1,0:T(8,128)(2,1)S(1)}, bf16[32,1024]{1,0:T(8,128)(2,1)S(1)}, u32[]{:S(2)}, u32[]{:S(2)}) collective-permute-start(bf16[32,1024]{1,0:T(8,128)(2,1)S(1)} %get-tuple-element.116), channel_id=1, source_target_pairs={{0,2},{1,3},{2,0},{3,1},{4,6},{5,7},{6,4},{7,5},{8,10},{9,11},{10,... | collective-permute-start | bytes 196616 | tf_op jit(solution)/shard_map/ppermute | solution.py:357
  23.2 5.4 collective-permute-start.1
  24.7 10.8 %collective-permute-start.2 = (bf16[32,1152]{1,0:T(8,128)(2,1)S(1)}, bf16[32,1152]{1,0:T(8,128)(2,1)S(1)}, u32[]{:S(2)}, u32[]{:S(2)}) collective-permute-start(bf16[32,1152]{1,0:T(8,128)(2,1)S(1)} %concatenate.32), channel_id=1, source_target_pairs={{0,16},{1,17},{2,18},{3,19},{4,20},{5,21},{6,22},{7,23},{8,24},{9,... | collective-permute-start | bytes 221192 | tf_op jit(solution)/shard_map/ppermute | solution.py:357
  35.6 8.5 %collective-permute-start.3 = (bf16[2,32,1024]{2,1,0:T(8,128)(2,1)S(1)}, bf16[2,32,1024]{2,1,0:T(8,128)(2,1)S(1)}, u32[]{:S(2)}, u32[]{:S(2)}) collective-permute-start(bf16[2,32,1024]{2,1,0:T(8,128)(2,1)S(1)} %broadcast_select_fusion.12), channel_id=1, source_target_pairs={{0,16},{1,17},{2,18},{3,19},{4,20},{5,21},{6,22},{7,23},{8,24},{9,... | collective-permute-start | bytes 393224 | tf_op jit(solution)/shard_map/ppermute | solution.py:357
  35.7 8.5 %collective-permute-start.4 = (bf16[2,32,1024]{2,1,0:T(8,128)(2,1)S(1)}, bf16[2,32,1024]{2,1,0:T(8,128)(2,1)S(1)}, u32[]{:S(2)}, u32[]{:S(2)}) collective-permute-start(bf16[2,32,1024]{2,1,0:T(8,128)(2,1)S(1)} %broadcast_select_fusion.11), channel_id=1, source_target_pairs={{0,2},{1,3},{2,0},{3,1},{4,6},{5,7},{6,4},{7,5},{8,10},{9,11},{10,... | collective-permute-start | bytes 393224 | tf_op jit(solution)/shard_map/ppermute | solution.py:357
  36.0 8.6 %collective-permute-start.5 = (bf16[2,32,1152]{2,1,0:T(8,128)(2,1)S(1)}, bf16[2,32,1152]{2,1,0:T(8,128)(2,1)S(1)}, u32[]{:S(2)}, u32[]{:S(2)}) collective-permute-start(bf16[2,32,1152]{2,1,0:T(8,128)(2,1)S(1)} %broadcast_select_fusion.10), channel_id=1, source_target_pairs={{0,8},{1,9},{2,10},{3,11},{4,12},{5,13},{6,14},{7,15},{8,0},{9,1},... | collective-permute-start | bytes 442376 | tf_op jit(solution)/shard_map/ppermute | solution.py:357
  44.8 22.3 %collective-permute-start.6 = (bf16[2,2,32,1024]{3,2,1,0:T(8,128)(2,1)S(1)}, bf16[2,2,32,1024]{3,2,1,0:T(8,128)(2,1)S(1)}, u32[]{:S(2)}, u32[]{:S(2)}) collective-permute-start(bf16[2,2,32,1024]{3,2,1,0:T(8,128)(2,1)S(1)} %broadcast_select_fusion.8), channel_id=1, source_target_pairs={{0,8},{1,9},{2,10},{3,11},{4,12},{5,13},{6,14},{7,15},{8,0},{9,1},... | collective-permute-start | bytes 786440 | tf_op jit(solution)/shard_map/ppermute | solution.py:357
  45.2 24.8 %collective-permute-start.7 = (bf16[2,2,32,1024]{3,2,1,0:T(8,128)(2,1)S(1)}, bf16[2,2,32,1024]{3,2,1,0:T(8,128)(2,1)S(1)}, u32[]{:S(2)}, u32[]{:S(2)}) collective-permute-start(bf16[2,2,32,1024]{3,2,1,0:T(8,128)(2,1)S(1)} %broadcast_select_fusion.7), channel_id=1, source_target_pairs={{0,16},{1,17},{2,18},{3,19},{4,20},{5,21},{6,22},{7,23},{8,24},{9,... | collective-permute-start | bytes 786440 | tf_op jit(solution)/shard_map/ppermute | solution.py:357
  47.1 23.0 %collective-permute-start.8 = (bf16[2,2,32,1152]{3,2,1,0:T(8,128)(2,1)S(1)}, bf16[2,2,32,1152]{3,2,1,0:T(8,128)(2,1)S(1)}, u32[]{:S(2)}, u32[]{:S(2)}) collective-permute-start(bf16[2,2,32,1152]{3,2,1,0:T(8,128)(2,1)S(1)} %broadcast_select_fusion.6), channel_id=1, source_target_pairs={{0,4},{1,5},{2,6},{3,7},{4,0},{5,1},{6,2},{7,3},{8,12},{9,13},{10,... | collective-permute-start | bytes 884744 | tf_op jit(solution)/shard_map/ppermute | solution.py:357
  70.2 9.2 %collective-permute-start.9 = (bf16[2,2,2,32,1024]{4,3,2,1,0:T(8,128)(2,1)S(1)}, bf16[2,2,2,32,1024]{4,3,2,1,0:T(8,128)(2,1)S(1)}, u32[]{:S(2)}, u32[]{:S(2)}) collective-permute-start(bf16[2,2,2,32,1024]{4,3,2,1,0:T(8,128)(2,1)S(1)} %broadcast_select_fusion.5), channel_id=1, source_target_pairs={{0,4},{1,5},{2,6},{3,7},{4,0},{5,1},{6,2},{7,3},{8,12},{9,13},{10,... | collective-permute-start | bytes 1572872 | tf_op jit(solution)/shard_map/ppermute | solution.py:357
  71.1 15.1 %collective-permute-start.10 = (bf16[2,2,2,32,1024]{4,3,2,1,0:T(8,128)(2,1)S(1)}, bf16[2,2,2,32,1024]{4,3,2,1,0:T(8,128)(2,1)S(1)}, u32[]{:S(2)}, u32[]{:S(2)}) collective-permute-start(bf16[2,2,2,32,1024]{4,3,2,1,0:T(8,128)(2,1)S(1)} %broadcast_select_fusion.4), channel_id=1, source_target_pairs={{0,8},{1,9},{2,10},{3,11},{4,12},{5,13},{6,14},{7,15},{8,0},{9,1},... | collective-permute-start | bytes 1572872 | tf_op jit(solution)/shard_map/ppermute | solution.py:357
  71.1 16.2 %collective-permute-start.11 = (bf16[2,2,2,32,1152]{4,3,2,1,0:T(8,128)(2,1)S(1)}, bf16[2,2,2,32,1152]{4,3,2,1,0:T(8,128)(2,1)S(1)}, u32[]{:S(2)}, u32[]{:S(2)}) collective-permute-start(bf16[2,2,2,32,1152]{4,3,2,1,0:T(8,128)(2,1)S(1)} %broadcast_select_fusion.3), channel_id=1, source_target_pairs={{0,2},{1,3},{2,0},{3,1},{4,6},{5,7},{6,4},{7,5},{8,10},{9,11},{10,... | collective-permute-start | bytes 1769480 | tf_op jit(solution)/shard_map/ppermute | solution.py:357
  88.5 9.3 %collective-permute-start.12 = (bf16[2,2,2,2,32,1152]{5,4,3,2,1,0:T(8,128)(2,1)}, bf16[2,2,2,2,32,1152]{5,4,3,2,1,0:T(8,128)(2,1)}, u32[]{:S(2)}, u32[]{:S(2)}) collective-permute-start(bf16[2,2,2,2,32,1152]{5,4,3,2,1,0:T(8,128)(2,1)} %broadcast_select_fusion), channel_id=1, source_target_pairs={{0,1},{1,0},{2,3},{3,2},{4,5},{5,4},{6,7},{7,6},{8,9},{9,8},{10,11... | collective-permute-start | bytes 3538952 | tf_op jit(solution)/shard_map/ppermute | solution.py:357
  89.8 19.4 %collective-permute-start.13 = (bf16[2,2,2,2,32,1024]{5,4,3,2,1,0:T(8,128)(2,1)S(1)}, bf16[2,2,2,2,32,1024]{5,4,3,2,1,0:T(8,128)(2,1)}, u32[]{:S(2)}, u32[]{:S(2)}) collective-permute-start(bf16[2,2,2,2,32,1024]{5,4,3,2,1,0:T(8,128)(2,1)S(1)} %broadcast_select_fusion.2), channel_id=1, source_target_pairs={{0,1},{1,0},{2,3},{3,2},{4,5},{5,4},{6,7},{7,6},{8,9},{9,8},{10,11... | collective-permute-start | bytes 3145736 | tf_op jit(solution)/shard_map/ppermute | solution.py:357
  90.3 18.9 %collective-permute-start.14 = (bf16[2,2,2,2,32,1024]{5,4,3,2,1,0:T(8,128)(2,1)}, bf16[2,2,2,2,32,1024]{5,4,3,2,1,0:T(8,128)(2,1)}, u32[]{:S(2)}, u32[]{:S(2)}) collective-permute-start(bf16[2,2,2,2,32,1024]{5,4,3,2,1,0:T(8,128)(2,1)} %broadcast_select_fusion.1), channel_id=1, source_target_pairs={{0,1},{1,0},{2,3},{3,2},{4,5},{5,4},{6,7},{7,6},{8,9},{9,8},{10,11... | collective-permute-start | bytes 3145736 | tf_op jit(solution)/shard_map/ppermute | solution.py:357
  279.4 7.2 %collective-permute-start.15 = (bf16[16,128,1024]{2,1,0:T(8,128)(2,1)S(1)}, bf16[16,128,1024]{2,1,0:T(8,128)(2,1)S(1)}, u32[]{:S(2)}, u32[]{:S(2)}) collective-permute-start(bf16[16,128,1024]{2,1,0:T(8,128)(2,1)S(1)} %get-tuple-element.137), channel_id=1, source_target_pairs={{0,1},{1,0},{2,3},{3,2},{4,5},{5,4},{6,7},{7,6},{8,9},{9,8},{10,11... | collective-permute-start | bytes 12582920 | tf_op jit(solution)/shard_map/ppermute | solution.py:357
  325.6 29.5 %collective-permute-start.16 = (bf16[16,32,4096]{2,1,0:T(8,128)(2,1)}, bf16[16,32,4096]{2,1,0:T(8,128)(2,1)}, u32[]{:S(2)}, u32[]{:S(2)}) collective-permute-start(bf16[16,32,4096]{2,1,0:T(8,128)(2,1)} %get-tuple-element.147), channel_id=1, source_target_pairs={{0,1},{1,0},{2,3},{3,2},{4,5},{5,4},{6,7},{7,6},{8,9},{9,8},{10,11... | collective-permute-start | bytes 12582920 | tf_op jit(solution)/shard_map/ppermute | solution.py:357
  325.9 270.5 %reduce-scatter.3.cloned.1.call-start = ((), (), s32[]{:S(2)}) async-start(), calls=%async_computation.4 | async-start | bytes 4456448 | tf_op jit(solution)/shard_map/reduce_scatter | solution.py:461
  373.0 23.3 %collective-permute-start.17 = (bf16[2,2,2,2,32,2048]{5,4,3,1,0,2:T(8,128)(2,1)}, bf16[2,2,2,2,32,2048]{5,4,3,1,0,2:T(8,128)(2,1)}, u32[]{:S(2)}, u32[]{:S(2)}) collective-permute-start(bf16[2,2,2,2,32,2048]{5,4,3,1,0,2:T(8,128)(2,1)} %copy_bitcast_fusion), channel_id=1, source_target_pairs={{0,1},{1,0},{2,3},{3,2},{4,5},{5,4},{6,7},{7,6},{8,9},{9,8},{10,11... | collective-permute-start | bytes 6291464 | tf_op jit(solution)/shard_map/ppermute | solution.py:357
  400.5 27.0 %collective-permute-start.18 = (bf16[2,2,2,32,2048]{4,3,2,1,0:T(8,128)(2,1)}, bf16[2,2,2,32,2048]{4,3,2,1,0:T(8,128)(2,1)}, u32[]{:S(2)}, u32[]{:S(2)}) collective-permute-start(bf16[2,2,2,32,2048]{4,3,2,1,0:T(8,128)(2,1)} %get-tuple-element.159), channel_id=1, source_target_pairs={{0,4},{1,5},{2,6},{3,7},{4,0},{5,1},{6,2},{7,3},{8,12},{9,13},{10,... | collective-permute-start | bytes 3145736 | tf_op jit(solution)/shard_map/ppermute | solution.py:357
  437.4 32.5 %collective-permute-start.20 = (bf16[2,2,2,2,32,1024]{5,4,0,2,1,3:T(8,128)(2,1)}, bf16[2,2,2,2,32,1024]{5,4,0,2,1,3:T(8,128)(2,1)}, u32[]{:S(2)}, u32[]{:S(2)}) collective-permute-start(bf16[2,2,2,2,32,1024]{5,4,0,2,1,3:T(8,128)(2,1)} %copy_bitcast_fusion.3), channel_id=1, source_target_pairs={{0,1},{1,0},{2,3},{3,2},{4,5},{5,4},{6,7},{7,6},{8,9},{9,8},{10,11... | collective-permute-start | bytes 3145736 | tf_op jit(solution)/shard_map/ppermute | solution.py:357
  441.8 25.6 %collective-permute-start.21 = (bf16[2,2,2,2,32,1024]{5,4,3,1,0,2:T(8,128)(2,1)}, bf16[2,2,2,2,32,1024]{5,4,3,1,0,2:T(8,128)(2,1)}, u32[]{:S(2)}, u32[]{:S(2)}) collective-permute-start(bf16[2,2,2,2,32,1024]{5,4,3,1,0,2:T(8,128)(2,1)} %copy_bitcast_fusion.2), channel_id=1, source_target_pairs={{0,1},{1,0},{2,3},{3,2},{4,5},{5,4},{6,7},{7,6},{8,9},{9,8},{10,11... | collective-permute-start | bytes 3145736 | tf_op jit(solution)/shard_map/ppermute | solution.py:357
  447.8 24.9 %collective-permute-start.22 = (bf16[2,2,2,2,32,1024]{5,4,2,3,0,1:T(8,128)(2,1)}, bf16[2,2,2,2,32,1024]{5,4,2,3,0,1:T(8,128)(2,1)}, u32[]{:S(2)}, u32[]{:S(2)}) collective-permute-start(bf16[2,2,2,2,32,1024]{5,4,2,3,0,1:T(8,128)(2,1)} %copy_bitcast_fusion.1), channel_id=1, source_target_pairs={{0,1},{1,0},{2,3},{3,2},{4,5},{5,4},{6,7},{7,6},{8,9},{9,8},{10,11... | collective-permute-start | bytes 3145736 | tf_op jit(solution)/shard_map/ppermute | solution.py:357
  475.3 39.8 %collective-permute-start.23 = (bf16[2,2,2,32,1024]{4,3,0,2,1:T(8,128)(2,1)S(1)}, bf16[2,2,2,32,1024]{4,3,0,2,1:T(8,128)(2,1)}, u32[]{:S(2)}, u32[]{:S(2)}) collective-permute-start(bf16[2,2,2,32,1024]{4,3,0,2,1:T(8,128)(2,1)S(1)} %get-tuple-element.182), channel_id=1, source_target_pairs={{0,2},{1,3},{2,0},{3,1},{4,6},{5,7},{6,4},{7,5},{8,10},{9,11},{10,... | collective-permute-start | bytes 1572872 | tf_op jit(solution)/shard_map/ppermute | solution.py:357
  485.1 31.3 %collective-permute-start.24 = (bf16[2,2,2,32,1024]{4,3,2,1,0:T(8,128)(2,1)}, bf16[2,2,2,32,1024]{4,3,2,1,0:T(8,128)(2,1)}, u32[]{:S(2)}, u32[]{:S(2)}) collective-permute-start(bf16[2,2,2,32,1024]{4,3,2,1,0:T(8,128)(2,1)} %get-tuple-element.183), channel_id=1, source_target_pairs={{0,4},{1,5},{2,6},{3,7},{4,0},{5,1},{6,2},{7,3},{8,12},{9,13},{10,... | collective-permute-start | bytes 1572872 | tf_op jit(solution)/shard_map/ppermute | solution.py:357
  485.3 32.3 %collective-permute-start.25 = (bf16[2,2,2,32,1024]{4,3,1,2,0:T(8,128)(2,1)}, bf16[2,2,2,32,1024]{4,3,1,2,0:T(8,128)(2,1)}, u32[]{:S(2)}, u32[]{:S(2)}) collective-permute-start(bf16[2,2,2,32,1024]{4,3,1,2,0:T(8,128)(2,1)} %get-tuple-element.184), channel_id=1, source_target_pairs={{0,8},{1,9},{2,10},{3,11},{4,12},{5,13},{6,14},{7,15},{8,0},{9,1},... | collective-permute-start | bytes 1572872 | tf_op jit(solution)/shard_map/ppermute | solution.py:357
  518.9 15.4 %collective-permute-start.29 = (bf16[2,2,32,1024]{3,2,1,0:T(8,128)(2,1)S(1)}, bf16[2,2,32,1024]{3,2,1,0:T(8,128)(2,1)S(1)}, u32[]{:S(2)}, u32[]{:S(2)}) collective-permute-start(bf16[2,2,32,1024]{3,2,1,0:T(8,128)(2,1)S(1)} %copy.174), channel_id=1, source_target_pairs={{0,16},{1,17},{2,18},{3,19},{4,20},{5,21},{6,22},{7,23},{8,24},{9,... | collective-permute-start | bytes 786440 | tf_op jit(solution)/shard_map/ppermute | solution.py:357
  520.9 6.4 %collective-permute-start.26 = (bf16[2,2,2,2,32,128]{5,4,2,3,0,1:T(8,128)(2,1)S(1)}, bf16[2,2,2,2,32,128]{5,4,2,3,0,1:T(8,128)(2,1)S(1)}, u32[]{:S(2)}, u32[]{:S(2)}) collective-permute-start(bf16[2,2,2,2,32,128]{5,4,2,3,0,1:T(8,128)(2,1)S(1)} %copy_bitcast_fusion.8), channel_id=1, source_target_pairs={{0,1},{1,0},{2,3},{3,2},{4,5},{5,4},{6,7},{7,6},{8,9},{9,8},{10,11... | collective-permute-start | bytes 393224 | tf_op jit(solution)/shard_map/ppermute | solution.py:357
  521.0 13.4 %collective-permute-start.27 = (bf16[2,2,32,1024]{3,2,1,0:T(8,128)(2,1)S(1)}, bf16[2,2,32,1024]{3,2,1,0:T(8,128)(2,1)S(1)}, u32[]{:S(2)}, u32[]{:S(2)}) collective-permute-start(bf16[2,2,32,1024]{3,2,1,0:T(8,128)(2,1)S(1)} %copy.173), channel_id=1, source_target_pairs={{0,4},{1,5},{2,6},{3,7},{4,0},{5,1},{6,2},{7,3},{8,12},{9,13},{10,... | collective-permute-start | bytes 786440 | tf_op jit(solution)/shard_map/ppermute | solution.py:357
  525.3 45.8 %collective-permute-start.19 = (bf16[2,2,32,2048]{3,2,1,0:T(8,128)(2,1)S(1)}, bf16[2,2,32,2048]{3,2,1,0:T(8,128)(2,1)S(1)}, u32[]{:S(2)}, u32[]{:S(2)}) collective-permute-start(bf16[2,2,32,2048]{3,2,1,0:T(8,128)(2,1)S(1)} %copy-done.35), channel_id=1, source_target_pairs={{0,8},{1,9},{2,10},{3,11},{4,12},{5,13},{6,14},{7,15},{8,0},{9,1},... | collective-permute-start | bytes 1572872 | tf_op jit(solution)/shard_map/ppermute | solution.py:357
  526.9 22.7 %collective-permute-start.28 = (bf16[2,2,32,1024]{3,2,1,0:T(8,128)(2,1)S(1)}, bf16[2,2,32,1024]{3,2,1,0:T(8,128)(2,1)S(1)}, u32[]{:S(2)}, u32[]{:S(2)}) collective-permute-start(bf16[2,2,32,1024]{3,2,1,0:T(8,128)(2,1)S(1)} %get-tuple-element.190), channel_id=1, source_target_pairs={{0,8},{1,9},{2,10},{3,11},{4,12},{5,13},{6,14},{7,15},{8,0},{9,1},... | collective-permute-start | bytes 786440 | tf_op jit(solution)/shard_map/ppermute | solution.py:357
  549.7 5.2 collective-permute-start.30
  549.8 9.0 %collective-permute-start.31 = (bf16[2,32,1024]{2,1,0:T(8,128)(2,1)S(1)}, bf16[2,32,1024]{2,1,0:T(8,128)(2,1)S(1)}, u32[]{:S(2)}, u32[]{:S(2)}) collective-permute-start(bf16[2,32,1024]{2,1,0:T(8,128)(2,1)S(1)} %get-tuple-element.194), channel_id=1, source_target_pairs={{0,8},{1,9},{2,10},{3,11},{4,12},{5,13},{6,14},{7,15},{8,0},{9,1},... | collective-permute-start | bytes 393224 | tf_op jit(solution)/shard_map/ppermute | solution.py:357
  551.8 7.0 %collective-permute-start.32 = (bf16[2,32,1024]{2,1,0:T(8,128)(2,1)S(1)}, bf16[2,32,1024]{2,1,0:T(8,128)(2,1)S(1)}, u32[]{:S(2)}, u32[]{:S(2)}) collective-permute-start(bf16[2,32,1024]{2,1,0:T(8,128)(2,1)S(1)} %get-tuple-element.195), channel_id=1, source_target_pairs={{0,16},{1,17},{2,18},{3,19},{4,20},{5,21},{6,22},{7,23},{8,24},{9,... | collective-permute-start | bytes 393224 | tf_op jit(solution)/shard_map/ppermute | solution.py:357
  554.9 5.0 collective-permute-start.33
  559.8 4.9 collective-permute-start.34
  564.8 5.6 collective-permute-start.35
  570.3 8.8 %collective-permute-start.37 = (bf16[32,128]{1,0:T(8,128)(2,1)S(1)}, bf16[32,128]{1,0:T(8,128)(2,1)S(1)}, u32[]{:S(2)}, u32[]{:S(2)}) collective-permute-start(bf16[32,128]{1,0:T(8,128)(2,1)S(1)} %fusion.82), channel_id=1, source_target_pairs={{0,4},{1,5},{2,6},{3,7},{4,0},{5,1},{6,2},{7,3},{8,12},{9,13},{10,... | collective-permute-start | bytes 24584 | tf_op jit(solution)/shard_map/ppermute | solution.py:357
  573.0 9.2 %collective-permute-start.38 = (bf16[32,1024]{1,0:T(8,128)(2,1)S(1)}, bf16[32,1024]{1,0:T(8,128)(2,1)S(1)}, u32[]{:S(2)}, u32[]{:S(2)}) collective-permute-start(bf16[32,1024]{1,0:T(8,128)(2,1)S(1)} %fusion.59), channel_id=1, source_target_pairs={{0,16},{1,17},{2,18},{3,19},{4,20},{5,21},{6,22},{7,23},{8,24},{9,... | collective-permute-start | bytes 196616 | tf_op jit(solution)/shard_map/ppermute | solution.py:357
  574.4 7.9 %collective-permute-start.39 = (bf16[32,1024]{1,0:T(8,128)(2,1)S(1)}, bf16[32,1024]{1,0:T(8,128)(2,1)S(1)}, u32[]{:S(2)}, u32[]{:S(2)}) collective-permute-start(bf16[32,1024]{1,0:T(8,128)(2,1)S(1)} %fusion.60), channel_id=1, source_target_pairs={{0,2},{1,3},{2,0},{3,1},{4,6},{5,7},{6,4},{7,5},{8,10},{9,11},{10,... | collective-permute-start | bytes 196616 | tf_op jit(solution)/shard_map/ppermute | solution.py:357
  576.4 5.9 collective-permute-start.40
  577.5 13.1 %collective-permute-start.36 = (bf16[2,32,2048]{2,1,0:T(8,128)(2,1)S(1)}, bf16[2,32,2048]{2,1,0:T(8,128)(2,1)S(1)}, u32[]{:S(2)}, u32[]{:S(2)}) collective-permute-start(bf16[2,32,2048]{2,1,0:T(8,128)(2,1)S(1)} %get-tuple-element.203), channel_id=1, source_target_pairs={{0,16},{1,17},{2,18},{3,19},{4,20},{5,21},{6,22},{7,23},{8,24},{9,... | collective-permute-start | bytes 786440 | tf_op jit(solution)/shard_map/ppermute | solution.py:357
  590.6 5.0 collective-permute-start.41
  (61 other events, 677.7 us)
Sparse Core Ops, SparseCore 0:
  11.5 115.3 all-gather.2
  129.7 75.6 all-gather.4
  326.1 93.8 reduce-scatter.4
  422.1 106.2 reduce-scatter.2

commit v3 on v2

--- a/solution.py
+++ b/solution.py
@@ -140,22 +140,22 @@
     refs[-1][...] = total
 
 
-def back_product(pieces, w):
+def back_product(pieces, weights):
     count = len(pieces)
     rows, width = pieces[0].shape
-    height = w.shape[0]
+    height = weights[0].shape[0]
     tile = 512
     whole = pl.BlockSpec((rows, width), lambda j: (0, 0))
-    parts = [pl.BlockSpec((tile, width), lambda j, i=i: (j, i)) for i in range(count)]
+    part = pl.BlockSpec((tile, width), lambda j: (j, 0))
     return pl.pallas_call(
         functools.partial(back_product_kernel, count),
         out_shape=jax.ShapeDtypeStruct((rows, height), F32),
         grid=(height // tile,),
-        in_specs=[whole] * count + parts,
+        in_specs=[whole] * count + [part] * count,
         out_specs=pl.BlockSpec((rows, tile), lambda j: (0, j)),
         cost_estimate=light(),
         name="back_product",
-    )(*pieces, *[w] * count)
+    )(*pieces, *weights)
 
 
 def slope_matmul(x, w, slope):
@@ -592,45 +592,43 @@
     up_keep, up_away = core_parts(mm(normed, d_up, TN))
     up_keep, up_away, d_up = tie(up_keep, up_away, d_up)
     up_other = swap(up_away, 0)
-    d_normed = back_product([d_up], wide)
+    d_normed = back_product([d_up], [wide])
     d_norm2, g_ln2, h_ln2 = norm_back(middle, ln2_gain, d_normed)
     d_middle = d_output + d_norm2
     d_branch = d_middle.astype(BF)
-    up_other, d_branch = tie(up_other, d_branch)
-    g_up = add(up_keep, up_other)
-    g_up, d_branch = tie(g_up, d_branch)
-    g_wup = chip_sum(g_up.reshape(-1, g_up.shape[-1])).astype(F32)
     g_bout = jnp.sum(d_branch.astype(F32), axis=0)
     out_stream = Scattering(jnp.concatenate([mm(attended, d_branch, TN).astype(BF), g_wlearn], axis=1), order_y)
     d_attended = mm(d_branch, w_out, NT).astype(BF)
     (d_attended,) = scatter_step([out_stream], d_attended)
-    filled = ()
-    for image in range(images):
+    filled = attention_backward(0, qkv, attended, d_attended, lse, lengths, ())
+    up_other, up_keep, *filled = scatter_step([out_stream], up_other, up_keep, *filled)
+    g_up = add(up_keep, up_other)
+    g_up, *filled = tie(g_up, *filled)
+    g_wup = chip_sum(g_up.reshape(-1, g_up.shape[-1])).astype(F32)
+    for image in range(1, images):
         filled = attention_backward(image, qkv, attended, d_attended, lse, lengths, filled)
-        filled = scatter_step([out_stream], *filled)
+    filled = scatter_step([out_stream], *filled)
     late = []
     parts = list(filled)
     for n, order in enumerate((order_x, order_y, order_z)):
         stream = Scattering(mm(hidden, parts[n], TN), order)
         parts = scatter_step([stream], *parts)
         late.append(stream)
-    d_hidden = back_product(parts, w_qkv)
     g_bqv = jnp.concatenate([jnp.sum(item.astype(F32), axis=0) for item in (parts[0], parts[2])])
-    (d_hidden,) = scatter_step(late, d_hidden)
+    g_bqv, *parts = scatter_step(late, g_bqv, *parts)
+    d_hidden = back_product(parts, [w_q, w_k, w_v])
     d_norm1, g_ln1, h_ln1 = norm_back(source, ln1_gain, d_hidden)
     grads = (g_ln1, h_ln1, g_bout, g_ln2, h_ln2, g_bdown, g_ln3, h_ln3, g_blearn, g_bqv, g_bup)
     lines = jnp.concatenate(
         [item.reshape(devices, -1, shard_rows).transpose(1, 0, 2).reshape(-1, D) for item in grads], axis=0
     )
     spread = jnp.concatenate([lines.T, g_map, jnp.zeros((D, pad), F32)], axis=1)
-    (spread,) = scatter_step(late, spread)
     small = Scattering(spread, order_z)
+    (pooled,) = scatter_step([small], pooled)
     d_image = (d_middle + d_norm1).reshape(tokens.shape)
-    (d_image,) = scatter_step([small], d_image)
     for _ in range(len(small.order)):
-        (d_image,) = scatter_step(late + [small], d_image)
-    for _ in range(len(small.order)):
-        (d_image,) = scatter_step([out_stream], d_image)
+        (d_image,) = scatter_step(late + [out_stream], d_image)
+        scatter_step([small])
     g_wqkv = jnp.concatenate([item.total() for item in late], axis=1)
     small = small.total()
     joint = out_stream.total()

time: 610 us -> 581 us (0.952)
  waiting for transfers between devices: 137 us -> 121 us
  local copies, waits for them, and re-layouts: 59.3 us -> 49.2 us
    ppermute x42, waiting for transfers between devices: 121 us -> 111 us  [swap(): lax.ppermute(value, 'fsdp', [(i, i ^ 1 << bit) for i in range(count)])]
    convert_element_type x1 -> x0, other arithmetic: 6.25 us -> none  [body(): d_branch = d_middle.astype(BF)]
    convert_element_type x14 -> x15, other arithmetic: 18.8 us -> 14.4 us  [split(): sum((pick(item, axis, mine).astype(F32) for item in self.parts)).astype(BF)]
  transfers between devices with their start and end apart: 46 -> 46, of which waited for: 19 -> 24; matrix products, arithmetic and copies ran while one was open for 26% -> 28% of each run, Pallas kernels for 20% -> 24%
where the time goes in v3:
time: 581 us; the launch traced here: 577 us
  Pallas kernels  147 us (25%)
  waiting for transfers between devices  121 us (21%)
  matrix products  107 us (18%)
  other arithmetic  77.9 us (13%)
  starting transfers between devices  60.2 us (10%)
  local copies, waits for them, and re-layouts  49.2 us (8%)
  between operations  15.3 us (3%)
    ppermute x42, waiting for transfers between devices, swap(): lax.ppermute(value, 'fsdp', [(i, i ^ 1 << bit) for i in range(count)])  111 us
    dot_general x15, matrix products, mm(): return lax.dot_general(left, right, dims, preferred_element_type=F32)  93.5 us
    ppermute x42, starting transfers between devices, swap(): lax.ppermute(value, 'fsdp', [(i, i ^ 1 << bit) for i in range(count)])  60 us
    pallas_call x2, Pallas kernels, gelu_matmul(): pl.pallas_call(functools.partial(gelu_matmul_kernel, rows // 4, tiles), o...  43.2 us
    pallas_call x2, Pallas kernels, attention_backward(): pl.pallas_call(held_in_place(kernel, len(filled)), out_shape=tuple((jax.S...  34 us
    pallas_call x2, Pallas kernels, back_product(): pl.pallas_call(functools.partial(back_product_kernel, count), out_shape=j...  30.6 us
    pallas_call x2, Pallas kernels, attention_forward(): pl.pallas_call(held_in_place(kernel, len(filled)), out_shape=(jax.ShapeDt...  21.8 us
    pallas_call x1, Pallas kernels, slope_matmul(): pl.pallas_call(functools.partial(slope_matmul_kernel, rows // 4), out_sha...  17.3 us
  transfers between devices with their start and end apart: 46, of which 24 were waited for; matrix products, arithmetic and copies ran while one was open for 28% of the time, Pallas kernels for 24%

profile of v3, /device:TPU:0, one launch (start us, length us, event | category | flops | bytes accessed | tf_op | source)
XLA Modules:
  0.0 577.0 jit_solution(1805958800819445652)
XLA Ops:
  28.9 6.6 %collective-permute-done.2 = bf16[32,1152]{1,0:T(8,128)(2,1)S(1)} collective-permute-done((bf16[32,1152]{1,0:T(8,128)(2,1)S(1)}, bf16[32,1152]{1,0:T(8,128)(2,1)S(1)}, u32[]{:S(2)}, u32[]{:S(2)}) %collective-permute-start.2) | collective-permute-done | bytes 73760 | tf_op jit(solution)/shard_map/ppermute | solution.py:357
  38.8 5.2 collective-permute-done.3
  48.4 18.2 %collective-permute-done.6 = bf16[2,2,32,1024]{3,2,1,0:T(8,128)(2,1)S(1)} collective-permute-done((bf16[2,2,32,1024]{3,2,1,0:T(8,128)(2,1)S(1)}, bf16[2,2,32,1024]{3,2,1,0:T(8,128)(2,1)S(1)}, u32[]{:S(2)}, u32[]{:S(2)}) %collective-permute-start.6) | collective-permute-done | bytes 262176 | tf_op jit(solution)/shard_map/ppermute | solution.py:357
  66.8 3.9 collective-permute-done.7
  75.3 6.6 %collective-permute-done.9 = bf16[2,2,2,32,1024]{4,3,2,1,0:T(8,128)(2,1)} collective-permute-done((bf16[2,2,2,32,1024]{4,3,2,1,0:T(8,128)(2,1)S(1)}, bf16[2,2,2,32,1024]{4,3,2,1,0:T(8,128)(2,1)}, u32[]{:S(2)}, u32[]{:S(2)}) %collective-permute-start.9) | collective-permute-done | bytes 524320 | tf_op jit(solution)/shard_map/ppermute | solution.py:357
  83.2 5.2 collective-permute-done.10
  119.7 9.9 %add_convert_fusion.refs_0_.refs_1_.refs_2_.refs_3_.refs_4_.refs_5_ = bf16[1152,3072]{1,0:T(8,128)(2,1)} fusion(bf16[1152,1024]{1,0:T(8,128)(2,1)S(1)} %fusion.13, f32[3072]{0:T(1024)S(1)} %bitcast.414, bf16[1024,1024]{1,0:T(8,128)(2,1)S(1)} %get-tuple-element.405.refs_5_, bf16[1024,1024]{1,0:T(8,128)(2,1)S(1)} %get-tuple-element.404.refs_4_, ...), kind=kOutput, calls=%fused_computation | convolution fusion | flops 7273709568 | bytes 15740928 | tf_op jit(solution)/shard_map/dot_general | solution.py:28
  129.7 13.4 %attention_forward.2 = (bf16[1152,1024]{1,0:T(8,128)(2,1)}, f32[8,4,576]{2,1,0:T(4,128)}) custom-call(s32[2]{0:T(128)} %bitcast.409, bf16[1152,3072]{1,0:T(8,128)(2,1)} %add_convert_fusion.refs_0_.refs_1_.refs_2_.refs_3_.refs_4_.refs_5_, bf16[1152,3072]{1,0:T(8,128)(2,1)} %add_convert_fusion.refs_0_.refs_1_.refs_2_.refs_3_.refs_4_.refs_5_, ...), custom_call_target="tpu_custom_call" | custom-call | flops 1024 | bytes 1024 | tf_op jit(solution)/shard_map/attention_forward/pallas_call | solution.py:300
  143.1 8.4 %attention_forward.3 = (bf16[1152,1024]{1,0:T(8,128)(2,1)}, f32[8,4,576]{2,1,0:T(4,128)}) custom-call(s32[2]{0:T(128)} %bitcast.410, bf16[1152,1024]{1,0:T(8,128)(2,1)} %get-tuple-element.128.refs_0_, f32[8,4,576]{2,1,0:T(4,128)} %get-tuple-element.129.refs_1_, ...), custom_call_target="tpu_custom_call", output_to_operand_aliasing={{0}: (1, {}), {1}: (2, {})} | custom-call | flops 1024 | bytes 1024 | tf_op jit(solution)/shard_map/attention_forward/pallas_call | solution.py:300
  152.4 5.3 fusion.96
  162.1 32.3 %gelu_matmul.2 = (bf16[1152,4096]{1,0:T(8,128)(2,1)}, bf16[1152,4096]{1,0:T(8,128)(2,1)}) custom-call(bf16[1152,1024]{1,0:T(8,128)(2,1)} %add_convert_fusion.4.x_ref, f32[1,4096]{1,0:T(1,128)} %reshape.572.b_ref, bf16[1024,6144]{1,0:T(8,128)(2,1)} %all-gather.3.cloned.1.call-done.refs_0_.refs_1_), custom_call_target="tpu_custom_call" | custom-call | flops 1024 | bytes 1024 | tf_op jit(solution)/shard_map/gelu_matmul/pallas_call | solution.py:125
  194.5 9.1 %all-gather.5.cloned.1.call-done.w_ref = bf16[4096,1024]{1,0:T(8,128)(2,1)} async-done(((bf16[128,1024]{1,0:T(8,128)(2,1)}), bf16[4096,1024]{1,0:T(8,128)(2,1)}) %all-gather.5.cloned.1.call-update) | async-done | bytes 8388624 | tf_op jit(solution)/shard_map/all_gather | solution.py:344
  203.6 15.7 %fusion.97 = (f32[1152]{0:T(1024)S(1)}, f32[1152,1024]{1,0:T(8,128)S(1)}) fusion(f32[1024]{0:T(1024)S(1)} %bitcast.415, f32[1152,1024]{1,0:T(8,128)} %copy-done.3, bf16[1152,4096]{1,0:T(8,128)(2,1)} %get-tuple-element.131, bf16[4096,1024]{1,0:T(8,128)(2,1)} %all-gather.5.cloned.1.call-done.w_ref), kind=kOutput, calls=%fused_computation.258 | convolution fusion | flops 9667214336 | bytes 27271680 | tf_op jit(solution)/shard_map/dot_general | solution.py:28
  220.0 4.1 fusion.76
  224.2 4.6 add_convert_fusion.3.x_ref
  228.8 10.8 %gelu_matmul.3 = (bf16[1152,1024]{1,0:T(8,128)(2,1)}, bf16[1152,1024]{1,0:T(8,128)(2,1)}) custom-call(bf16[1152,1024]{1,0:T(8,128)(2,1)} %add_convert_fusion.3.x_ref, f32[1,1024]{1,0:T(1,128)} %get-tuple-element.390.b_ref, bf16[1024,6144]{1,0:T(8,128)(2,1)} %all-gather.3.cloned.1.call-done.refs_0_.refs_1_), custom_call_target="tpu_custom_call" | custom-call | flops 1024 | bytes 1024 | tf_op jit(solution)/shard_map/gelu_matmul/pallas_call | solution.py:125
  242.3 3.9 fusion.78
  247.9 6.1 %multiply_reduce_fusion = (bf16[1024]{0:T(1024)(128)(2,1)S(1)}, f32[1152]{0:T(1024)S(1)}, f32[1152]{0:T(1024)S(1)}, bf16[1024]{0:T(1024)(128)(2,1)S(1)}, f32[1152,1024]{1,0:T(8,128)S(1)}) fusion(f32[1152,1024]{1,0:T(8,128)S(1)} %bitcast.374, f32[1152]{0:T(1024)S(1)} %add_rsqrt_fusion, f32[1152]{0:T(1024)S(1)} %broadcast_multiply_fusion.7, ...), kind=kOutput, calls=%fused_computation.31 | convolution fusion | flops 2426531840 | bytes 13920256 | tf_op jit(solution)/shard_map/dot_general | solution.py:28
  254.0 3.3 fusion.91
  257.3 13.7 %convolution_convert_fusion = bf16[4096,1024]{1,0:T(8,128)(2,1)} fusion(bf16[1152,4096]{1,0:T(8,128)(2,1)S(1)} %bitcast.429, bf16[1152,1024]{1,0:T(8,128)(2,1)S(1)} %get-tuple-element.140.x_ref), kind=kOutput, calls=%fused_computation.3 | convolution fusion | flops 9667870720 | bytes 20185088 | tf_op jit(solution)/shard_map/dot_general | solution.py:28
  271.0 4.9 dynamic-slice_bitcast_fusion.2
  276.3 4.2 convolution_convert_fusion.7
  283.2 4.2 add_convert_fusion.2
  287.4 17.3 %slope_matmul.1 = (bf16[1152,4096]{1,0:T(8,128)(2,1)}, f32[1,4096]{1,0:T(1,128)}) custom-call(bf16[1152,1024]{1,0:T(8,128)(2,1)} %copy-done.16, bf16[4096,1024]{1,0:T(8,128)(2,1)} %all-gather.5.cloned.1.call-done.w_ref, bf16[1152,4096]{1,0:T(8,128)(2,1)} %get-tuple-element.141.slope_ref), custom_call_target="tpu_custom_call" | custom-call | flops 1024 | bytes 1024 | tf_op jit(solution)/shard_map/slope_matmul/pallas_call | solution.py:166
  304.7 13.7 %convolution_convert_fusion.1 = bf16[1024,4096]{1,0:T(8,128)(2,1)S(1)} fusion(bf16[1152,1024]{1,0:T(8,128)(2,1)S(1)} %copy-done.17, bf16[1152,4096]{1,0:T(8,128)(2,1)} %get-tuple-element.143.refs_0_), kind=kOutput, calls=%fused_computation.4 | convolution fusion | flops 9667870720 | bytes 20185088 | tf_op jit(solution)/shard_map/dot_general | solution.py:28
  318.4 3.9 dynamic-slice_bitcast_fusion
  322.6 16.9 %back_product.2 = f32[1152,1024]{1,0:T(8,128)} custom-call(bf16[1152,4096]{1,0:T(8,128)(2,1)} %get-tuple-element.143.refs_0_, bf16[1024,6144]{1,0:T(8,128)(2,1)} %all-gather.3.cloned.1.call-done.refs_0_.refs_1_), custom_call_target="tpu_custom_call" | custom-call | flops 1024 | bytes 1024 | tf_op jit(solution)/shard_map/back_product/pallas_call | solution.py:150
  339.5 5.6 multiply_reduce_fusion.1
  345.1 4.8 convert_reduce_fusion.4
  355.5 5.8 %convolution_convert_fusion.2.refs_4_.refs_7_ = bf16[1152,1024]{1,0:T(8,128)(2,1)} fusion(bf16[1024,6144]{1,0:T(8,128)(2,1)} %all-gather.3.cloned.1.call-done.refs_0_.refs_1_, f32[1152,1024]{1,0:T(8,128)S(1)} %get-tuple-element.337), kind=kOutput, calls=%fused_computation.54 | convolution fusion | flops 2418278400 | bytes 9175040 | tf_op jit(solution)/shard_map/dot_general | solution.py:28
  362.3 5.3 fusion.80
  367.6 23.3 %attention_backward.2 = (bf16[1152,1024]{1,0:T(8,128)(2,1)}, bf16[1152,1024]{1,0:T(8,128)(2,1)}, bf16[1152,1024]{1,0:T(8,128)(2,1)}) custom-call(s32[2]{0:T(128)} %bitcast.411, bf16[1152,3072]{1,0:T(8,128)(2,1)} %add_convert_fusion.refs_0_.refs_1_.refs_2_.refs_3_.refs_4_.refs_5_, ...), custom_call_target="tpu_custom_call" | custom-call | flops 1024 | bytes 1024 | tf_op jit(solution)/shard_map/attention_backward/pallas_call | solution.py:325
  391.2 4.2 fusion.27
  396.9 5.7 add_convert_fusion.1
  402.6 10.7 %attention_backward.3 = (bf16[1152,1024]{1,0:T(8,128)(2,1)}, bf16[1152,1024]{1,0:T(8,128)(2,1)}, bf16[1152,1024]{1,0:T(8,128)(2,1)}) custom-call(s32[2]{0:T(128)} %bitcast.412, bf16[1152,1024]{1,0:T(8,128)(2,1)} %get-tuple-element.159.refs_0_, ...), custom_call_target="tpu_custom_call", output_to_operand_aliasing={{0}: (1, {}), {1}: (2, {}), {2}: (3, {})} | custom-call | flops 1024 | bytes 1024 | tf_op jit(solution)/shard_map/attention_backward/pallas_call | solution.py:325
  415.9 5.0 convolution_convert_fusion.5
  424.9 3.3 convolution_convert_fusion.3
  428.8 24.3 %collective-permute-start.25 = (bf16[2,2,32,2048]{3,2,1,0:T(8,128)(2,1)}, bf16[2,2,32,2048]{3,2,1,0:T(8,128)(2,1)}, u32[]{:S(2)}, u32[]{:S(2)}) collective-permute-start(bf16[2,2,32,2048]{3,2,1,0:T(8,128)(2,1)} %get-tuple-element.189), channel_id=1, source_target_pairs={{0,8},{1,9},{2,10},{3,11},{4,12},{5,13},{6,14},{7,15},{8,0},{9,1},... | collective-permute-start | bytes 1572872 | tf_op jit(solution)/shard_map/ppermute | solution.py:357
  458.0 13.8 %back_product.3 = f32[1152,1024]{1,0:T(8,128)} custom-call(bf16[1152,1024]{1,0:T(8,128)(2,1)} %get-tuple-element.180.refs_0_, bf16[1152,1024]{1,0:T(8,128)(2,1)} %get-tuple-element.181.refs_1_, bf16[1152,1024]{1,0:T(8,128)(2,1)} %get-tuple-element.182.refs_2_, bf16[1024,1024]{1,0:T(8,128)(2,1)} %copy-done.19, bf16[1024,1024]{1,0:T(8,128)(2,1)} %copy-done.20, ...), custom_call_target="tpu_custom_call" | custom-call | flops 1024 | bytes 1024 | tf_op jit(solution)/shard_map/back_product/pallas_call | solution.py:150
  471.9 4.2 fusion.15
  484.8 8.6 %collective-permute-done.34 = bf16[2,2,2,32,128]{3,4,1,2,0:T(8,128)(2,1)S(1)} collective-permute-done((bf16[2,2,2,32,128]{3,4,1,2,0:T(8,128)(2,1)S(1)}, bf16[2,2,2,32,128]{3,4,1,2,0:T(8,128)(2,1)S(1)}, u32[]{:S(2)}, u32[]{:S(2)}) %collective-permute-start.34) | collective-permute-done | bytes 65568 | tf_op jit(solution)/shard_map/ppermute | solution.py:357
  493.5 15.9 %collective-permute-done.35 = bf16[2,2,32,128]{2,3,1,0:T(8,128)(2,1)S(1)} collective-permute-done((bf16[2,2,32,128]{2,3,1,0:T(8,128)(2,1)S(1)}, bf16[2,2,32,128]{2,3,1,0:T(8,128)(2,1)S(1)}, u32[]{:S(2)}, u32[]{:S(2)}) %collective-permute-start.35) | collective-permute-done | bytes 32800 | tf_op jit(solution)/shard_map/ppermute | solution.py:357
  509.6 4.2 collective-permute-done.36
  514.0 4.8 fusion.18
  522.1 3.4 collective-permute-start.28
  526.1 8.5 %collective-permute-done.27 = bf16[2,2,32,1024]{3,2,1,0:T(8,128)(2,1)S(1)} collective-permute-done((bf16[2,2,32,1024]{3,2,1,0:T(8,128)(2,1)S(1)}, bf16[2,2,32,1024]{3,2,1,0:T(8,128)(2,1)S(1)}, u32[]{:S(2)}, u32[]{:S(2)}) %collective-permute-start.27) | collective-permute-done | bytes 262176 | tf_op jit(solution)/shard_map/ppermute | solution.py:357
  534.7 9.1 %collective-permute-done.28 = bf16[2,2,32,1024]{3,2,1,0:T(8,128)(2,1)S(1)} collective-permute-done((bf16[2,2,32,1024]{3,2,1,0:T(8,128)(2,1)S(1)}, bf16[2,2,32,1024]{3,2,1,0:T(8,128)(2,1)S(1)}, u32[]{:S(2)}, u32[]{:S(2)}) %collective-permute-start.28) | collective-permute-done | bytes 262176 | tf_op jit(solution)/shard_map/ppermute | solution.py:357
  547.5 3.4 collective-permute-start.31
  (346 shorter events, 136.3 us)
Async XLA Ops:
  7.2 212.8 %copy-start = (f32[2,1,8,1024]{3,2,1,0:T(8,128)S(1)}, f32[2,1,8,1024]{3,2,1,0:T(8,128)}, u32[]{:S(2)}) copy-start(f32[2,1,8,1024]{3,2,1,0:T(8,128)} %param.22) | copy-start | bytes 196612
  7.2 66.0 %copy-start.4 = (bf16[2,1,576,1024]{3,2,1,0:T(8,128)(2,1)S(1)}, bf16[2,1,576,1024]{3,2,1,0:T(8,128)(2,1)}, u32[]{:S(2)}) copy-start(bf16[2,1,576,1024]{3,2,1,0:T(8,128)(2,1)} %param.20) | copy-start | bytes 7077892
  7.2 145.1 %all-gather.3.cloned.1.call-start = ((), (), s32[]{:S(2)}) async-start(), calls=%async_computation.2 | async-start | bytes 12976128 | tf_op jit(solution)/shard_map/all_gather | solution.py:344
  9.2 194.4 %all-gather.5.cloned.1.call-start = ((), (), s32[]{:S(2)}) async-start(), calls=%async_computation.3 | async-start | bytes 8650752 | tf_op jit(solution)/shard_map/all_gather | solution.py:344
  10.0 556.7 %reduce-scatter.5.cloned.1.call-start = ((), (), s32[]{:S(2)}) async-start(), calls=%async_computation.5 | async-start | bytes 4456448 | tf_op jit(solution)/shard_map/reduce_scatter | solution.py:461
  20.3 7.1 %collective-permute-start = (bf16[32,1024]{1,0:T(8,128)(2,1)S(1)}, bf16[32,1024]{1,0:T(8,128)(2,1)S(1)}, u32[]{:S(2)}, u32[]{:S(2)}) collective-permute-start(bf16[32,1024]{1,0:T(8,128)(2,1)S(1)} %get-tuple-element.113), channel_id=1, source_target_pairs={{0,2},{1,3},{2,0},{3,1},{4,6},{5,7},{6,4},{7,5},{8,10},{9,11},{10,... | collective-permute-start | bytes 196616 | tf_op jit(solution)/shard_map/ppermute | solution.py:357
  23.3 5.5 collective-permute-start.1
  24.8 10.7 %collective-permute-start.2 = (bf16[32,1152]{1,0:T(8,128)(2,1)S(1)}, bf16[32,1152]{1,0:T(8,128)(2,1)S(1)}, u32[]{:S(2)}, u32[]{:S(2)}) collective-permute-start(bf16[32,1152]{1,0:T(8,128)(2,1)S(1)} %concatenate.34), channel_id=1, source_target_pairs={{0,16},{1,17},{2,18},{3,19},{4,20},{5,21},{6,22},{7,23},{8,24},{9,... | collective-permute-start | bytes 221192 | tf_op jit(solution)/shard_map/ppermute | solution.py:357
  35.6 8.5 %collective-permute-start.3 = (bf16[2,32,1024]{2,1,0:T(8,128)(2,1)S(1)}, bf16[2,32,1024]{2,1,0:T(8,128)(2,1)S(1)}, u32[]{:S(2)}, u32[]{:S(2)}) collective-permute-start(bf16[2,32,1024]{2,1,0:T(8,128)(2,1)S(1)} %broadcast_select_fusion.12), channel_id=1, source_target_pairs={{0,16},{1,17},{2,18},{3,19},{4,20},{5,21},{6,22},{7,23},{8,24},{9,... | collective-permute-start | bytes 393224 | tf_op jit(solution)/shard_map/ppermute | solution.py:357
  35.7 8.5 %collective-permute-start.4 = (bf16[2,32,1024]{2,1,0:T(8,128)(2,1)S(1)}, bf16[2,32,1024]{2,1,0:T(8,128)(2,1)S(1)}, u32[]{:S(2)}, u32[]{:S(2)}) collective-permute-start(bf16[2,32,1024]{2,1,0:T(8,128)(2,1)S(1)} %broadcast_select_fusion.11), channel_id=1, source_target_pairs={{0,2},{1,3},{2,0},{3,1},{4,6},{5,7},{6,4},{7,5},{8,10},{9,11},{10,... | collective-permute-start | bytes 393224 | tf_op jit(solution)/shard_map/ppermute | solution.py:357
  36.6 8.0 %collective-permute-start.5 = (bf16[2,32,1152]{2,1,0:T(8,128)(2,1)S(1)}, bf16[2,32,1152]{2,1,0:T(8,128)(2,1)S(1)}, u32[]{:S(2)}, u32[]{:S(2)}) collective-permute-start(bf16[2,32,1152]{2,1,0:T(8,128)(2,1)S(1)} %broadcast_select_fusion.10), channel_id=1, source_target_pairs={{0,8},{1,9},{2,10},{3,11},{4,12},{5,13},{6,14},{7,15},{8,0},{9,1},... | collective-permute-start | bytes 442376 | tf_op jit(solution)/shard_map/ppermute | solution.py:357
  44.7 21.9 %collective-permute-start.6 = (bf16[2,2,32,1024]{3,2,1,0:T(8,128)(2,1)S(1)}, bf16[2,2,32,1024]{3,2,1,0:T(8,128)(2,1)S(1)}, u32[]{:S(2)}, u32[]{:S(2)}) collective-permute-start(bf16[2,2,32,1024]{3,2,1,0:T(8,128)(2,1)S(1)} %broadcast_select_fusion.8), channel_id=1, source_target_pairs={{0,8},{1,9},{2,10},{3,11},{4,12},{5,13},{6,14},{7,15},{8,0},{9,1},... | collective-permute-start | bytes 786440 | tf_op jit(solution)/shard_map/ppermute | solution.py:357
  45.2 25.5 %collective-permute-start.7 = (bf16[2,2,32,1024]{3,2,1,0:T(8,128)(2,1)S(1)}, bf16[2,2,32,1024]{3,2,1,0:T(8,128)(2,1)S(1)}, u32[]{:S(2)}, u32[]{:S(2)}) collective-permute-start(bf16[2,2,32,1024]{3,2,1,0:T(8,128)(2,1)S(1)} %broadcast_select_fusion.7), channel_id=1, source_target_pairs={{0,16},{1,17},{2,18},{3,19},{4,20},{5,21},{6,22},{7,23},{8,24},{9,... | collective-permute-start | bytes 786440 | tf_op jit(solution)/shard_map/ppermute | solution.py:357
  47.2 24.4 %collective-permute-start.8 = (bf16[2,2,32,1152]{3,2,1,0:T(8,128)(2,1)S(1)}, bf16[2,2,32,1152]{3,2,1,0:T(8,128)(2,1)S(1)}, u32[]{:S(2)}, u32[]{:S(2)}) collective-permute-start(bf16[2,2,32,1152]{3,2,1,0:T(8,128)(2,1)S(1)} %broadcast_select_fusion.6), channel_id=1, source_target_pairs={{0,4},{1,5},{2,6},{3,7},{4,0},{5,1},{6,2},{7,3},{8,12},{9,13},{10,... | collective-permute-start | bytes 884744 | tf_op jit(solution)/shard_map/ppermute | solution.py:357
  72.6 9.3 %collective-permute-start.9 = (bf16[2,2,2,32,1024]{4,3,2,1,0:T(8,128)(2,1)S(1)}, bf16[2,2,2,32,1024]{4,3,2,1,0:T(8,128)(2,1)}, u32[]{:S(2)}, u32[]{:S(2)}) collective-permute-start(bf16[2,2,2,32,1024]{4,3,2,1,0:T(8,128)(2,1)S(1)} %broadcast_select_fusion.5), channel_id=1, source_target_pairs={{0,4},{1,5},{2,6},{3,7},{4,0},{5,1},{6,2},{7,3},{8,12},{9,13},{10,... | collective-permute-start | bytes 1572872 | tf_op jit(solution)/shard_map/ppermute | solution.py:357
  73.2 15.3 %collective-permute-start.10 = (bf16[2,2,2,32,1024]{4,3,2,1,0:T(8,128)(2,1)}, bf16[2,2,2,32,1024]{4,3,2,1,0:T(8,128)(2,1)}, u32[]{:S(2)}, u32[]{:S(2)}) collective-permute-start(bf16[2,2,2,32,1024]{4,3,2,1,0:T(8,128)(2,1)} %broadcast_select_fusion.4), channel_id=1, source_target_pairs={{0,8},{1,9},{2,10},{3,11},{4,12},{5,13},{6,14},{7,15},{8,0},{9,1},... | collective-permute-start | bytes 1572872 | tf_op jit(solution)/shard_map/ppermute | solution.py:357
  73.6 17.2 %collective-permute-start.11 = (bf16[2,2,2,32,1152]{4,3,2,1,0:T(8,128)(2,1)}, bf16[2,2,2,32,1152]{4,3,2,1,0:T(8,128)(2,1)}, u32[]{:S(2)}, u32[]{:S(2)}) collective-permute-start(bf16[2,2,2,32,1152]{4,3,2,1,0:T(8,128)(2,1)} %broadcast_select_fusion.3), channel_id=1, source_target_pairs={{0,2},{1,3},{2,0},{3,1},{4,6},{5,7},{6,4},{7,5},{8,10},{9,11},{10,... | collective-permute-start | bytes 1769480 | tf_op jit(solution)/shard_map/ppermute | solution.py:357
  93.2 8.8 %collective-permute-start.12 = (bf16[2,2,2,2,32,1152]{5,4,3,2,1,0:T(8,128)(2,1)}, bf16[2,2,2,2,32,1152]{5,4,3,2,1,0:T(8,128)(2,1)}, u32[]{:S(2)}, u32[]{:S(2)}) collective-permute-start(bf16[2,2,2,2,32,1152]{5,4,3,2,1,0:T(8,128)(2,1)} %broadcast_select_fusion), channel_id=1, source_target_pairs={{0,1},{1,0},{2,3},{3,2},{4,5},{5,4},{6,7},{7,6},{8,9},{9,8},{10,11... | collective-permute-start | bytes 3538952 | tf_op jit(solution)/shard_map/ppermute | solution.py:357
  94.1 19.4 %collective-permute-start.13 = (bf16[2,2,2,2,32,1024]{5,4,3,2,1,0:T(8,128)(2,1)S(1)}, bf16[2,2,2,2,32,1024]{5,4,3,2,1,0:T(8,128)(2,1)}, u32[]{:S(2)}, u32[]{:S(2)}) collective-permute-start(bf16[2,2,2,2,32,1024]{5,4,3,2,1,0:T(8,128)(2,1)S(1)} %broadcast_select_fusion.2), channel_id=1, source_target_pairs={{0,1},{1,0},{2,3},{3,2},{4,5},{5,4},{6,7},{7,6},{8,9},{9,8},{10,11... | collective-permute-start | bytes 3145736 | tf_op jit(solution)/shard_map/ppermute | solution.py:357
  94.7 18.8 %collective-permute-start.14 = (bf16[2,2,2,2,32,1024]{5,4,3,2,1,0:T(8,128)(2,1)}, bf16[2,2,2,2,32,1024]{5,4,3,2,1,0:T(8,128)(2,1)}, u32[]{:S(2)}, u32[]{:S(2)}) collective-permute-start(bf16[2,2,2,2,32,1024]{5,4,3,2,1,0:T(8,128)(2,1)} %broadcast_select_fusion.1), channel_id=1, source_target_pairs={{0,1},{1,0},{2,3},{3,2},{4,5},{5,4},{6,7},{7,6},{8,9},{9,8},{10,11... | collective-permute-start | bytes 3145736 | tf_op jit(solution)/shard_map/ppermute | solution.py:357
  276.0 7.2 %collective-permute-start.15 = (bf16[16,128,1024]{2,1,0:T(8,128)(2,1)S(1)}, bf16[16,128,1024]{2,1,0:T(8,128)(2,1)S(1)}, u32[]{:S(2)}, u32[]{:S(2)}) collective-permute-start(bf16[16,128,1024]{2,1,0:T(8,128)(2,1)S(1)} %get-tuple-element.134), channel_id=1, source_target_pairs={{0,1},{1,0},{2,3},{3,2},{4,5},{5,4},{6,7},{7,6},{8,9},{9,8},{10,11... | collective-permute-start | bytes 12582920 | tf_op jit(solution)/shard_map/ppermute | solution.py:357
  287.4 281.1 %reduce-scatter.3.cloned.1.call-start = ((), (), s32[]{:S(2)}) async-start(), calls=%async_computation.4 | async-start | bytes 4456448 | tf_op jit(solution)/shard_map/reduce_scatter | solution.py:461
  322.4 73.0 %collective-permute-start.17 = (bf16[16,32,4096]{2,1,0:T(8,128)(2,1)}, bf16[16,32,4096]{2,1,0:T(8,128)(2,1)}, u32[]{:S(2)}, u32[]{:S(2)}) collective-permute-start(bf16[16,32,4096]{2,1,0:T(8,128)(2,1)} %get-tuple-element.146), channel_id=1, source_target_pairs={{0,1},{1,0},{2,3},{3,2},{4,5},{5,4},{6,7},{7,6},{8,9},{9,8},{10,11... | collective-permute-start | bytes 12582920 | tf_op jit(solution)/shard_map/ppermute | solution.py:357
  361.3 29.9 %collective-permute-start.16 = (bf16[2,2,2,2,32,2048]{5,4,3,1,0,2:T(8,128)(2,1)}, bf16[2,2,2,2,32,2048]{5,4,3,1,0,2:T(8,128)(2,1)}, u32[]{:S(2)}, u32[]{:S(2)}) collective-permute-start(bf16[2,2,2,2,32,2048]{5,4,3,1,0,2:T(8,128)(2,1)} %copy_bitcast_fusion), channel_id=1, source_target_pairs={{0,1},{1,0},{2,3},{3,2},{4,5},{5,4},{6,7},{7,6},{8,9},{9,8},{10,11... | collective-permute-start | bytes 6291464 | tf_op jit(solution)/shard_map/ppermute | solution.py:357
  395.4 17.9 %collective-permute-start.18 = (bf16[2,2,2,32,2048]{4,3,2,1,0:T(8,128)(2,1)}, bf16[2,2,2,32,2048]{4,3,2,1,0:T(8,128)(2,1)}, u32[]{:S(2)}, u32[]{:S(2)}) collective-permute-start(bf16[2,2,2,32,2048]{4,3,2,1,0:T(8,128)(2,1)} %get-tuple-element.153), channel_id=1, source_target_pairs={{0,4},{1,5},{2,6},{3,7},{4,0},{5,1},{6,2},{7,3},{8,12},{9,13},{10,... | collective-permute-start | bytes 3145736 | tf_op jit(solution)/shard_map/ppermute | solution.py:357
  421.0 34.2 %collective-permute-start.19 = (bf16[2,2,2,2,32,1024]{5,4,0,2,1,3:T(8,128)(2,1)S(1)}, bf16[2,2,2,2,32,1024]{5,4,0,2,1,3:T(8,128)(2,1)S(1)}, u32[]{:S(2)}, u32[]{:S(2)}) collective-permute-start(bf16[2,2,2,2,32,1024]{5,4,0,2,1,3:T(8,128)(2,1)S(1)} %copy_bitcast_fusion.3), channel_id=1, source_target_pairs={{0,1},{1,0},{2,3},{3,2},{4,5},{5,4},{6,7},{7,6},{8,9},{9,8},{10,11... | collective-permute-start | bytes 3145736 | tf_op jit(solution)/shard_map/ppermute | solution.py:357
  424.4 29.4 %collective-permute-start.20 = (bf16[2,2,2,2,32,1024]{5,4,3,1,0,2:T(8,128)(2,1)S(1)}, bf16[2,2,2,2,32,1024]{5,4,3,1,0,2:T(8,128)(2,1)S(1)}, u32[]{:S(2)}, u32[]{:S(2)}) collective-permute-start(bf16[2,2,2,2,32,1024]{5,4,3,1,0,2:T(8,128)(2,1)S(1)} %copy_bitcast_fusion.2), channel_id=1, source_target_pairs={{0,1},{1,0},{2,3},{3,2},{4,5},{5,4},{6,7},{7,6},{8,9},{9,8},{10,11... | collective-permute-start | bytes 3145736 | tf_op jit(solution)/shard_map/ppermute | solution.py:357
  428.3 28.3 %collective-permute-start.21 = (bf16[2,2,2,2,32,1024]{5,4,2,3,0,1:T(8,128)(2,1)S(1)}, bf16[2,2,2,2,32,1024]{5,4,2,3,0,1:T(8,128)(2,1)S(1)}, u32[]{:S(2)}, u32[]{:S(2)}) collective-permute-start(bf16[2,2,2,2,32,1024]{5,4,2,3,0,1:T(8,128)(2,1)S(1)} %copy_bitcast_fusion.1), channel_id=1, source_target_pairs={{0,1},{1,0},{2,3},{3,2},{4,5},{5,4},{6,7},{7,6},{8,9},{9,8},{10,11... | collective-permute-start | bytes 3145736 | tf_op jit(solution)/shard_map/ppermute | solution.py:357
  428.8 53.4 %collective-permute-start.25 = (bf16[2,2,32,2048]{3,2,1,0:T(8,128)(2,1)}, bf16[2,2,32,2048]{3,2,1,0:T(8,128)(2,1)}, u32[]{:S(2)}, u32[]{:S(2)}) collective-permute-start(bf16[2,2,32,2048]{3,2,1,0:T(8,128)(2,1)} %get-tuple-element.189), channel_id=1, source_target_pairs={{0,8},{1,9},{2,10},{3,11},{4,12},{5,13},{6,14},{7,15},{8,0},{9,1},... | collective-permute-start | bytes 1572872 | tf_op jit(solution)/shard_map/ppermute | solution.py:357
  477.7 2.3 collective-permute-start.33
  481.1 12.2 %collective-permute-start.34 = (bf16[2,2,2,32,128]{3,4,1,2,0:T(8,128)(2,1)S(1)}, bf16[2,2,2,32,128]{3,4,1,2,0:T(8,128)(2,1)S(1)}, u32[]{:S(2)}, u32[]{:S(2)}) collective-permute-start(bf16[2,2,2,32,128]{3,4,1,2,0:T(8,128)(2,1)S(1)} %get-tuple-element.353), channel_id=1, source_target_pairs={{0,8},{1,9},{2,10},{3,11},{4,12},{5,13},{6,14},{7,15},{8,0},{9,1},... | collective-permute-start | bytes 196616 | tf_op jit(solution)/shard_map/ppermute | solution.py:357
  483.5 35.3 %collective-permute-start.22 = (bf16[2,2,2,32,1024]{4,3,0,2,1:T(8,128)(2,1)}, bf16[2,2,2,32,1024]{4,3,0,2,1:T(8,128)(2,1)S(1)}, u32[]{:S(2)}, u32[]{:S(2)}) collective-permute-start(bf16[2,2,2,32,1024]{4,3,0,2,1:T(8,128)(2,1)} %get-tuple-element.186), channel_id=1, source_target_pairs={{0,2},{1,3},{2,0},{3,1},{4,6},{5,7},{6,4},{7,5},{8,10},{9,11},{10,... | collective-permute-start | bytes 1572872 | tf_op jit(solution)/shard_map/ppermute | solution.py:357
  483.6 35.5 %collective-permute-start.23 = (bf16[2,2,2,32,1024]{4,3,2,1,0:T(8,128)(2,1)}, bf16[2,2,2,32,1024]{4,3,2,1,0:T(8,128)(2,1)S(1)}, u32[]{:S(2)}, u32[]{:S(2)}) collective-permute-start(bf16[2,2,2,32,1024]{4,3,2,1,0:T(8,128)(2,1)} %get-tuple-element.187), channel_id=1, source_target_pairs={{0,4},{1,5},{2,6},{3,7},{4,0},{5,1},{6,2},{7,3},{8,12},{9,13},{10,... | collective-permute-start | bytes 1572872 | tf_op jit(solution)/shard_map/ppermute | solution.py:357
  483.7 35.6 %collective-permute-start.24 = (bf16[2,2,2,32,1024]{4,3,1,2,0:T(8,128)(2,1)}, bf16[2,2,2,32,1024]{4,3,1,2,0:T(8,128)(2,1)S(1)}, u32[]{:S(2)}, u32[]{:S(2)}) collective-permute-start(bf16[2,2,2,32,1024]{4,3,1,2,0:T(8,128)(2,1)} %get-tuple-element.188), channel_id=1, source_target_pairs={{0,8},{1,9},{2,10},{3,11},{4,12},{5,13},{6,14},{7,15},{8,0},{9,1},... | collective-permute-start | bytes 1572872 | tf_op jit(solution)/shard_map/ppermute | solution.py:357
  493.5 16.0 %collective-permute-start.35 = (bf16[2,2,32,128]{2,3,1,0:T(8,128)(2,1)S(1)}, bf16[2,2,32,128]{2,3,1,0:T(8,128)(2,1)S(1)}, u32[]{:S(2)}, u32[]{:S(2)}) collective-permute-start(bf16[2,2,32,128]{2,3,1,0:T(8,128)(2,1)S(1)} %copy.313), channel_id=1, source_target_pairs={{0,16},{1,17},{2,18},{3,19},{4,20},{5,21},{6,22},{7,23},{8,24},{9,... | collective-permute-start | bytes 98312 | tf_op jit(solution)/shard_map/ppermute | solution.py:357
  509.5 4.3 collective-permute-start.36
  513.9 4.9 collective-permute-start.37
  519.5 6.5 %collective-permute-start.26 = (bf16[2,2,32,1024]{3,2,1,0:T(8,128)(2,1)S(1)}, bf16[2,2,32,1024]{3,2,1,0:T(8,128)(2,1)S(1)}, u32[]{:S(2)}, u32[]{:S(2)}) collective-permute-start(bf16[2,2,32,1024]{3,2,1,0:T(8,128)(2,1)S(1)} %copy.309), channel_id=1, source_target_pairs={{0,4},{1,5},{2,6},{3,7},{4,0},{5,1},{6,2},{7,3},{8,12},{9,13},{10,... | collective-permute-start | bytes 786440 | tf_op jit(solution)/shard_map/ppermute | solution.py:357
  522.0 12.5 %collective-permute-start.27 = (bf16[2,2,32,1024]{3,2,1,0:T(8,128)(2,1)S(1)}, bf16[2,2,32,1024]{3,2,1,0:T(8,128)(2,1)S(1)}, u32[]{:S(2)}, u32[]{:S(2)}) collective-permute-start(bf16[2,2,32,1024]{3,2,1,0:T(8,128)(2,1)S(1)} %get-tuple-element.191), channel_id=1, source_target_pairs={{0,8},{1,9},{2,10},{3,11},{4,12},{5,13},{6,14},{7,15},{8,0},{9,1},... | collective-permute-start | bytes 786440 | tf_op jit(solution)/shard_map/ppermute | solution.py:357
  522.1 21.7 %collective-permute-start.28 = (bf16[2,2,32,1024]{3,2,1,0:T(8,128)(2,1)S(1)}, bf16[2,2,32,1024]{3,2,1,0:T(8,128)(2,1)S(1)}, u32[]{:S(2)}, u32[]{:S(2)}) collective-permute-start(bf16[2,2,32,1024]{3,2,1,0:T(8,128)(2,1)S(1)} %copy.311), channel_id=1, source_target_pairs={{0,16},{1,17},{2,18},{3,19},{4,20},{5,21},{6,22},{7,23},{8,24},{9,... | collective-permute-start | bytes 786440 | tf_op jit(solution)/shard_map/ppermute | solution.py:357
  525.5 21.0 %collective-permute-start.29 = (bf16[2,32,2048]{2,1,0:T(8,128)(2,1)S(1)}, bf16[2,32,2048]{2,1,0:T(8,128)(2,1)S(1)}, u32[]{:S(2)}, u32[]{:S(2)}) collective-permute-start(bf16[2,32,2048]{2,1,0:T(8,128)(2,1)S(1)} %get-tuple-element.193), channel_id=1, source_target_pairs={{0,16},{1,17},{2,18},{3,19},{4,20},{5,21},{6,22},{7,23},{8,24},{9,... | collective-permute-start | bytes 786440 | tf_op jit(solution)/shard_map/ppermute | solution.py:357
  546.6 8.1 %collective-permute-start.30 = (bf16[2,32,1024]{2,1,0:T(8,128)(2,1)S(1)}, bf16[2,32,1024]{2,1,0:T(8,128)(2,1)S(1)}, u32[]{:S(2)}, u32[]{:S(2)}) collective-permute-start(bf16[2,32,1024]{2,1,0:T(8,128)(2,1)S(1)} %get-tuple-element.195), channel_id=1, source_target_pairs={{0,8},{1,9},{2,10},{3,11},{4,12},{5,13},{6,14},{7,15},{8,0},{9,1},... | collective-permute-start | bytes 393224 | tf_op jit(solution)/shard_map/ppermute | solution.py:357
  547.5 7.8 %collective-permute-start.31 = (bf16[2,32,1024]{2,1,0:T(8,128)(2,1)S(1)}, bf16[2,32,1024]{2,1,0:T(8,128)(2,1)S(1)}, u32[]{:S(2)}, u32[]{:S(2)}) collective-permute-start(bf16[2,32,1024]{2,1,0:T(8,128)(2,1)S(1)} %get-tuple-element.196), channel_id=1, source_target_pairs={{0,16},{1,17},{2,18},{3,19},{4,20},{5,21},{6,22},{7,23},{8,24},{9,... | collective-permute-start | bytes 393224 | tf_op jit(solution)/shard_map/ppermute | solution.py:357
  552.6 5.0 collective-permute-start.32
  552.9 6.2 %collective-permute-start.41 = (bf16[32,2048]{1,0:T(8,128)(2,1)S(1)}, bf16[32,2048]{1,0:T(8,128)(2,1)S(1)}, u32[]{:S(2)}, u32[]{:S(2)}) collective-permute-start(bf16[32,2048]{1,0:T(8,128)(2,1)S(1)} %fusion.57), channel_id=1, source_target_pairs={{0,2},{1,3},{2,0},{3,1},{4,6},{5,7},{6,4},{7,5},{8,10},{9,11},{10,... | collective-permute-start | bytes 393224 | tf_op jit(solution)/shard_map/ppermute | solution.py:357
  557.6 4.3 collective-permute-start.40
  559.8 4.3 collective-permute-start.39
  560.7 5.2 collective-permute-start.38
  (48 other events, 504.8 us)
Sparse Core Ops, SparseCore 0:
  11.5 113.2 all-gather.2
  127.7 75.8 all-gather.4
  287.5 93.6 reduce-scatter.4
  402.7 105.5 reduce-scatter.2

commit v4 on v3

--- a/solution.py
+++ b/solution.py
@@ -186,8 +186,8 @@
     return jnp.where(lax.broadcasted_iota(jnp.int32, scores.shape, 0) < length, scores, -1e30)
 
 
-def attention_forward_kernel(slots, image, len_ref, q_ref, k_ref, v_ref, o_ref, lse_ref):
-    length = len_ref[image]
+def attention_forward_kernel(slots, len_ref, q_ref, k_ref, v_ref, o_ref, lse_ref):
+    length = len_ref[pl.program_id(0)]
 
     def attend(rows, masked):
         for pair in range(PAIRS):
@@ -289,30 +289,29 @@
     return whole
 
 
-def attention_forward(image, qkv, lengths, filled):
+def attention_forward(qkv, lengths):
     images = lengths.shape[0]
     slots = qkv.shape[0] // images
     steps = HEADS // (2 * PAIRS)
-    block = head_blocks(slots, image)
-    outs = (block, lse_blocks(slots, image))
-    kernel = functools.partial(attention_forward_kernel, slots, image)
-    anywhere = [pl.BlockSpec(memory_space=pl.ANY)] * len(filled)
+
+    def heads(part):
+        return pl.BlockSpec((slots, PAIRS * PAIR), lambda b, h, lens: (b, part * steps + h))
+
     return pl.pallas_call(
-        held_in_place(kernel, len(filled)),
+        functools.partial(attention_forward_kernel, slots),
         out_shape=(
             jax.ShapeDtypeStruct((images * slots, D), BF),
             jax.ShapeDtypeStruct((images * steps, 2 * PAIRS, slots), F32),
         ),
         grid_spec=pltpu.PrefetchScalarGridSpec(
             num_scalar_prefetch=1,
-            grid=(steps,),
-            in_specs=anywhere + [head_blocks(slots, image, part) for part in range(3)],
-            out_specs=outs,
+            grid=(images, steps),
+            in_specs=[heads(part) for part in range(3)],
+            out_specs=(heads(0), pl.BlockSpec((1, 2 * PAIRS, slots), lambda b, h, lens: (b * steps + h, 0, 0))),
         ),
-        input_output_aliases={1 + i: i for i in range(len(filled))},
         cost_estimate=light(),
         name="attention_forward",
-    )(lengths, *filled, qkv, qkv, qkv)
+    )(lengths, qkv, qkv, qkv)
 
 
 def attention_backward(image, qkv, attended, d_attended, lse, lengths, filled):
@@ -364,7 +363,7 @@
 def rotations():
     bits = (lax.axis_size("fsdp") - 1).bit_length()
     if bits == 5:
-        return ((1, 2, 3, 4), (2, 3, 4, 1), (3, 4, 1, 2))
+        return ((1, 2, 3, 4), (2, 3, 1, 4), (3, 1, 2, 4))
     rest = tuple(range(1, bits))
     third = max(1, len(rest) // 3)
     return (rest, rest[third:] + rest[:third], rest[2 * third :] + rest[: 2 * third])
@@ -541,10 +540,7 @@
     hidden = layer_norm(source, ln1_gain, ln1_bias).astype(BF)
     qkv_bias = jnp.concatenate([b_qv[:, :D], jnp.zeros((1, D), F32), b_qv[:, D:]], axis=1)
     qkv = (mm(hidden, w_qkv, NN) + qkv_bias).astype(BF)
-    filled = ()
-    for image in range(images):
-        filled = attention_forward(image, qkv, lengths, filled)
-    attended, lse = filled
+    attended, lse = attention_forward(qkv, lengths)
     middle = source + mm(attended, w_out, NN) + b_out
     normed = layer_norm(middle, ln2_gain, ln2_bias).astype(BF)
     up_act, up_slope = gelu_matmul(normed, [(wide, 0, 4 * D)], b_up)
@@ -557,7 +553,6 @@
     squashed = jax.nn.sigmoid(logits)
     pool_maps = (squashed * pool_share).reshape(images, slots, -1)
     by_image = output.reshape(images, slots, D)
-    pooled = jnp.einsum("bsm,bsd->bmd", pool_maps, by_image, precision=lax.Precision.HIGHEST)
     pool_grad = cotangent.reshape(images, -1, D)
     d_maps = jnp.einsum("bsd,bmd->bsm", by_image, pool_grad, precision=lax.Precision.HIGHEST)
     d_maps = d_maps.reshape(row_total, -1)
@@ -624,11 +619,16 @@
     )
     spread = jnp.concatenate([lines.T, g_map, jnp.zeros((D, pad), F32)], axis=1)
     small = Scattering(spread, order_z)
-    (pooled,) = scatter_step([small], pooled)
+    scatter_step([small])
     d_image = (d_middle + d_norm1).reshape(tokens.shape)
-    for _ in range(len(small.order)):
+    by_image, d_image = tie(by_image, d_image)
+    pooled = jnp.einsum("bsm,bsd->bmd", pool_maps, by_image, precision=lax.Precision.HIGHEST)
+    for step in range(len(small.order)):
         (d_image,) = scatter_step(late + [out_stream], d_image)
-        scatter_step([small])
+        if step == 2:
+            (pooled,) = scatter_step([small], pooled)
+        else:
+            scatter_step([small])
     g_wqkv = jnp.concatenate([item.total() for item in late], axis=1)
     small = small.total()
     joint = out_stream.total()

time: 581 us -> 571 us (0.983)
  waiting for transfers between devices: 121 us -> 106 us
  local copies, waits for them, and re-layouts: 49.2 us -> 60 us
    ppermute x42, waiting for transfers between devices: 111 us -> 89.9 us  [swap(): lax.ppermute(value, 'fsdp', [(i, i ^ 1 << bit) for i in range(count)])]
    all_gather x2, waiting for transfers between devices: 9.14 us -> 15.4 us  [gather(): return lax.all_gather(shard, 'fsdp', axis=0, tiled=True)]
    pallas_call x2 -> x1, Pallas kernels: 21.8 us -> 19.3 us  [attention_forward(): pl.pallas_call(functools.partial(attention_forward_kernel, slots), out_sh...]
  transfers between devices with their start and end apart: 46 -> 46, of which waited for: 24 -> 26; matrix products, arithmetic and copies ran while one was open for 28% -> 30% of each run, Pallas kernels for 24% -> 24%
where the time goes in v4:
time: 571 us; the launch traced here: 565 us
  Pallas kernels  145 us (25%)
  waiting for transfers between devices  106 us (19%)
  matrix products  104 us (18%)
  other arithmetic  77.7 us (14%)
  local copies, waits for them, and re-layouts  60 us (11%)
  starting transfers between devices  57.5 us (10%)
  between operations  15.3 us (3%)
    dot_general x15, matrix products, mm(): return lax.dot_general(left, right, dims, preferred_element_type=F32)  92.9 us
    ppermute x42, waiting for transfers between devices, swap(): lax.ppermute(value, 'fsdp', [(i, i ^ 1 << bit) for i in range(count)])  89.9 us
    ppermute x42, starting transfers between devices, swap(): lax.ppermute(value, 'fsdp', [(i, i ^ 1 << bit) for i in range(count)])  57.3 us
    pallas_call x2, Pallas kernels, gelu_matmul(): pl.pallas_call(functools.partial(gelu_matmul_kernel, rows // 4, tiles), o...  43.6 us
    pallas_call x2, Pallas kernels, attention_backward(): pl.pallas_call(held_in_place(kernel, len(filled)), out_shape=tuple((jax.S...  34 us
    pallas_call x2, Pallas kernels, back_product(): pl.pallas_call(functools.partial(back_product_kernel, count), out_shape=j...  30.7 us
    pallas_call x1, Pallas kernels, attention_forward(): pl.pallas_call(functools.partial(attention_forward_kernel, slots), out_sh...  19.3 us
    pallas_call x1, Pallas kernels, slope_matmul(): pl.pallas_call(functools.partial(slope_matmul_kernel, rows // 4), out_sha...  17.5 us
  transfers between devices with their start and end apart: 46, of which 26 were waited for; matrix products, arithmetic and copies ran while one was open for 30% of the time, Pallas kernels for 24%

profile of v4, /device:TPU:0, one launch (start us, length us, event | category | flops | bytes accessed | tf_op | source)
XLA Modules:
  0.0 565.4 jit_solution(13065702428920423130)
XLA Ops:
  20.3 4.1 collective-permute-start.1
  27.3 5.2 collective-permute-done.1
  32.5 5.0 collective-permute-done
  37.6 4.2 collective-permute-done.2
  49.4 5.4 collective-permute-done.5
  55.2 12.7 %collective-permute-done.6 = bf16[2,2,32,1024]{3,2,1,0:T(8,128)(2,1)S(1)} collective-permute-done((bf16[2,2,32,1024]{3,2,1,0:T(8,128)(2,1)S(1)}, bf16[2,2,32,1024]{3,2,1,0:T(8,128)(2,1)S(1)}, u32[]{:S(2)}, u32[]{:S(2)}) %collective-permute-start.6) | collective-permute-done | bytes 262176 | tf_op jit(solution)/shard_map/ppermute | solution.py:356
  71.7 9.8 %collective-permute-done.9 = bf16[2,2,2,32,1024]{4,3,2,1,0:T(8,128)(2,1)} collective-permute-done((bf16[2,2,2,32,1024]{4,3,2,1,0:T(8,128)(2,1)S(1)}, bf16[2,2,2,32,1024]{4,3,2,1,0:T(8,128)(2,1)}, u32[]{:S(2)}, u32[]{:S(2)}) %collective-permute-start.9) | collective-permute-done | bytes 524320 | tf_op jit(solution)/shard_map/ppermute | solution.py:356
  82.8 4.1 collective-permute-done.10
  118.1 9.9 %add_convert_fusion.q_ref.k_ref.v_ref.refs_0_.refs_1_.refs_2_.refs_3_.refs_4_.refs_5_ = bf16[1152,3072]{1,0:T(8,128)(2,1)} fusion(bf16[1152,1024]{1,0:T(8,128)(2,1)S(1)} %fusion.13, f32[3072]{0:T(1024)S(1)} %bitcast.417, bf16[1024,1024]{1,0:T(8,128)(2,1)S(1)} %get-tuple-element.409.refs_5_, bf16[1024,1024]{1,0:T(8,128)(2,1)S(1)} %get-tuple-element.408.refs_4_, ...), kind=kOutput, calls=%fused_computation | convolution fusion | flops 7273709568 | bytes 15740928 | tf_op jit(solution)/shard_map/dot_general | solution.py:28
  128.0 19.3 %attention_forward.1 = (bf16[1152,1024]{1,0:T(8,128)(2,1)}, f32[8,4,576]{2,1,0:T(4,128)}) custom-call(s32[2]{0:T(128)} %bitcast.418, bf16[1152,3072]{1,0:T(8,128)(2,1)} %add_convert_fusion.q_ref.k_ref.v_ref.refs_0_.refs_1_.refs_2_.refs_3_.refs_4_.refs_5_, bf16[1152,3072]{1,0:T(8,128)(2,1)} %add_convert_fusion.q_ref.k_ref.v_ref.refs_0_.refs_1_.refs_2_.refs_3_.refs_4_.refs_5_, ...), custom_call_target="tpu_custom_call" | custom-call | flops 1024 | bytes 1024 | tf_op jit(solution)/shard_map/attention_forward/pallas_call | solution.py:300
  148.2 5.3 fusion.96
  157.9 32.4 %gelu_matmul.2 = (bf16[1152,4096]{1,0:T(8,128)(2,1)}, bf16[1152,4096]{1,0:T(8,128)(2,1)}) custom-call(bf16[1152,1024]{1,0:T(8,128)(2,1)} %add_convert_fusion.4.x_ref, f32[1,4096]{1,0:T(1,128)} %reshape.572.b_ref, bf16[1024,6144]{1,0:T(8,128)(2,1)} %all-gather.3.cloned.1.call-done.refs_0_.refs_1_), custom_call_target="tpu_custom_call" | custom-call | flops 1024 | bytes 1024 | tf_op jit(solution)/shard_map/gelu_matmul/pallas_call | solution.py:125
  190.3 15.4 %all-gather.5.cloned.1.call-done.w_ref = bf16[4096,1024]{1,0:T(8,128)(2,1)} async-done(((bf16[128,1024]{1,0:T(8,128)(2,1)}), bf16[4096,1024]{1,0:T(8,128)(2,1)}) %all-gather.5.cloned.1.call-update) | async-done | bytes 8388624 | tf_op jit(solution)/shard_map/all_gather | solution.py:343
  205.8 15.3 %fusion.97 = (f32[1152]{0:T(1024)S(1)}, f32[1152,1024]{1,0:T(8,128)S(1)}) fusion(f32[1024]{0:T(1024)S(1)} %bitcast.422, f32[1152,1024]{1,0:T(8,128)} %copy-done.3, bf16[1152,4096]{1,0:T(8,128)(2,1)} %get-tuple-element.129, bf16[4096,1024]{1,0:T(8,128)(2,1)} %all-gather.5.cloned.1.call-done.w_ref), kind=kOutput, calls=%fused_computation.266 | convolution fusion | flops 9667214336 | bytes 27271680 | tf_op jit(solution)/shard_map/dot_general | solution.py:28
  221.8 4.1 fusion.76
  226.0 4.6 add_convert_fusion.3.x_ref
  230.6 11.1 %gelu_matmul.3 = (bf16[1152,1024]{1,0:T(8,128)(2,1)}, bf16[1152,1024]{1,0:T(8,128)(2,1)}) custom-call(bf16[1152,1024]{1,0:T(8,128)(2,1)} %add_convert_fusion.3.x_ref, f32[1,1024]{1,0:T(1,128)} %get-tuple-element.394.b_ref, bf16[1024,6144]{1,0:T(8,128)(2,1)} %all-gather.3.cloned.1.call-done.refs_0_.refs_1_), custom_call_target="tpu_custom_call" | custom-call | flops 1024 | bytes 1024 | tf_op jit(solution)/shard_map/gelu_matmul/pallas_call | solution.py:125
  244.4 3.9 fusion.78
  250.0 6.1 %multiply_reduce_fusion = (bf16[1024]{0:T(1024)(128)(2,1)S(1)}, f32[1152]{0:T(1024)S(1)}, f32[1152]{0:T(1024)S(1)}, bf16[1024]{0:T(1024)(128)(2,1)S(1)}, f32[1152,1024]{1,0:T(8,128)S(1)}) fusion(f32[1152,1024]{1,0:T(8,128)S(1)} %bitcast.379, f32[1152]{0:T(1024)S(1)} %add_rsqrt_fusion, f32[1152]{0:T(1024)S(1)} %broadcast_multiply_fusion.7, ...), kind=kOutput, calls=%fused_computation.31 | convolution fusion | flops 2426531840 | bytes 13920256 | tf_op jit(solution)/shard_map/dot_general | solution.py:28
  256.1 3.4 fusion.91
  259.6 13.3 %convolution_convert_fusion = bf16[4096,1024]{1,0:T(8,128)(2,1)} fusion(bf16[1152,4096]{1,0:T(8,128)(2,1)S(1)} %bitcast.436, bf16[1152,1024]{1,0:T(8,128)(2,1)S(1)} %get-tuple-element.138.x_ref), kind=kOutput, calls=%fused_computation.3 | convolution fusion | flops 9667870720 | bytes 20185088 | tf_op jit(solution)/shard_map/dot_general | solution.py:28
  272.9 4.9 dynamic-slice_bitcast_fusion.2
  278.2 4.1 convolution_convert_fusion.7
  285.0 4.1 add_convert_fusion.2
  289.3 17.5 %slope_matmul.1 = (bf16[1152,4096]{1,0:T(8,128)(2,1)}, f32[1,4096]{1,0:T(1,128)}) custom-call(bf16[1152,1024]{1,0:T(8,128)(2,1)} %copy-done.15, bf16[4096,1024]{1,0:T(8,128)(2,1)} %all-gather.5.cloned.1.call-done.w_ref, bf16[1152,4096]{1,0:T(8,128)(2,1)} %get-tuple-element.139.slope_ref), custom_call_target="tpu_custom_call" | custom-call | flops 1024 | bytes 1024 | tf_op jit(solution)/shard_map/slope_matmul/pallas_call | solution.py:166
  306.7 13.7 %convolution_convert_fusion.1 = bf16[1024,4096]{1,0:T(8,128)(2,1)S(1)} fusion(bf16[1152,1024]{1,0:T(8,128)(2,1)S(1)} %copy-done.16, bf16[1152,4096]{1,0:T(8,128)(2,1)} %get-tuple-element.141.refs_0_), kind=kOutput, calls=%fused_computation.4 | convolution fusion | flops 9667870720 | bytes 20185088 | tf_op jit(solution)/shard_map/dot_general | solution.py:28
  320.5 3.9 dynamic-slice_bitcast_fusion
  324.7 16.9 %back_product.2 = f32[1152,1024]{1,0:T(8,128)} custom-call(bf16[1152,4096]{1,0:T(8,128)(2,1)} %get-tuple-element.141.refs_0_, bf16[1024,6144]{1,0:T(8,128)(2,1)} %all-gather.3.cloned.1.call-done.refs_0_.refs_1_), custom_call_target="tpu_custom_call" | custom-call | flops 1024 | bytes 1024 | tf_op jit(solution)/shard_map/back_product/pallas_call | solution.py:150
  341.6 5.6 multiply_reduce_fusion.1
  347.3 4.8 convert_reduce_fusion.4
  352.2 3.2 convolution_convert_fusion.6
  357.6 5.8 %convolution_convert_fusion.2.refs_4_.refs_7_ = bf16[1152,1024]{1,0:T(8,128)(2,1)} fusion(bf16[1024,6144]{1,0:T(8,128)(2,1)} %all-gather.3.cloned.1.call-done.refs_0_.refs_1_, f32[1152,1024]{1,0:T(8,128)S(1)} %get-tuple-element.337), kind=kOutput, calls=%fused_computation.54 | convolution fusion | flops 2418278400 | bytes 9175040 | tf_op jit(solution)/shard_map/dot_general | solution.py:28
  367.2 23.5 %attention_backward.2 = (bf16[1152,1024]{1,0:T(8,128)(2,1)}, bf16[1152,1024]{1,0:T(8,128)(2,1)}, bf16[1152,1024]{1,0:T(8,128)(2,1)}) custom-call(s32[2]{0:T(128)} %bitcast.419, bf16[1152,3072]{1,0:T(8,128)(2,1)} %add_convert_fusion.q_ref.k_ref.v_ref.refs_0_.refs_1_.refs_2_.refs_3_.refs_4_.refs_5_, ...), custom_call_target="tpu_custom_call" | custom-call | flops 1024 | bytes 1024 | tf_op jit(solution)/shard_map/attention_backward/pallas_call | solution.py:324
  394.8 3.3 fusion.27
  398.1 5.7 %add_convert_fusion.1 = bf16[16,32,4096]{2,1,0:T(8,128)(2,1)} fusion(bf16[16,32,4096]{2,1,0:T(8,128)(2,1)} %collective-permute-done.17, bf16[16,32,4096]{2,1,0:T(8,128)(2,1)S(1)} %copy-done.11), kind=kLoop, calls=%fused_computation.1 | loop fusion | flops 8388608 | bytes 12582912 | tf_op jit(solution)/shard_map/convert_element_type | solution.py:576
  403.8 10.5 %attention_backward.3 = (bf16[1152,1024]{1,0:T(8,128)(2,1)}, bf16[1152,1024]{1,0:T(8,128)(2,1)}, bf16[1152,1024]{1,0:T(8,128)(2,1)}) custom-call(s32[2]{0:T(128)} %bitcast.420, bf16[1152,1024]{1,0:T(8,128)(2,1)} %get-tuple-element.157.refs_0_, ...), custom_call_target="tpu_custom_call", output_to_operand_aliasing={{0}: (1, {}), {1}: (2, {}), {2}: (3, {})} | custom-call | flops 1024 | bytes 1024 | tf_op jit(solution)/shard_map/attention_backward/pallas_call | solution.py:324
  416.7 5.0 convolution_convert_fusion.5
  421.9 3.1 convolution_convert_fusion.4
  425.7 3.3 convolution_convert_fusion.3
  430.5 24.3 %collective-permute-start.28 = (bf16[2,2,32,2048]{3,2,1,0:T(8,128)(2,1)}, bf16[2,2,32,2048]{3,2,1,0:T(8,128)(2,1)}, u32[]{:S(2)}, u32[]{:S(2)}) collective-permute-start(bf16[2,2,32,2048]{3,2,1,0:T(8,128)(2,1)} %copy.330), channel_id=1, source_target_pairs={{0,8},{1,9},{2,10},{3,11},{4,12},{5,13},{6,14},{7,15},{8,0},{9,1},... | collective-permute-start | bytes 1572872 | tf_op jit(solution)/shard_map/ppermute | solution.py:356
  459.4 13.8 %back_product.3 = f32[1152,1024]{1,0:T(8,128)} custom-call(bf16[1152,1024]{1,0:T(8,128)(2,1)} %get-tuple-element.178.refs_0_, bf16[1152,1024]{1,0:T(8,128)(2,1)} %get-tuple-element.179.refs_1_, bf16[1152,1024]{1,0:T(8,128)(2,1)} %get-tuple-element.180.refs_2_, bf16[1024,1024]{1,0:T(8,128)(2,1)} %copy-done.18, bf16[1024,1024]{1,0:T(8,128)(2,1)} %copy-done.19, ...), custom_call_target="tpu_custom_call" | custom-call | flops 1024 | bytes 1024 | tf_op jit(solution)/shard_map/back_product/pallas_call | solution.py:150
  473.2 4.2 fusion.15
  485.5 6.5 %fusion.18 = f32[1152,1024]{1,0:T(8,128)} fusion(f32[1152,1024]{1,0:T(8,128)} %copy-done.9, bf16[2,1,576,1024]{3,2,1,0:T(8,128)(2,1)S(1)} %copy-done.5, f32[1152,1024]{1,0:T(8,128)} %back_product.3, f32[1152]{0:T(1024)S(1)} %broadcast_multiply_fusion.1, f32[1152]{0:T(1024)S(1)} %broadcast_multiply_fusion.2, f32[1024]{0:T(1024)S(1)} %bitcast.405, ...), kind=kLoop, calls=%fused_computation.29 | loop fusion | flops 10616832 | bytes 16537600 | tf_op jit(solution)/shard_map/add | solution.py:623
  492.1 4.7 collective-permute-done.23
  497.0 3.0 fusion.80
  508.6 7.4 %collective-permute-done.37 = bf16[32,128]{0,1:T(8,128)(2,1)S(1)} collective-permute-done((bf16[32,128]{0,1:T(8,128)(2,1)S(1)}, bf16[32,128]{0,1:T(8,128)(2,1)S(1)}, u32[]{:S(2)}, u32[]{:S(2)}) %collective-permute-start.37) | collective-permute-done | bytes 8224 | tf_op jit(solution)/shard_map/ppermute | solution.py:356
  525.6 3.0 collective-permute-done.31
  542.4 5.2 collective-permute-done.41
  (355 shorter events, 144.2 us)
Async XLA Ops:
  7.2 214.6 %copy-start = (f32[2,1,8,1024]{3,2,1,0:T(8,128)S(1)}, f32[2,1,8,1024]{3,2,1,0:T(8,128)}, u32[]{:S(2)}) copy-start(f32[2,1,8,1024]{3,2,1,0:T(8,128)} %param.22) | copy-start | bytes 196612
  7.2 63.6 %copy-start.4 = (bf16[2,1,576,1024]{3,2,1,0:T(8,128)(2,1)S(1)}, bf16[2,1,576,1024]{3,2,1,0:T(8,128)(2,1)}, u32[]{:S(2)}) copy-start(bf16[2,1,576,1024]{3,2,1,0:T(8,128)(2,1)} %param.20) | copy-start | bytes 7077892
  7.2 140.9 %all-gather.3.cloned.1.call-start = ((), (), s32[]{:S(2)}) async-start(), calls=%async_computation.2 | async-start | bytes 12976128 | tf_op jit(solution)/shard_map/all_gather | solution.py:343
  9.2 196.6 %all-gather.5.cloned.1.call-start = ((), (), s32[]{:S(2)}) async-start(), calls=%async_computation.3 | async-start | bytes 8650752 | tf_op jit(solution)/shard_map/all_gather | solution.py:343
  10.0 545.0 %reduce-scatter.5.cloned.1.call-start = ((), (), s32[]{:S(2)}) async-start(), calls=%async_computation.5 | async-start | bytes 4456448 | tf_op jit(solution)/shard_map/reduce_scatter | solution.py:460
  20.3 12.2 %collective-permute-start.1 = (bf16[32,1024]{1,0:T(8,128)(2,1)S(1)}, bf16[32,1024]{1,0:T(8,128)(2,1)S(1)}, u32[]{:S(2)}, u32[]{:S(2)}) collective-permute-start(bf16[32,1024]{1,0:T(8,128)(2,1)S(1)} %get-tuple-element.114), channel_id=1, source_target_pairs={{0,16},{1,17},{2,18},{3,19},{4,20},{5,21},{6,22},{7,23},{8,24},{9,... | collective-permute-start | bytes 196616 | tf_op jit(solution)/shard_map/ppermute | solution.py:356
  24.4 13.1 %collective-permute-start = (bf16[32,1024]{1,0:T(8,128)(2,1)S(1)}, bf16[32,1024]{1,0:T(8,128)(2,1)S(1)}, u32[]{:S(2)}, u32[]{:S(2)}) collective-permute-start(bf16[32,1024]{1,0:T(8,128)(2,1)S(1)} %get-tuple-element.113), channel_id=1, source_target_pairs={{0,16},{1,17},{2,18},{3,19},{4,20},{5,21},{6,22},{7,23},{8,24},{9,... | collective-permute-start | bytes 196616 | tf_op jit(solution)/shard_map/ppermute | solution.py:356
  24.5 17.4 %collective-permute-start.2 = (bf16[32,1152]{1,0:T(8,128)(2,1)S(1)}, bf16[32,1152]{1,0:T(8,128)(2,1)S(1)}, u32[]{:S(2)}, u32[]{:S(2)}) collective-permute-start(bf16[32,1152]{1,0:T(8,128)(2,1)S(1)} %concatenate.34), channel_id=1, source_target_pairs={{0,16},{1,17},{2,18},{3,19},{4,20},{5,21},{6,22},{7,23},{8,24},{9,... | collective-permute-start | bytes 221192 | tf_op jit(solution)/shard_map/ppermute | solution.py:356
  41.9 5.3 collective-permute-start.3
  44.3 5.0 collective-permute-start.4
  45.9 9.0 %collective-permute-start.5 = (bf16[2,32,1152]{2,1,0:T(8,128)(2,1)S(1)}, bf16[2,32,1152]{2,1,0:T(8,128)(2,1)S(1)}, u32[]{:S(2)}, u32[]{:S(2)}) collective-permute-start(bf16[2,32,1152]{2,1,0:T(8,128)(2,1)S(1)} %broadcast_select_fusion.10), channel_id=1, source_target_pairs={{0,8},{1,9},{2,10},{3,11},{4,12},{5,13},{6,14},{7,15},{8,0},{9,1},... | collective-permute-start | bytes 442376 | tf_op jit(solution)/shard_map/ppermute | solution.py:356
  55.0 12.9 %collective-permute-start.6 = (bf16[2,2,32,1024]{3,2,1,0:T(8,128)(2,1)S(1)}, bf16[2,2,32,1024]{3,2,1,0:T(8,128)(2,1)S(1)}, u32[]{:S(2)}, u32[]{:S(2)}) collective-permute-start(bf16[2,2,32,1024]{3,2,1,0:T(8,128)(2,1)S(1)} %broadcast_select_fusion.8), channel_id=1, source_target_pairs={{0,8},{1,9},{2,10},{3,11},{4,12},{5,13},{6,14},{7,15},{8,0},{9,1},... | collective-permute-start | bytes 786440 | tf_op jit(solution)/shard_map/ppermute | solution.py:356
  55.0 13.0 %collective-permute-start.7 = (bf16[2,2,32,1024]{3,2,1,0:T(8,128)(2,1)S(1)}, bf16[2,2,32,1024]{3,2,1,0:T(8,128)(2,1)S(1)}, u32[]{:S(2)}, u32[]{:S(2)}) collective-permute-start(bf16[2,2,32,1024]{3,2,1,0:T(8,128)(2,1)S(1)} %broadcast_select_fusion.7), channel_id=1, source_target_pairs={{0,2},{1,3},{2,0},{3,1},{4,6},{5,7},{6,4},{7,5},{8,10},{9,11},{10,... | collective-permute-start | bytes 786440 | tf_op jit(solution)/shard_map/ppermute | solution.py:356
  55.1 13.9 %collective-permute-start.8 = (bf16[2,2,32,1152]{3,2,1,0:T(8,128)(2,1)S(1)}, bf16[2,2,32,1152]{3,2,1,0:T(8,128)(2,1)S(1)}, u32[]{:S(2)}, u32[]{:S(2)}) collective-permute-start(bf16[2,2,32,1152]{3,2,1,0:T(8,128)(2,1)S(1)} %broadcast_select_fusion.6), channel_id=1, source_target_pairs={{0,4},{1,5},{2,6},{3,7},{4,0},{5,1},{6,2},{7,3},{8,12},{9,13},{10,... | collective-permute-start | bytes 884744 | tf_op jit(solution)/shard_map/ppermute | solution.py:356
  69.9 11.5 %collective-permute-start.9 = (bf16[2,2,2,32,1024]{4,3,2,1,0:T(8,128)(2,1)S(1)}, bf16[2,2,2,32,1024]{4,3,2,1,0:T(8,128)(2,1)}, u32[]{:S(2)}, u32[]{:S(2)}) collective-permute-start(bf16[2,2,2,32,1024]{4,3,2,1,0:T(8,128)(2,1)S(1)} %broadcast_select_fusion.5), channel_id=1, source_target_pairs={{0,4},{1,5},{2,6},{3,7},{4,0},{5,1},{6,2},{7,3},{8,12},{9,13},{10,... | collective-permute-start | bytes 1572872 | tf_op jit(solution)/shard_map/ppermute | solution.py:356
  69.9 16.9 %collective-permute-start.10 = (bf16[2,2,2,32,1024]{4,3,2,1,0:T(8,128)(2,1)}, bf16[2,2,2,32,1024]{4,3,2,1,0:T(8,128)(2,1)}, u32[]{:S(2)}, u32[]{:S(2)}) collective-permute-start(bf16[2,2,2,32,1024]{4,3,2,1,0:T(8,128)(2,1)} %broadcast_select_fusion.4), channel_id=1, source_target_pairs={{0,8},{1,9},{2,10},{3,11},{4,12},{5,13},{6,14},{7,15},{8,0},{9,1},... | collective-permute-start | bytes 1572872 | tf_op jit(solution)/shard_map/ppermute | solution.py:356
  71.2 18.0 %collective-permute-start.11 = (bf16[2,2,2,32,1152]{4,3,2,1,0:T(8,128)(2,1)}, bf16[2,2,2,32,1152]{4,3,2,1,0:T(8,128)(2,1)}, u32[]{:S(2)}, u32[]{:S(2)}) collective-permute-start(bf16[2,2,2,32,1152]{4,3,2,1,0:T(8,128)(2,1)} %broadcast_select_fusion.3), channel_id=1, source_target_pairs={{0,2},{1,3},{2,0},{3,1},{4,6},{5,7},{6,4},{7,5},{8,10},{9,11},{10,... | collective-permute-start | bytes 1769480 | tf_op jit(solution)/shard_map/ppermute | solution.py:356
  91.6 8.7 %collective-permute-start.12 = (bf16[2,2,2,2,32,1152]{5,4,3,2,1,0:T(8,128)(2,1)}, bf16[2,2,2,2,32,1152]{5,4,3,2,1,0:T(8,128)(2,1)}, u32[]{:S(2)}, u32[]{:S(2)}) collective-permute-start(bf16[2,2,2,2,32,1152]{5,4,3,2,1,0:T(8,128)(2,1)} %broadcast_select_fusion), channel_id=1, source_target_pairs={{0,1},{1,0},{2,3},{3,2},{4,5},{5,4},{6,7},{7,6},{8,9},{9,8},{10,11... | collective-permute-start | bytes 3538952 | tf_op jit(solution)/shard_map/ppermute | solution.py:356
  92.5 19.3 %collective-permute-start.13 = (bf16[2,2,2,2,32,1024]{5,4,3,2,1,0:T(8,128)(2,1)S(1)}, bf16[2,2,2,2,32,1024]{5,4,3,2,1,0:T(8,128)(2,1)}, u32[]{:S(2)}, u32[]{:S(2)}) collective-permute-start(bf16[2,2,2,2,32,1024]{5,4,3,2,1,0:T(8,128)(2,1)S(1)} %broadcast_select_fusion.2), channel_id=1, source_target_pairs={{0,1},{1,0},{2,3},{3,2},{4,5},{5,4},{6,7},{7,6},{8,9},{9,8},{10,11... | collective-permute-start | bytes 3145736 | tf_op jit(solution)/shard_map/ppermute | solution.py:356
  93.0 18.8 %collective-permute-start.14 = (bf16[2,2,2,2,32,1024]{5,4,3,2,1,0:T(8,128)(2,1)}, bf16[2,2,2,2,32,1024]{5,4,3,2,1,0:T(8,128)(2,1)}, u32[]{:S(2)}, u32[]{:S(2)}) collective-permute-start(bf16[2,2,2,2,32,1024]{5,4,3,2,1,0:T(8,128)(2,1)} %broadcast_select_fusion.1), channel_id=1, source_target_pairs={{0,1},{1,0},{2,3},{3,2},{4,5},{5,4},{6,7},{7,6},{8,9},{9,8},{10,11... | collective-permute-start | bytes 3145736 | tf_op jit(solution)/shard_map/ppermute | solution.py:356
  277.8 7.2 %collective-permute-start.15 = (bf16[16,128,1024]{2,1,0:T(8,128)(2,1)S(1)}, bf16[16,128,1024]{2,1,0:T(8,128)(2,1)S(1)}, u32[]{:S(2)}, u32[]{:S(2)}) collective-permute-start(bf16[16,128,1024]{2,1,0:T(8,128)(2,1)S(1)} %get-tuple-element.132), channel_id=1, source_target_pairs={{0,1},{1,0},{2,3},{3,2},{4,5},{5,4},{6,7},{7,6},{8,9},{9,8},{10,11... | collective-permute-start | bytes 12582920 | tf_op jit(solution)/shard_map/ppermute | solution.py:356
  289.2 267.6 %reduce-scatter.3.cloned.1.call-start = ((), (), s32[]{:S(2)}) async-start(), calls=%async_computation.4 | async-start | bytes 4456448 | tf_op jit(solution)/shard_map/reduce_scatter | solution.py:460
  324.4 73.7 %collective-permute-start.17 = (bf16[16,32,4096]{2,1,0:T(8,128)(2,1)}, bf16[16,32,4096]{2,1,0:T(8,128)(2,1)}, u32[]{:S(2)}, u32[]{:S(2)}) collective-permute-start(bf16[16,32,4096]{2,1,0:T(8,128)(2,1)} %get-tuple-element.144), channel_id=1, source_target_pairs={{0,1},{1,0},{2,3},{3,2},{4,5},{5,4},{6,7},{7,6},{8,9},{9,8},{10,11... | collective-permute-start | bytes 12582920 | tf_op jit(solution)/shard_map/ppermute | solution.py:356
  363.4 31.3 %collective-permute-start.16 = (bf16[2,2,2,2,32,2048]{5,4,0,3,1,2:T(8,128)(2,1)}, bf16[2,2,2,2,32,2048]{5,4,0,3,1,2:T(8,128)(2,1)}, u32[]{:S(2)}, u32[]{:S(2)}) collective-permute-start(bf16[2,2,2,2,32,2048]{5,4,0,3,1,2:T(8,128)(2,1)} %copy_bitcast_fusion), channel_id=1, source_target_pairs={{0,1},{1,0},{2,3},{3,2},{4,5},{5,4},{6,7},{7,6},{8,9},{9,8},{10,11... | collective-permute-start | bytes 6291464 | tf_op jit(solution)/shard_map/ppermute | solution.py:356
  398.1 16.3 %collective-permute-start.18 = (bf16[2,2,2,32,2048]{4,3,0,2,1:T(8,128)(2,1)}, bf16[2,2,2,32,2048]{4,3,0,2,1:T(8,128)(2,1)}, u32[]{:S(2)}, u32[]{:S(2)}) collective-permute-start(bf16[2,2,2,32,2048]{4,3,0,2,1:T(8,128)(2,1)} %get-tuple-element.151), channel_id=1, source_target_pairs={{0,4},{1,5},{2,6},{3,7},{4,0},{5,1},{6,2},{7,3},{8,12},{9,13},{10,... | collective-permute-start | bytes 3145736 | tf_op jit(solution)/shard_map/ppermute | solution.py:356
  421.8 33.8 %collective-permute-start.19 = (bf16[2,2,2,2,32,1024]{5,4,0,2,1,3:T(8,128)(2,1)S(1)}, bf16[2,2,2,2,32,1024]{5,4,0,2,1,3:T(8,128)(2,1)S(1)}, u32[]{:S(2)}, u32[]{:S(2)}) collective-permute-start(bf16[2,2,2,2,32,1024]{5,4,0,2,1,3:T(8,128)(2,1)S(1)} %copy_bitcast_fusion.5), channel_id=1, source_target_pairs={{0,1},{1,0},{2,3},{3,2},{4,5},{5,4},{6,7},{7,6},{8,9},{9,8},{10,11... | collective-permute-start | bytes 3145736 | tf_op jit(solution)/shard_map/ppermute | solution.py:356
  425.2 31.6 %collective-permute-start.20 = (bf16[2,2,2,2,32,1024]{5,4,0,3,1,2:T(8,128)(2,1)S(1)}, bf16[2,2,2,2,32,1024]{5,4,0,3,1,2:T(8,128)(2,1)S(1)}, u32[]{:S(2)}, u32[]{:S(2)}) collective-permute-start(bf16[2,2,2,2,32,1024]{5,4,0,3,1,2:T(8,128)(2,1)S(1)} %copy_bitcast_fusion.4), channel_id=1, source_target_pairs={{0,1},{1,0},{2,3},{3,2},{4,5},{5,4},{6,7},{7,6},{8,9},{9,8},{10,11... | collective-permute-start | bytes 3145736 | tf_op jit(solution)/shard_map/ppermute | solution.py:356
  429.2 28.8 %collective-permute-start.21 = (bf16[2,2,2,2,32,1024]{5,4,0,3,2,1:T(8,128)(2,1)S(1)}, bf16[2,2,2,2,32,1024]{5,4,0,3,2,1:T(8,128)(2,1)S(1)}, u32[]{:S(2)}, u32[]{:S(2)}) collective-permute-start(bf16[2,2,2,2,32,1024]{5,4,0,3,2,1:T(8,128)(2,1)S(1)} %copy_bitcast_fusion.3), channel_id=1, source_target_pairs={{0,1},{1,0},{2,3},{3,2},{4,5},{5,4},{6,7},{7,6},{8,9},{9,8},{10,11... | collective-permute-start | bytes 3145736 | tf_op jit(solution)/shard_map/ppermute | solution.py:356
  430.5 76.8 %collective-permute-start.28 = (bf16[2,2,32,2048]{3,2,1,0:T(8,128)(2,1)}, bf16[2,2,32,2048]{3,2,1,0:T(8,128)(2,1)}, u32[]{:S(2)}, u32[]{:S(2)}) collective-permute-start(bf16[2,2,32,2048]{3,2,1,0:T(8,128)(2,1)} %copy.330), channel_id=1, source_target_pairs={{0,8},{1,9},{2,10},{3,11},{4,12},{5,13},{6,14},{7,15},{8,0},{9,1},... | collective-permute-start | bytes 1572872 | tf_op jit(solution)/shard_map/ppermute | solution.py:356
  483.0 2.0 collective-permute-start.22
  485.1 11.6 %collective-permute-start.23 = (bf16[2,2,2,32,128]{3,4,0,2,1:T(8,128)(2,1)S(1)}, bf16[2,2,2,32,128]{3,4,0,2,1:T(8,128)(2,1)S(1)}, u32[]{:S(2)}, u32[]{:S(2)}) collective-permute-start(bf16[2,2,2,32,128]{3,4,0,2,1:T(8,128)(2,1)S(1)} %get-tuple-element.355), channel_id=1, source_target_pairs={{0,8},{1,9},{2,10},{3,11},{4,12},{5,13},{6,14},{7,15},{8,0},{9,1},... | collective-permute-start | bytes 196616 | tf_op jit(solution)/shard_map/ppermute | solution.py:356
  496.9 5.2 collective-permute-start.24
  502.2 5.1 collective-permute-start.36
  502.3 13.7 %collective-permute-start.25 = (bf16[2,2,2,32,1024]{4,3,0,2,1:T(8,128)(2,1)S(1)}, bf16[2,2,2,32,1024]{4,3,0,2,1:T(8,128)(2,1)S(1)}, u32[]{:S(2)}, u32[]{:S(2)}) collective-permute-start(bf16[2,2,2,32,1024]{4,3,0,2,1:T(8,128)(2,1)S(1)} %copy-done.30), channel_id=1, source_target_pairs={{0,2},{1,3},{2,0},{3,1},{4,6},{5,7},{6,4},{7,5},{8,10},{9,11},{10,... | collective-permute-start | bytes 1572872 | tf_op jit(solution)/shard_map/ppermute | solution.py:356
  502.6 13.8 %collective-permute-start.26 = (bf16[2,2,2,32,1024]{4,3,0,2,1:T(8,128)(2,1)}, bf16[2,2,2,32,1024]{4,3,0,2,1:T(8,128)(2,1)S(1)}, u32[]{:S(2)}, u32[]{:S(2)}) collective-permute-start(bf16[2,2,2,32,1024]{4,3,0,2,1:T(8,128)(2,1)} %get-tuple-element.186), channel_id=1, source_target_pairs={{0,4},{1,5},{2,6},{3,7},{4,0},{5,1},{6,2},{7,3},{8,12},{9,13},{10,... | collective-permute-start | bytes 1572872 | tf_op jit(solution)/shard_map/ppermute | solution.py:356
  504.6 13.1 %collective-permute-start.27 = (bf16[2,2,2,32,1024]{4,3,0,2,1:T(8,128)(2,1)}, bf16[2,2,2,32,1024]{4,3,0,2,1:T(8,128)(2,1)S(1)}, u32[]{:S(2)}, u32[]{:S(2)}) collective-permute-start(bf16[2,2,2,32,1024]{4,3,0,2,1:T(8,128)(2,1)} %get-tuple-element.187), channel_id=1, source_target_pairs={{0,8},{1,9},{2,10},{3,11},{4,12},{5,13},{6,14},{7,15},{8,0},{9,1},... | collective-permute-start | bytes 1572872 | tf_op jit(solution)/shard_map/ppermute | solution.py:356
  507.3 8.7 %collective-permute-start.37 = (bf16[32,128]{0,1:T(8,128)(2,1)S(1)}, bf16[32,128]{0,1:T(8,128)(2,1)S(1)}, u32[]{:S(2)}, u32[]{:S(2)}) collective-permute-start(bf16[32,128]{0,1:T(8,128)(2,1)S(1)} %fusion.84), channel_id=1, source_target_pairs={{0,16},{1,17},{2,18},{3,19},{4,20},{5,21},{6,22},{7,23},{8,24},{9,... | collective-permute-start | bytes 24584 | tf_op jit(solution)/shard_map/ppermute | solution.py:356
  517.9 6.4 %collective-permute-start.29 = (bf16[2,2,32,1024]{3,2,1,0:T(8,128)(2,1)S(1)}, bf16[2,2,32,1024]{3,2,1,0:T(8,128)(2,1)S(1)}, u32[]{:S(2)}, u32[]{:S(2)}) collective-permute-start(bf16[2,2,32,1024]{3,2,1,0:T(8,128)(2,1)S(1)} %copy.331), channel_id=1, source_target_pairs={{0,4},{1,5},{2,6},{3,7},{4,0},{5,1},{6,2},{7,3},{8,12},{9,13},{10,... | collective-permute-start | bytes 786440 | tf_op jit(solution)/shard_map/ppermute | solution.py:356
  518.9 6.6 %collective-permute-start.30 = (bf16[2,2,32,1024]{3,2,1,0:T(8,128)(2,1)S(1)}, bf16[2,2,32,1024]{3,2,1,0:T(8,128)(2,1)S(1)}, u32[]{:S(2)}, u32[]{:S(2)}) collective-permute-start(bf16[2,2,32,1024]{3,2,1,0:T(8,128)(2,1)S(1)} %copy.333), channel_id=1, source_target_pairs={{0,8},{1,9},{2,10},{3,11},{4,12},{5,13},{6,14},{7,15},{8,0},{9,1},... | collective-permute-start | bytes 786440 | tf_op jit(solution)/shard_map/ppermute | solution.py:356
  521.2 7.4 %collective-permute-start.31 = (bf16[2,2,32,1024]{3,2,1,0:T(8,128)(2,1)S(1)}, bf16[2,2,32,1024]{3,2,1,0:T(8,128)(2,1)S(1)}, u32[]{:S(2)}, u32[]{:S(2)}) collective-permute-start(bf16[2,2,32,1024]{3,2,1,0:T(8,128)(2,1)S(1)} %copy.334), channel_id=1, source_target_pairs={{0,2},{1,3},{2,0},{3,1},{4,6},{5,7},{6,4},{7,5},{8,10},{9,11},{10,... | collective-permute-start | bytes 786440 | tf_op jit(solution)/shard_map/ppermute | solution.py:356
  521.5 9.8 %collective-permute-start.32 = (bf16[2,32,2048]{2,1,0:T(8,128)(2,1)S(1)}, bf16[2,32,2048]{2,1,0:T(8,128)(2,1)S(1)}, u32[]{:S(2)}, u32[]{:S(2)}) collective-permute-start(bf16[2,32,2048]{2,1,0:T(8,128)(2,1)S(1)} %get-tuple-element.193), channel_id=1, source_target_pairs={{0,2},{1,3},{2,0},{3,1},{4,6},{5,7},{6,4},{7,5},{8,10},{9,11},{10,... | collective-permute-start | bytes 786440 | tf_op jit(solution)/shard_map/ppermute | solution.py:356
  531.4 7.5 %collective-permute-start.33 = (bf16[2,32,1024]{2,1,0:T(8,128)(2,1)S(1)}, bf16[2,32,1024]{2,1,0:T(8,128)(2,1)S(1)}, u32[]{:S(2)}, u32[]{:S(2)}) collective-permute-start(bf16[2,32,1024]{2,1,0:T(8,128)(2,1)S(1)} %get-tuple-element.195), channel_id=1, source_target_pairs={{0,8},{1,9},{2,10},{3,11},{4,12},{5,13},{6,14},{7,15},{8,0},{9,1},... | collective-permute-start | bytes 393224 | tf_op jit(solution)/shard_map/ppermute | solution.py:356
  533.3 5.6 collective-permute-start.34
  536.3 5.0 collective-permute-start.35
  538.0 9.6 %collective-permute-start.41 = (bf16[32,2048]{1,0:T(8,128)(2,1)S(1)}, bf16[32,2048]{1,0:T(8,128)(2,1)S(1)}, u32[]{:S(2)}, u32[]{:S(2)}) collective-permute-start(bf16[32,2048]{1,0:T(8,128)(2,1)S(1)} %fusion.57), channel_id=1, source_target_pairs={{0,16},{1,17},{2,18},{3,19},{4,20},{5,21},{6,22},{7,23},{8,24},{9,... | collective-permute-start | bytes 393224 | tf_op jit(solution)/shard_map/ppermute | solution.py:356
  541.3 10.0 %collective-permute-start.40 = (bf16[32,1024]{1,0:T(8,128)(2,1)S(1)}, bf16[32,1024]{1,0:T(8,128)(2,1)S(1)}, u32[]{:S(2)}, u32[]{:S(2)}) collective-permute-start(bf16[32,1024]{1,0:T(8,128)(2,1)S(1)} %fusion.70), channel_id=1, source_target_pairs={{0,16},{1,17},{2,18},{3,19},{4,20},{5,21},{6,22},{7,23},{8,24},{9,... | collective-permute-start | bytes 196616 | tf_op jit(solution)/shard_map/ppermute | solution.py:356
  548.3 5.2 collective-permute-start.39
  548.3 5.9 %collective-permute-start.38 = (bf16[32,1024]{1,0:T(8,128)(2,1)S(1)}, bf16[32,1024]{1,0:T(8,128)(2,1)S(1)}, u32[]{:S(2)}, u32[]{:S(2)}) collective-permute-start(bf16[32,1024]{1,0:T(8,128)(2,1)S(1)} %fusion.68), channel_id=1, source_target_pairs={{0,16},{1,17},{2,18},{3,19},{4,20},{5,21},{6,22},{7,23},{8,24},{9,... | collective-permute-start | bytes 196616 | tf_op jit(solution)/shard_map/ppermute | solution.py:356
  (51 other events, 531.0 us)
Sparse Core Ops, SparseCore 0:
  11.5 115.6 all-gather.2
  130.1 75.6 all-gather.4
  289.3 93.7 reduce-scatter.4
  403.9 95.4 reduce-scatter.2

commit v5 on v4

--- a/solution.py
+++ b/solution.py
@@ -626,7 +626,7 @@
     for step in range(len(small.order)):
         (d_image,) = scatter_step(late + [out_stream], d_image)
         if step == 2:
-            (pooled,) = scatter_step([small], pooled)
+            pooled, g_wdown = scatter_step([small], pooled, g_wdown)
         else:
             scatter_step([small])
     g_wqkv = jnp.concatenate([item.total() for item in late], axis=1)

time: 571 us -> 589 us (1.032)
  Pallas kernels: 145 us -> 163 us
  starting transfers between devices: 57.5 us -> 40.2 us
  waiting for transfers between devices: 106 us -> 122 us
    ppermute x42, waiting for transfers between devices: 89.9 us -> 111 us  [swap(): lax.ppermute(value, 'fsdp', [(i, i ^ 1 << bit) for i in range(count)])]
    ppermute x42, starting transfers between devices: 57.3 us -> 40.1 us  [swap(): lax.ppermute(value, 'fsdp', [(i, i ^ 1 << bit) for i in range(count)])]
    pallas_call x2, Pallas kernels: 34 us -> 46.8 us  [attention_backward(): pl.pallas_call(held_in_place(kernel, len(filled)), out_shape=tuple((jax.S...]
  transfers between devices with their start and end apart: 46 -> 46, of which waited for: 26 -> 22; matrix products, arithmetic and copies ran while one was open for 30% -> 29% of each run, Pallas kernels for 24% -> 26%
where the time goes in v5:
time: 589 us; the launch traced here: 583 us
  Pallas kernels  163 us (28%)
  waiting for transfers between devices  122 us (21%)
  matrix products  106 us (18%)
  other arithmetic  76.5 us (13%)
  local copies, waits for them, and re-layouts  60.3 us (10%)
  starting transfers between devices  40.2 us (7%)
  between operations  15.2 us (3%)
    ppermute x42, waiting for transfers between devices, swap(): lax.ppermute(value, 'fsdp', [(i, i ^ 1 << bit) for i in range(count)])  111 us
    dot_general x15, matrix products, mm(): return lax.dot_general(left, right, dims, preferred_element_type=F32)  93.1 us
    pallas_call x2, Pallas kernels, attention_backward(): pl.pallas_call(held_in_place(kernel, len(filled)), out_shape=tuple((jax.S...  46.8 us
    pallas_call x2, Pallas kernels, gelu_matmul(): pl.pallas_call(functools.partial(gelu_matmul_kernel, rows // 4, tiles), o...  43.6 us
    ppermute x42, starting transfers between devices, swap(): lax.ppermute(value, 'fsdp', [(i, i ^ 1 << bit) for i in range(count)])  40.1 us
    pallas_call x2, Pallas kernels, back_product(): pl.pallas_call(functools.partial(back_product_kernel, count), out_shape=j...  30.7 us
    pallas_call x1, Pallas kernels, attention_forward(): pl.pallas_call(functools.partial(attention_forward_kernel, slots), out_sh...  24.5 us
    pallas_call x1, Pallas kernels, slope_matmul(): pl.pallas_call(functools.partial(slope_matmul_kernel, rows // 4), out_sha...  17.4 us
  transfers between devices with their start and end apart: 46, of which 22 were waited for; matrix products, arithmetic and copies ran while one was open for 29% of the time, Pallas kernels for 26%

profile of v5, /device:TPU:0, one launch (start us, length us, event | category | flops | bytes accessed | tf_op | source)
XLA Modules:
  0.0 583.2 jit_solution(6596924383344778023)
XLA Ops:
  20.3 4.1 collective-permute-start.1
  27.3 5.2 collective-permute-done.1
  32.5 5.0 collective-permute-done
  37.6 4.2 collective-permute-done.2
  49.4 5.4 collective-permute-done.5
  55.2 12.7 %collective-permute-done.6 = bf16[2,2,32,1024]{3,2,1,0:T(8,128)(2,1)S(1)} collective-permute-done((bf16[2,2,32,1024]{3,2,1,0:T(8,128)(2,1)S(1)}, bf16[2,2,32,1024]{3,2,1,0:T(8,128)(2,1)S(1)}, u32[]{:S(2)}, u32[]{:S(2)}) %collective-permute-start.6) | collective-permute-done | bytes 262176 | tf_op jit(solution)/shard_map/ppermute | solution.py:356
  71.6 9.8 %collective-permute-done.9 = bf16[2,2,2,32,1024]{4,3,2,1,0:T(8,128)(2,1)} collective-permute-done((bf16[2,2,2,32,1024]{4,3,2,1,0:T(8,128)(2,1)S(1)}, bf16[2,2,2,32,1024]{4,3,2,1,0:T(8,128)(2,1)}, u32[]{:S(2)}, u32[]{:S(2)}) %collective-permute-start.9) | collective-permute-done | bytes 524320 | tf_op jit(solution)/shard_map/ppermute | solution.py:356
  82.8 4.1 collective-permute-done.10
  118.1 10.0 %add_convert_fusion.q_ref.k_ref.v_ref.refs_0_.refs_1_.refs_2_.refs_3_.refs_4_.refs_5_ = bf16[1152,3072]{1,0:T(8,128)(2,1)} fusion(bf16[1152,1024]{1,0:T(8,128)(2,1)S(1)} %fusion.13, f32[3072]{0:T(1024)S(1)} %bitcast.415, bf16[1024,1024]{1,0:T(8,128)(2,1)S(1)} %get-tuple-element.411.refs_5_, bf16[1024,1024]{1,0:T(8,128)(2,1)S(1)} %get-tuple-element.410.refs_4_, ...), kind=kOutput, calls=%fused_computation | convolution fusion | flops 7273709568 | bytes 15740928 | tf_op jit(solution)/shard_map/dot_general | solution.py:28
  128.1 24.5 %attention_forward.1 = (bf16[1152,1024]{1,0:T(8,128)(2,1)}, f32[8,4,576]{2,1,0:T(4,128)}) custom-call(s32[2]{0:T(128)} %bitcast.416, bf16[1152,3072]{1,0:T(8,128)(2,1)} %add_convert_fusion.q_ref.k_ref.v_ref.refs_0_.refs_1_.refs_2_.refs_3_.refs_4_.refs_5_, bf16[1152,3072]{1,0:T(8,128)(2,1)} %add_convert_fusion.q_ref.k_ref.v_ref.refs_0_.refs_1_.refs_2_.refs_3_.refs_4_.refs_5_, ...), custom_call_target="tpu_custom_call" | custom-call | flops 1024 | bytes 1024 | tf_op jit(solution)/shard_map/attention_forward/pallas_call | solution.py:300
  153.4 5.5 fusion.96
  163.4 32.5 %gelu_matmul.2 = (bf16[1152,4096]{1,0:T(8,128)(2,1)}, bf16[1152,4096]{1,0:T(8,128)(2,1)}) custom-call(bf16[1152,1024]{1,0:T(8,128)(2,1)} %add_convert_fusion.4.x_ref, f32[1,4096]{1,0:T(1,128)} %reshape.572.b_ref, bf16[1024,6144]{1,0:T(8,128)(2,1)} %all-gather.3.cloned.1.call-done.refs_0_.refs_1_), custom_call_target="tpu_custom_call" | custom-call | flops 1024 | bytes 1024 | tf_op jit(solution)/shard_map/gelu_matmul/pallas_call | solution.py:125
  196.0 9.6 %all-gather.5.cloned.1.call-done.w_ref = bf16[4096,1024]{1,0:T(8,128)(2,1)} async-done(((bf16[128,1024]{1,0:T(8,128)(2,1)}), bf16[4096,1024]{1,0:T(8,128)(2,1)}) %all-gather.5.cloned.1.call-update) | async-done | bytes 8388624 | tf_op jit(solution)/shard_map/all_gather | solution.py:343
  205.5 15.3 %fusion.97 = (f32[1152]{0:T(1024)S(1)}, f32[1152,1024]{1,0:T(8,128)S(1)}) fusion(f32[1024]{0:T(1024)S(1)} %bitcast.420, f32[1152,1024]{1,0:T(8,128)} %copy-done.3, bf16[1152,4096]{1,0:T(8,128)(2,1)} %get-tuple-element.130, bf16[4096,1024]{1,0:T(8,128)(2,1)} %all-gather.5.cloned.1.call-done.w_ref), kind=kOutput, calls=%fused_computation.266 | convolution fusion | flops 9667214336 | bytes 27271680 | tf_op jit(solution)/shard_map/dot_general | solution.py:28
  221.5 4.1 fusion.76
  225.8 4.6 add_convert_fusion.3.x_ref
  230.3 11.1 %gelu_matmul.3 = (bf16[1152,1024]{1,0:T(8,128)(2,1)}, bf16[1152,1024]{1,0:T(8,128)(2,1)}) custom-call(bf16[1152,1024]{1,0:T(8,128)(2,1)} %add_convert_fusion.3.x_ref, f32[1,1024]{1,0:T(1,128)} %get-tuple-element.396.b_ref, bf16[1024,6144]{1,0:T(8,128)(2,1)} %all-gather.3.cloned.1.call-done.refs_0_.refs_1_), custom_call_target="tpu_custom_call" | custom-call | flops 1024 | bytes 1024 | tf_op jit(solution)/shard_map/gelu_matmul/pallas_call | solution.py:125
  244.1 3.9 fusion.78
  249.7 6.1 %multiply_reduce_fusion = (bf16[1024]{0:T(1024)(128)(2,1)S(1)}, f32[1152]{0:T(1024)S(1)}, f32[1152]{0:T(1024)S(1)}, bf16[1024]{0:T(1024)(128)(2,1)S(1)}, f32[1152,1024]{1,0:T(8,128)S(1)}) fusion(f32[1152,1024]{1,0:T(8,128)S(1)} %bitcast.380, f32[1152]{0:T(1024)S(1)} %add_rsqrt_fusion, f32[1152]{0:T(1024)S(1)} %broadcast_multiply_fusion.7, ...), kind=kOutput, calls=%fused_computation.31 | convolution fusion | flops 2426531840 | bytes 13920256 | tf_op jit(solution)/shard_map/dot_general | solution.py:28
  255.8 3.4 fusion.91
  259.3 13.3 %convolution_convert_fusion = bf16[4096,1024]{1,0:T(8,128)(2,1)} fusion(bf16[1152,4096]{1,0:T(8,128)(2,1)S(1)} %bitcast.434, bf16[1152,1024]{1,0:T(8,128)(2,1)S(1)} %get-tuple-element.139.x_ref), kind=kOutput, calls=%fused_computation.3 | convolution fusion | flops 9667870720 | bytes 20185088 | tf_op jit(solution)/shard_map/dot_general | solution.py:28
  272.6 4.9 dynamic-slice_bitcast_fusion.2
  277.9 4.2 convolution_convert_fusion.7
  284.7 4.2 add_convert_fusion.2
  289.0 17.4 %slope_matmul.1 = (bf16[1152,4096]{1,0:T(8,128)(2,1)}, f32[1,4096]{1,0:T(1,128)}) custom-call(bf16[1152,1024]{1,0:T(8,128)(2,1)} %copy-done.15, bf16[4096,1024]{1,0:T(8,128)(2,1)} %all-gather.5.cloned.1.call-done.w_ref, bf16[1152,4096]{1,0:T(8,128)(2,1)} %get-tuple-element.140.slope_ref), custom_call_target="tpu_custom_call" | custom-call | flops 1024 | bytes 1024 | tf_op jit(solution)/shard_map/slope_matmul/pallas_call | solution.py:166
  306.4 13.7 %convolution_convert_fusion.1 = bf16[1024,4096]{1,0:T(8,128)(2,1)S(1)} fusion(bf16[1152,1024]{1,0:T(8,128)(2,1)S(1)} %copy-done.16, bf16[1152,4096]{1,0:T(8,128)(2,1)} %get-tuple-element.142.refs_0_), kind=kOutput, calls=%fused_computation.4 | convolution fusion | flops 9667870720 | bytes 20185088 | tf_op jit(solution)/shard_map/dot_general | solution.py:28
  320.1 3.9 dynamic-slice_bitcast_fusion
  324.3 16.9 %back_product.2 = f32[1152,1024]{1,0:T(8,128)} custom-call(bf16[1152,4096]{1,0:T(8,128)(2,1)} %get-tuple-element.142.refs_0_, bf16[1024,6144]{1,0:T(8,128)(2,1)} %all-gather.3.cloned.1.call-done.refs_0_.refs_1_), custom_call_target="tpu_custom_call" | custom-call | flops 1024 | bytes 1024 | tf_op jit(solution)/shard_map/back_product/pallas_call | solution.py:150
  341.3 5.6 multiply_reduce_fusion.1
  347.0 4.8 convert_reduce_fusion.4
  357.3 5.8 convolution_convert_fusion.2.refs_4_.refs_7_
  366.9 23.5 %attention_backward.2 = (bf16[1152,1024]{1,0:T(8,128)(2,1)}, bf16[1152,1024]{1,0:T(8,128)(2,1)}, bf16[1152,1024]{1,0:T(8,128)(2,1)}) custom-call(s32[2]{0:T(128)} %bitcast.417, bf16[1152,3072]{1,0:T(8,128)(2,1)} %add_convert_fusion.q_ref.k_ref.v_ref.refs_0_.refs_1_.refs_2_.refs_3_.refs_4_.refs_5_, ...), custom_call_target="tpu_custom_call" | custom-call | flops 1024 | bytes 1024 | tf_op jit(solution)/shard_map/attention_backward/pallas_call | solution.py:324
  397.8 5.7 add_convert_fusion.1
  403.5 23.2 %attention_backward.3 = (bf16[1152,1024]{1,0:T(8,128)(2,1)}, bf16[1152,1024]{1,0:T(8,128)(2,1)}, bf16[1152,1024]{1,0:T(8,128)(2,1)}) custom-call(s32[2]{0:T(128)} %bitcast.418, bf16[1152,1024]{1,0:T(8,128)(2,1)} %get-tuple-element.158.refs_0_, ...), custom_call_target="tpu_custom_call", output_to_operand_aliasing={{0}: (1, {}), {1}: (2, {}), {2}: (3, {})} | custom-call | flops 1024 | bytes 1024 | tf_op jit(solution)/shard_map/attention_backward/pallas_call | solution.py:324
  428.4 5.0 convolution_convert_fusion.5
  437.4 3.3 convolution_convert_fusion.3
  443.3 24.3 %collective-permute-done.28 = bf16[2,2,32,2048]{3,2,1,0:T(8,128)(2,1)S(1)} collective-permute-done((bf16[2,2,32,2048]{3,2,1,0:T(8,128)(2,1)S(1)}, bf16[2,2,32,2048]{3,2,1,0:T(8,128)(2,1)S(1)}, u32[]{:S(2)}, u32[]{:S(2)}) %collective-permute-start.28) | collective-permute-done | bytes 524320 | tf_op jit(solution)/shard_map/ppermute | solution.py:356
  472.3 13.8 %back_product.3 = f32[1152,1024]{1,0:T(8,128)} custom-call(bf16[1152,1024]{1,0:T(8,128)(2,1)} %get-tuple-element.179.refs_0_, bf16[1152,1024]{1,0:T(8,128)(2,1)} %get-tuple-element.180.refs_1_, bf16[1152,1024]{1,0:T(8,128)(2,1)} %get-tuple-element.181.refs_2_, bf16[1024,1024]{1,0:T(8,128)(2,1)} %copy-done.18, bf16[1024,1024]{1,0:T(8,128)(2,1)} %copy-done.19, ...), custom_call_target="tpu_custom_call" | custom-call | flops 1024 | bytes 1024 | tf_op jit(solution)/shard_map/back_product/pallas_call | solution.py:150
  486.1 4.2 fusion.15
  499.6 6.2 %fusion.18 = f32[1152,1024]{1,0:T(8,128)} fusion(f32[1152,1024]{1,0:T(8,128)} %copy-done.9, bf16[2,1,576,1024]{3,2,1,0:T(8,128)(2,1)S(1)} %copy-done.5, f32[1152,1024]{1,0:T(8,128)} %back_product.3, f32[1152]{0:T(1024)S(1)} %broadcast_multiply_fusion.1, f32[1152]{0:T(1024)S(1)} %broadcast_multiply_fusion.2, f32[1024]{0:T(1024)S(1)} %bitcast.403, ...), kind=kLoop, calls=%fused_computation.29 | loop fusion | flops 10616832 | bytes 16537600 | tf_op jit(solution)/shard_map/add | solution.py:623
  505.9 4.7 collective-permute-done.25
  517.0 6.5 %collective-permute-done.23 = bf16[2,2,2,32,128]{3,4,0,2,1:T(8,128)(2,1)S(1)} collective-permute-done((bf16[2,2,2,32,128]{3,4,0,2,1:T(8,128)(2,1)S(1)}, bf16[2,2,2,32,128]{3,4,0,2,1:T(8,128)(2,1)S(1)}, u32[]{:S(2)}, u32[]{:S(2)}) %collective-permute-start.23) | collective-permute-done | bytes 65568 | tf_op jit(solution)/shard_map/ppermute | solution.py:356
  527.3 4.3 collective-permute-done.32
  532.0 5.3 fusion.80
  539.6 8.1 %collective-permute-start.41 = (bf16[32,2048]{1,0:T(8,128)(2,1)S(1)}, bf16[32,2048]{1,0:T(8,128)(2,1)S(1)}, u32[]{:S(2)}, u32[]{:S(2)}) collective-permute-start(bf16[32,2048]{1,0:T(8,128)(2,1)S(1)} %fusion.57), channel_id=1, source_target_pairs={{0,16},{1,17},{2,18},{3,19},{4,20},{5,21},{6,22},{7,23},{8,24},{9,... | collective-permute-start | bytes 393224 | tf_op jit(solution)/shard_map/ppermute | solution.py:356
  547.8 4.3 collective-permute-start.40
  556.1 5.1 collective-permute-done.39
  568.3 3.9 collective-permute-done.37
  (348 shorter events, 140.5 us)
Async XLA Ops:
  7.2 214.3 %copy-start = (f32[2,1,8,1024]{3,2,1,0:T(8,128)S(1)}, f32[2,1,8,1024]{3,2,1,0:T(8,128)}, u32[]{:S(2)}) copy-start(f32[2,1,8,1024]{3,2,1,0:T(8,128)} %param.22) | copy-start | bytes 196612
  7.2 63.6 %copy-start.4 = (bf16[2,1,576,1024]{3,2,1,0:T(8,128)(2,1)S(1)}, bf16[2,1,576,1024]{3,2,1,0:T(8,128)(2,1)}, u32[]{:S(2)}) copy-start(bf16[2,1,576,1024]{3,2,1,0:T(8,128)(2,1)} %param.20) | copy-start | bytes 7077892
  7.2 146.2 %all-gather.3.cloned.1.call-start = ((), (), s32[]{:S(2)}) async-start(), calls=%async_computation.2 | async-start | bytes 12976128 | tf_op jit(solution)/shard_map/all_gather | solution.py:343
  9.2 196.3 %all-gather.5.cloned.1.call-start = ((), (), s32[]{:S(2)}) async-start(), calls=%async_computation.3 | async-start | bytes 8650752 | tf_op jit(solution)/shard_map/all_gather | solution.py:343
  10.0 551.3 %reduce-scatter.3.cloned.1.call-start = ((), (), s32[]{:S(2)}) async-start(), calls=%async_computation.4 | async-start | bytes 4456448 | tf_op jit(solution)/shard_map/reduce_scatter | solution.py:460
  20.3 12.2 %collective-permute-start.1 = (bf16[32,1024]{1,0:T(8,128)(2,1)S(1)}, bf16[32,1024]{1,0:T(8,128)(2,1)S(1)}, u32[]{:S(2)}, u32[]{:S(2)}) collective-permute-start(bf16[32,1024]{1,0:T(8,128)(2,1)S(1)} %get-tuple-element.115), channel_id=1, source_target_pairs={{0,16},{1,17},{2,18},{3,19},{4,20},{5,21},{6,22},{7,23},{8,24},{9,... | collective-permute-start | bytes 196616 | tf_op jit(solution)/shard_map/ppermute | solution.py:356
  24.4 13.1 %collective-permute-start = (bf16[32,1024]{1,0:T(8,128)(2,1)S(1)}, bf16[32,1024]{1,0:T(8,128)(2,1)S(1)}, u32[]{:S(2)}, u32[]{:S(2)}) collective-permute-start(bf16[32,1024]{1,0:T(8,128)(2,1)S(1)} %get-tuple-element.114), channel_id=1, source_target_pairs={{0,16},{1,17},{2,18},{3,19},{4,20},{5,21},{6,22},{7,23},{8,24},{9,... | collective-permute-start | bytes 196616 | tf_op jit(solution)/shard_map/ppermute | solution.py:356
  24.5 17.4 %collective-permute-start.2 = (bf16[32,1152]{1,0:T(8,128)(2,1)S(1)}, bf16[32,1152]{1,0:T(8,128)(2,1)S(1)}, u32[]{:S(2)}, u32[]{:S(2)}) collective-permute-start(bf16[32,1152]{1,0:T(8,128)(2,1)S(1)} %concatenate.34), channel_id=1, source_target_pairs={{0,16},{1,17},{2,18},{3,19},{4,20},{5,21},{6,22},{7,23},{8,24},{9,... | collective-permute-start | bytes 221192 | tf_op jit(solution)/shard_map/ppermute | solution.py:356
  41.9 5.3 collective-permute-start.3
  44.3 5.0 collective-permute-start.4
  45.9 9.0 %collective-permute-start.5 = (bf16[2,32,1152]{2,1,0:T(8,128)(2,1)S(1)}, bf16[2,32,1152]{2,1,0:T(8,128)(2,1)S(1)}, u32[]{:S(2)}, u32[]{:S(2)}) collective-permute-start(bf16[2,32,1152]{2,1,0:T(8,128)(2,1)S(1)} %broadcast_select_fusion.10), channel_id=1, source_target_pairs={{0,8},{1,9},{2,10},{3,11},{4,12},{5,13},{6,14},{7,15},{8,0},{9,1},... | collective-permute-start | bytes 442376 | tf_op jit(solution)/shard_map/ppermute | solution.py:356
  55.0 12.9 %collective-permute-start.6 = (bf16[2,2,32,1024]{3,2,1,0:T(8,128)(2,1)S(1)}, bf16[2,2,32,1024]{3,2,1,0:T(8,128)(2,1)S(1)}, u32[]{:S(2)}, u32[]{:S(2)}) collective-permute-start(bf16[2,2,32,1024]{3,2,1,0:T(8,128)(2,1)S(1)} %broadcast_select_fusion.8), channel_id=1, source_target_pairs={{0,8},{1,9},{2,10},{3,11},{4,12},{5,13},{6,14},{7,15},{8,0},{9,1},... | collective-permute-start | bytes 786440 | tf_op jit(solution)/shard_map/ppermute | solution.py:356
  55.0 13.0 %collective-permute-start.7 = (bf16[2,2,32,1024]{3,2,1,0:T(8,128)(2,1)S(1)}, bf16[2,2,32,1024]{3,2,1,0:T(8,128)(2,1)S(1)}, u32[]{:S(2)}, u32[]{:S(2)}) collective-permute-start(bf16[2,2,32,1024]{3,2,1,0:T(8,128)(2,1)S(1)} %broadcast_select_fusion.7), channel_id=1, source_target_pairs={{0,2},{1,3},{2,0},{3,1},{4,6},{5,7},{6,4},{7,5},{8,10},{9,11},{10,... | collective-permute-start | bytes 786440 | tf_op jit(solution)/shard_map/ppermute | solution.py:356
  55.1 13.9 %collective-permute-start.8 = (bf16[2,2,32,1152]{3,2,1,0:T(8,128)(2,1)S(1)}, bf16[2,2,32,1152]{3,2,1,0:T(8,128)(2,1)S(1)}, u32[]{:S(2)}, u32[]{:S(2)}) collective-permute-start(bf16[2,2,32,1152]{3,2,1,0:T(8,128)(2,1)S(1)} %broadcast_select_fusion.6), channel_id=1, source_target_pairs={{0,4},{1,5},{2,6},{3,7},{4,0},{5,1},{6,2},{7,3},{8,12},{9,13},{10,... | collective-permute-start | bytes 884744 | tf_op jit(solution)/shard_map/ppermute | solution.py:356
  69.9 11.5 %collective-permute-start.9 = (bf16[2,2,2,32,1024]{4,3,2,1,0:T(8,128)(2,1)S(1)}, bf16[2,2,2,32,1024]{4,3,2,1,0:T(8,128)(2,1)}, u32[]{:S(2)}, u32[]{:S(2)}) collective-permute-start(bf16[2,2,2,32,1024]{4,3,2,1,0:T(8,128)(2,1)S(1)} %broadcast_select_fusion.5), channel_id=1, source_target_pairs={{0,4},{1,5},{2,6},{3,7},{4,0},{5,1},{6,2},{7,3},{8,12},{9,13},{10,... | collective-permute-start | bytes 1572872 | tf_op jit(solution)/shard_map/ppermute | solution.py:356
  69.9 16.9 %collective-permute-start.10 = (bf16[2,2,2,32,1024]{4,3,2,1,0:T(8,128)(2,1)}, bf16[2,2,2,32,1024]{4,3,2,1,0:T(8,128)(2,1)}, u32[]{:S(2)}, u32[]{:S(2)}) collective-permute-start(bf16[2,2,2,32,1024]{4,3,2,1,0:T(8,128)(2,1)} %broadcast_select_fusion.4), channel_id=1, source_target_pairs={{0,8},{1,9},{2,10},{3,11},{4,12},{5,13},{6,14},{7,15},{8,0},{9,1},... | collective-permute-start | bytes 1572872 | tf_op jit(solution)/shard_map/ppermute | solution.py:356
  71.2 18.0 %collective-permute-start.11 = (bf16[2,2,2,32,1152]{4,3,2,1,0:T(8,128)(2,1)}, bf16[2,2,2,32,1152]{4,3,2,1,0:T(8,128)(2,1)}, u32[]{:S(2)}, u32[]{:S(2)}) collective-permute-start(bf16[2,2,2,32,1152]{4,3,2,1,0:T(8,128)(2,1)} %broadcast_select_fusion.3), channel_id=1, source_target_pairs={{0,2},{1,3},{2,0},{3,1},{4,6},{5,7},{6,4},{7,5},{8,10},{9,11},{10,... | collective-permute-start | bytes 1769480 | tf_op jit(solution)/shard_map/ppermute | solution.py:356
  91.6 8.7 %collective-permute-start.12 = (bf16[2,2,2,2,32,1152]{5,4,3,2,1,0:T(8,128)(2,1)}, bf16[2,2,2,2,32,1152]{5,4,3,2,1,0:T(8,128)(2,1)}, u32[]{:S(2)}, u32[]{:S(2)}) collective-permute-start(bf16[2,2,2,2,32,1152]{5,4,3,2,1,0:T(8,128)(2,1)} %broadcast_select_fusion), channel_id=1, source_target_pairs={{0,1},{1,0},{2,3},{3,2},{4,5},{5,4},{6,7},{7,6},{8,9},{9,8},{10,11... | collective-permute-start | bytes 3538952 | tf_op jit(solution)/shard_map/ppermute | solution.py:356
  92.5 19.3 %collective-permute-start.13 = (bf16[2,2,2,2,32,1024]{5,4,3,2,1,0:T(8,128)(2,1)S(1)}, bf16[2,2,2,2,32,1024]{5,4,3,2,1,0:T(8,128)(2,1)}, u32[]{:S(2)}, u32[]{:S(2)}) collective-permute-start(bf16[2,2,2,2,32,1024]{5,4,3,2,1,0:T(8,128)(2,1)S(1)} %broadcast_select_fusion.2), channel_id=1, source_target_pairs={{0,1},{1,0},{2,3},{3,2},{4,5},{5,4},{6,7},{7,6},{8,9},{9,8},{10,11... | collective-permute-start | bytes 3145736 | tf_op jit(solution)/shard_map/ppermute | solution.py:356
  93.0 18.8 %collective-permute-start.14 = (bf16[2,2,2,2,32,1024]{5,4,3,2,1,0:T(8,128)(2,1)}, bf16[2,2,2,2,32,1024]{5,4,3,2,1,0:T(8,128)(2,1)}, u32[]{:S(2)}, u32[]{:S(2)}) collective-permute-start(bf16[2,2,2,2,32,1024]{5,4,3,2,1,0:T(8,128)(2,1)} %broadcast_select_fusion.1), channel_id=1, source_target_pairs={{0,1},{1,0},{2,3},{3,2},{4,5},{5,4},{6,7},{7,6},{8,9},{9,8},{10,11... | collective-permute-start | bytes 3145736 | tf_op jit(solution)/shard_map/ppermute | solution.py:356
  277.5 7.2 %collective-permute-start.15 = (bf16[16,128,1024]{2,1,0:T(8,128)(2,1)S(1)}, bf16[16,128,1024]{2,1,0:T(8,128)(2,1)S(1)}, u32[]{:S(2)}, u32[]{:S(2)}) collective-permute-start(bf16[16,128,1024]{2,1,0:T(8,128)(2,1)S(1)} %get-tuple-element.133), channel_id=1, source_target_pairs={{0,1},{1,0},{2,3},{3,2},{4,5},{5,4},{6,7},{7,6},{8,9},{9,8},{10,11... | collective-permute-start | bytes 12582920 | tf_op jit(solution)/shard_map/ppermute | solution.py:356
  288.9 285.7 %reduce-scatter.5.cloned.1.call-start = ((), (), s32[]{:S(2)}) async-start(), calls=%async_computation.5 | async-start | bytes 4456448 | tf_op jit(solution)/shard_map/reduce_scatter | solution.py:460
  324.0 73.8 %collective-permute-start.17 = (bf16[16,32,4096]{2,1,0:T(8,128)(2,1)}, bf16[16,32,4096]{2,1,0:T(8,128)(2,1)}, u32[]{:S(2)}, u32[]{:S(2)}) collective-permute-start(bf16[16,32,4096]{2,1,0:T(8,128)(2,1)} %get-tuple-element.145), channel_id=1, source_target_pairs={{0,1},{1,0},{2,3},{3,2},{4,5},{5,4},{6,7},{7,6},{8,9},{9,8},{10,11... | collective-permute-start | bytes 12582920 | tf_op jit(solution)/shard_map/ppermute | solution.py:356
  363.1 31.4 %collective-permute-start.16 = (bf16[2,2,2,2,32,2048]{5,4,0,3,1,2:T(8,128)(2,1)}, bf16[2,2,2,2,32,2048]{5,4,0,3,1,2:T(8,128)(2,1)}, u32[]{:S(2)}, u32[]{:S(2)}) collective-permute-start(bf16[2,2,2,2,32,2048]{5,4,0,3,1,2:T(8,128)(2,1)} %copy_bitcast_fusion), channel_id=1, source_target_pairs={{0,1},{1,0},{2,3},{3,2},{4,5},{5,4},{6,7},{7,6},{8,9},{9,8},{10,11... | collective-permute-start | bytes 6291464 | tf_op jit(solution)/shard_map/ppermute | solution.py:356
  397.8 29.0 %collective-permute-start.18 = (bf16[2,2,2,32,2048]{4,3,0,2,1:T(8,128)(2,1)}, bf16[2,2,2,32,2048]{4,3,0,2,1:T(8,128)(2,1)}, u32[]{:S(2)}, u32[]{:S(2)}) collective-permute-start(bf16[2,2,2,32,2048]{4,3,0,2,1:T(8,128)(2,1)} %get-tuple-element.152), channel_id=1, source_target_pairs={{0,4},{1,5},{2,6},{3,7},{4,0},{5,1},{6,2},{7,3},{8,12},{9,13},{10,... | collective-permute-start | bytes 3145736 | tf_op jit(solution)/shard_map/ppermute | solution.py:356
  433.5 35.0 %collective-permute-start.19 = (bf16[2,2,2,2,32,1024]{5,4,0,2,1,3:T(8,128)(2,1)S(1)}, bf16[2,2,2,2,32,1024]{5,4,0,2,1,3:T(8,128)(2,1)S(1)}, u32[]{:S(2)}, u32[]{:S(2)}) collective-permute-start(bf16[2,2,2,2,32,1024]{5,4,0,2,1,3:T(8,128)(2,1)S(1)} %copy_bitcast_fusion.5), channel_id=1, source_target_pairs={{0,1},{1,0},{2,3},{3,2},{4,5},{5,4},{6,7},{7,6},{8,9},{9,8},{10,11... | collective-permute-start | bytes 3145736 | tf_op jit(solution)/shard_map/ppermute | solution.py:356
  436.9 32.8 %collective-permute-start.20 = (bf16[2,2,2,2,32,1024]{5,4,0,3,1,2:T(8,128)(2,1)S(1)}, bf16[2,2,2,2,32,1024]{5,4,0,3,1,2:T(8,128)(2,1)S(1)}, u32[]{:S(2)}, u32[]{:S(2)}) collective-permute-start(bf16[2,2,2,2,32,1024]{5,4,0,3,1,2:T(8,128)(2,1)S(1)} %copy_bitcast_fusion.4), channel_id=1, source_target_pairs={{0,1},{1,0},{2,3},{3,2},{4,5},{5,4},{6,7},{7,6},{8,9},{9,8},{10,11... | collective-permute-start | bytes 3145736 | tf_op jit(solution)/shard_map/ppermute | solution.py:356
  440.9 30.1 %collective-permute-start.21 = (bf16[2,2,2,2,32,1024]{5,4,0,3,2,1:T(8,128)(2,1)S(1)}, bf16[2,2,2,2,32,1024]{5,4,0,3,2,1:T(8,128)(2,1)S(1)}, u32[]{:S(2)}, u32[]{:S(2)}) collective-permute-start(bf16[2,2,2,2,32,1024]{5,4,0,3,2,1:T(8,128)(2,1)S(1)} %copy_bitcast_fusion.3), channel_id=1, source_target_pairs={{0,1},{1,0},{2,3},{3,2},{4,5},{5,4},{6,7},{7,6},{8,9},{9,8},{10,11... | collective-permute-start | bytes 3145736 | tf_op jit(solution)/shard_map/ppermute | solution.py:356
  442.9 24.7 %collective-permute-start.28 = (bf16[2,2,32,2048]{3,2,1,0:T(8,128)(2,1)S(1)}, bf16[2,2,32,2048]{3,2,1,0:T(8,128)(2,1)S(1)}, u32[]{:S(2)}, u32[]{:S(2)}) collective-permute-start(bf16[2,2,32,2048]{3,2,1,0:T(8,128)(2,1)S(1)} %copy.330), channel_id=1, source_target_pairs={{0,8},{1,9},{2,10},{3,11},{4,12},{5,13},{6,14},{7,15},{8,0},{9,1},... | collective-permute-start | bytes 1572872 | tf_op jit(solution)/shard_map/ppermute | solution.py:356
  496.0 18.1 %collective-permute-start.22 = (bf16[2,2,2,2,32,128]{4,5,0,3,2,1:T(8,128)(2,1)S(1)}, bf16[2,2,2,2,32,128]{4,5,0,3,2,1:T(8,128)(2,1)S(1)}, u32[]{:S(2)}, u32[]{:S(2)}) collective-permute-start(bf16[2,2,2,2,32,128]{4,5,0,3,2,1:T(8,128)(2,1)S(1)} %dynamic-slice_bitcast_fusion.4), channel_id=1, source_target_pairs={{0,1},{1,0},{2,3},{3,2},{4,5},{5,4},{6,7},{7,6},{8,9},{9,8},{10,11... | collective-permute-start | bytes 393224 | tf_op jit(solution)/shard_map/ppermute | solution.py:356
  496.1 14.6 %collective-permute-start.25 = (bf16[2,2,2,32,1024]{4,3,0,2,1:T(8,128)(2,1)}, bf16[2,2,2,32,1024]{4,3,0,2,1:T(8,128)(2,1)S(1)}, u32[]{:S(2)}, u32[]{:S(2)}) collective-permute-start(bf16[2,2,2,32,1024]{4,3,0,2,1:T(8,128)(2,1)} %get-tuple-element.187), channel_id=1, source_target_pairs={{0,2},{1,3},{2,0},{3,1},{4,6},{5,7},{6,4},{7,5},{8,10},{9,11},{10,... | collective-permute-start | bytes 1572872 | tf_op jit(solution)/shard_map/ppermute | solution.py:356
  496.1 15.6 %collective-permute-start.26 = (bf16[2,2,2,32,1024]{4,3,0,2,1:T(8,128)(2,1)}, bf16[2,2,2,32,1024]{4,3,0,2,1:T(8,128)(2,1)S(1)}, u32[]{:S(2)}, u32[]{:S(2)}) collective-permute-start(bf16[2,2,2,32,1024]{4,3,0,2,1:T(8,128)(2,1)} %get-tuple-element.188), channel_id=1, source_target_pairs={{0,4},{1,5},{2,6},{3,7},{4,0},{5,1},{6,2},{7,3},{8,12},{9,13},{10,... | collective-permute-start | bytes 1572872 | tf_op jit(solution)/shard_map/ppermute | solution.py:356
  499.3 13.9 %collective-permute-start.27 = (bf16[2,2,2,32,1024]{4,3,0,2,1:T(8,128)(2,1)}, bf16[2,2,2,32,1024]{4,3,0,2,1:T(8,128)(2,1)S(1)}, u32[]{:S(2)}, u32[]{:S(2)}) collective-permute-start(bf16[2,2,2,32,1024]{4,3,0,2,1:T(8,128)(2,1)} %get-tuple-element.189), channel_id=1, source_target_pairs={{0,8},{1,9},{2,10},{3,11},{4,12},{5,13},{6,14},{7,15},{8,0},{9,1},... | collective-permute-start | bytes 1572872 | tf_op jit(solution)/shard_map/ppermute | solution.py:356
  513.5 12.2 %collective-permute-start.29 = (bf16[2,2,32,1024]{3,2,1,0:T(8,128)(2,1)S(1)}, bf16[2,2,32,1024]{3,2,1,0:T(8,128)(2,1)S(1)}, u32[]{:S(2)}, u32[]{:S(2)}) collective-permute-start(bf16[2,2,32,1024]{3,2,1,0:T(8,128)(2,1)S(1)} %copy.331), channel_id=1, source_target_pairs={{0,4},{1,5},{2,6},{3,7},{4,0},{5,1},{6,2},{7,3},{8,12},{9,13},{10,... | collective-permute-start | bytes 786440 | tf_op jit(solution)/shard_map/ppermute | solution.py:356
  514.2 9.3 %collective-permute-start.23 = (bf16[2,2,2,32,128]{3,4,0,2,1:T(8,128)(2,1)S(1)}, bf16[2,2,2,32,128]{3,4,0,2,1:T(8,128)(2,1)S(1)}, u32[]{:S(2)}, u32[]{:S(2)}) collective-permute-start(bf16[2,2,2,32,128]{3,4,0,2,1:T(8,128)(2,1)S(1)} %get-tuple-element.357), channel_id=1, source_target_pairs={{0,8},{1,9},{2,10},{3,11},{4,12},{5,13},{6,14},{7,15},{8,0},{9,1},... | collective-permute-start | bytes 196616 | tf_op jit(solution)/shard_map/ppermute | solution.py:356
  514.6 12.6 %collective-permute-start.30 = (bf16[2,2,32,1024]{3,2,1,0:T(8,128)(2,1)S(1)}, bf16[2,2,32,1024]{3,2,1,0:T(8,128)(2,1)S(1)}, u32[]{:S(2)}, u32[]{:S(2)}) collective-permute-start(bf16[2,2,32,1024]{3,2,1,0:T(8,128)(2,1)S(1)} %copy.333), channel_id=1, source_target_pairs={{0,8},{1,9},{2,10},{3,11},{4,12},{5,13},{6,14},{7,15},{8,0},{9,1},... | collective-permute-start | bytes 786440 | tf_op jit(solution)/shard_map/ppermute | solution.py:356
  516.4 10.8 %collective-permute-start.31 = (bf16[2,2,32,1024]{3,2,1,0:T(8,128)(2,1)S(1)}, bf16[2,2,32,1024]{3,2,1,0:T(8,128)(2,1)S(1)}, u32[]{:S(2)}, u32[]{:S(2)}) collective-permute-start(bf16[2,2,32,1024]{3,2,1,0:T(8,128)(2,1)S(1)} %copy.334), channel_id=1, source_target_pairs={{0,2},{1,3},{2,0},{3,1},{4,6},{5,7},{6,4},{7,5},{8,10},{9,11},{10,... | collective-permute-start | bytes 786440 | tf_op jit(solution)/shard_map/ppermute | solution.py:356
  523.6 14.6 %collective-permute-start.24 = (bf16[2,2,32,128]{2,3,1,0:T(8,128)(2,1)S(1)}, bf16[2,2,32,128]{2,3,1,0:T(8,128)(2,1)S(1)}, u32[]{:S(2)}, u32[]{:S(2)}) collective-permute-start(bf16[2,2,32,128]{2,3,1,0:T(8,128)(2,1)S(1)} %copy.325), channel_id=1, source_target_pairs={{0,2},{1,3},{2,0},{3,1},{4,6},{5,7},{6,4},{7,5},{8,10},{9,11},{10,... | collective-permute-start | bytes 98312 | tf_op jit(solution)/shard_map/ppermute | solution.py:356
  524.2 7.4 %collective-permute-start.32 = (bf16[2,32,2048]{2,1,0:T(8,128)(2,1)}, bf16[2,32,2048]{2,1,0:T(8,128)(2,1)S(1)}, u32[]{:S(2)}, u32[]{:S(2)}) collective-permute-start(bf16[2,32,2048]{2,1,0:T(8,128)(2,1)} %get-tuple-element.195), channel_id=1, source_target_pairs={{0,2},{1,3},{2,0},{3,1},{4,6},{5,7},{6,4},{7,5},{8,10},{9,11},{10,... | collective-permute-start | bytes 786440 | tf_op jit(solution)/shard_map/ppermute | solution.py:356
  531.6 16.1 %collective-permute-start.33 = (bf16[2,32,1024]{2,1,0:T(8,128)(2,1)S(1)}, bf16[2,32,1024]{2,1,0:T(8,128)(2,1)S(1)}, u32[]{:S(2)}, u32[]{:S(2)}) collective-permute-start(bf16[2,32,1024]{2,1,0:T(8,128)(2,1)S(1)} %get-tuple-element.197), channel_id=1, source_target_pairs={{0,8},{1,9},{2,10},{3,11},{4,12},{5,13},{6,14},{7,15},{8,0},{9,1},... | collective-permute-start | bytes 393224 | tf_op jit(solution)/shard_map/ppermute | solution.py:356
  537.3 10.5 %collective-permute-start.34 = (bf16[2,32,1024]{2,1,0:T(8,128)(2,1)S(1)}, bf16[2,32,1024]{2,1,0:T(8,128)(2,1)S(1)}, u32[]{:S(2)}, u32[]{:S(2)}) collective-permute-start(bf16[2,32,1024]{2,1,0:T(8,128)(2,1)S(1)} %get-tuple-element.198), channel_id=1, source_target_pairs={{0,2},{1,3},{2,0},{3,1},{4,6},{5,7},{6,4},{7,5},{8,10},{9,11},{10,... | collective-permute-start | bytes 393224 | tf_op jit(solution)/shard_map/ppermute | solution.py:356
  538.2 9.6 %collective-permute-start.35 = (bf16[2,32,1024]{2,1,0:T(8,128)(2,1)S(1)}, bf16[2,32,1024]{2,1,0:T(8,128)(2,1)S(1)}, u32[]{:S(2)}, u32[]{:S(2)}) collective-permute-start(bf16[2,32,1024]{2,1,0:T(8,128)(2,1)S(1)} %get-tuple-element.199), channel_id=1, source_target_pairs={{0,4},{1,5},{2,6},{3,7},{4,0},{5,1},{6,2},{7,3},{8,12},{9,13},{10,... | collective-permute-start | bytes 393224 | tf_op jit(solution)/shard_map/ppermute | solution.py:356
  539.6 15.7 %collective-permute-start.41 = (bf16[32,2048]{1,0:T(8,128)(2,1)S(1)}, bf16[32,2048]{1,0:T(8,128)(2,1)S(1)}, u32[]{:S(2)}, u32[]{:S(2)}) collective-permute-start(bf16[32,2048]{1,0:T(8,128)(2,1)S(1)} %fusion.57), channel_id=1, source_target_pairs={{0,16},{1,17},{2,18},{3,19},{4,20},{5,21},{6,22},{7,23},{8,24},{9,... | collective-permute-start | bytes 393224 | tf_op jit(solution)/shard_map/ppermute | solution.py:356
  547.8 8.2 %collective-permute-start.40 = (bf16[32,1024]{1,0:T(8,128)(2,1)S(1)}, bf16[32,1024]{1,0:T(8,128)(2,1)S(1)}, u32[]{:S(2)}, u32[]{:S(2)}) collective-permute-start(bf16[32,1024]{1,0:T(8,128)(2,1)S(1)} %fusion.70), channel_id=1, source_target_pairs={{0,16},{1,17},{2,18},{3,19},{4,20},{5,21},{6,22},{7,23},{8,24},{9,... | collective-permute-start | bytes 196616 | tf_op jit(solution)/shard_map/ppermute | solution.py:356
  552.1 12.1 %collective-permute-start.38 = (bf16[32,1024]{1,0:T(8,128)(2,1)S(1)}, bf16[32,1024]{1,0:T(8,128)(2,1)S(1)}, u32[]{:S(2)}, u32[]{:S(2)}) collective-permute-start(bf16[32,1024]{1,0:T(8,128)(2,1)S(1)} %fusion.68), channel_id=1, source_target_pairs={{0,16},{1,17},{2,18},{3,19},{4,20},{5,21},{6,22},{7,23},{8,24},{9,... | collective-permute-start | bytes 196616 | tf_op jit(solution)/shard_map/ppermute | solution.py:356
  556.1 5.2 collective-permute-start.39
  563.1 4.3 collective-permute-start.36
  567.4 4.9 collective-permute-start.37
  (48 other events, 494.8 us)
Sparse Core Ops, SparseCore 0:
  11.5 115.6 all-gather.2
  130.1 75.4 all-gather.4
  289.0 93.7 reduce-scatter.2
  403.7 95.1 reduce-scatter.4
